TPU v7x, 32 devices: a whole 2x2x4 slice. The times are simulated.
32 devices in a mesh: rep: 8 (over z, x), shard: 4 (over y, core).
Axes of the slice: x: 2, y: 2, z: 4, core: 2. Of those that a mesh axis runs over, the one named last changes fastest.
Arguments:
- latent_tokens: bfloat16 [256, 256, 384], P(('rep', 'shard')), may hold values from -6 to 6
- cond: bfloat16 [256, 384], P(('rep', 'shard')), may hold values from -6 to 6
- w_ada: bfloat16 [384, 2304], P('shard'), may hold values from -0.3125 to 0.3125
- b_ada: bfloat16 [2304], P('shard'), may hold values from -3 to 3
- w_qkv: bfloat16 [384, 1152], P('shard'), may hold values from -0.3125 to 0.3125
- b_qv: bfloat16 [768], P('shard'), may hold values from -3 to 3
- w_o: bfloat16 [384, 384], P('shard'), may hold values from -0.875 to 0.875
- b_o: bfloat16 [384], P('shard'), may hold values from -3 to 3
- w_1: bfloat16 [384, 1536], P('shard'), may hold values from -0.3125 to 0.3125
- b_1: bfloat16 [1536], P('shard'), may hold values from -3 to 3
- w_2: bfloat16 [1536, 384], P('shard'), may hold values from -0.15625 to 0.15625
- b_2: bfloat16 [384], P('shard'), may hold values from -3 to 3
- grad_out: bfloat16 [256, 256, 384], P(('rep', 'shard')), may hold values from -6 to 6
Outputs:
- block_out: bfloat16 [256, 256, 384], P(('rep', 'shard'))
- grad_tokens: float32 [256, 256, 384], P(('rep', 'shard'))
- grad_cond: float32 [256, 384], P(('rep', 'shard'))
- grad_w_ada: float32 [384, 2304], P('shard')
- grad_b_ada: float32 [2304], P('shard')
- grad_w_qkv: float32 [384, 1152], P('shard')
- grad_b_qv: float32 [768], P('shard')
- grad_w_o: float32 [384, 384], P('shard')
- grad_b_o: float32 [384], P('shard')
- grad_w_1: float32 [384, 1536], P('shard')
- grad_b_1: float32 [1536], P('shard')
- grad_w_2: float32 [1536, 384], P('shard')
- grad_b_2: float32 [384], P('shard')
All inputs are finite; a program needn't handle non-finite values.
Results may differ from a plain program's by a relative error of at most 0.019.
The roundings to bfloat16 on the way count: a program that leaves them out, or rounds other values in their place, can miss the bound.
Values may be sent and summed in bfloat16 or wider, within the bound.
No kernel may reach another device: no remote copies, remote signals or barrier semaphores. Data moves between devices by JAX's collectives and lax.ppermute only.
A program may use at most 128 MiB of HBM per device.

v0:
```python
import math

import jax
import jax.numpy as jnp
from jax import lax
from jax.sharding import PartitionSpec as P

HEADS = 6


def layer_norm(value):
    centred = value - jnp.mean(value, axis=-1, keepdims=True)
    factor = lax.rsqrt(jnp.mean(centred * centred, axis=-1, keepdims=True) + 1e-06)
    return (centred * factor, factor)


def norm_back(normed, factor, grad_normed):
    inner = jnp.mean(grad_normed, axis=-1, keepdims=True)
    along = jnp.mean(grad_normed * normed, axis=-1, keepdims=True)
    return factor * (grad_normed - inner - normed * along)


def project(left, right):
    return jnp.einsum("lsd,de->lse", left, right, preferred_element_type=jnp.float32)


def weight_grad(left, right):
    return jnp.einsum("lsd,lse->de", left, right, preferred_element_type=jnp.float32)


def attend(items):
    query, key, value = items
    scores = jnp.einsum("lqhd,lkhd->lhqk", query, key, preferred_element_type=jnp.float32) * 0.125
    top = jnp.max(scores, axis=-1, keepdims=True)
    expo = jnp.exp(scores - top)
    total = jnp.sum(expo, axis=-1, keepdims=True)
    probs = (expo / total).astype(jnp.bfloat16)
    attended = jnp.einsum("lhqk,lkhd->lqhd", probs, value, preferred_element_type=jnp.float32)
    return (attended.astype(jnp.bfloat16), top + jnp.log(total))


def attend_back(items):
    query, key, value, logsum, grad_att = items
    scores = jnp.einsum("lqhd,lkhd->lhqk", query, key, preferred_element_type=jnp.float32) * 0.125
    probs = jnp.exp(scores - logsum)
    rounded = probs.astype(jnp.bfloat16)
    grad_value = jnp.einsum(
        "lhqk,lqhd->lkhd", rounded, grad_att, preferred_element_type=jnp.float32
    )
    grad_probs = jnp.einsum("lqhd,lkhd->lhqk", grad_att, value, preferred_element_type=jnp.float32)
    row_total = jnp.sum(probs * grad_probs, axis=-1, keepdims=True)
    grad_scores = (probs * (grad_probs - row_total)).astype(jnp.bfloat16)
    grad_query = (
        jnp.einsum("lhqk,lkhd->lqhd", grad_scores, key, preferred_element_type=jnp.float32) * 0.125
    )
    grad_key = (
        jnp.einsum("lhqk,lqhd->lkhd", grad_scores, query, preferred_element_type=jnp.float32)
        * 0.125
    )
    return (
        grad_query.astype(jnp.bfloat16),
        grad_key.astype(jnp.bfloat16),
        grad_value.astype(jnp.bfloat16),
    )


def on_device(
    latent_tokens, cond, w_ada, b_ada, w_qkv, b_qv, w_o, b_o, w_1, b_1, w_2, b_2, grad_out
):
    count, length, width = latent_tokens.shape
    head_size = width // HEADS
    per_block = math.gcd(count, max(1, 512 // length))
    blocks = count // per_block
    whole = (
        lax.all_gather(w_ada, "shard", axis=0, tiled=True),
        lax.all_gather(b_ada, "shard", axis=0, tiled=True),
        lax.all_gather(w_qkv, "shard", axis=0, tiled=True),
        lax.all_gather(b_qv, "shard", axis=0, tiled=True),
        lax.all_gather(w_o, "shard", axis=0, tiled=True),
        lax.all_gather(b_o, "shard", axis=0, tiled=True),
        lax.all_gather(w_1, "shard", axis=0, tiled=True),
        lax.all_gather(b_1, "shard", axis=0, tiled=True),
        lax.all_gather(w_2, "shard", axis=0, tiled=True),
        lax.all_gather(b_2, "shard", axis=0, tiled=True),
    )
    f_ada, f_bada, f_qkv, f_bqv, f_wo, f_bo, f_w1, f_b1, f_w2, f_b2 = whole
    tokens = latent_tokens.astype(jnp.float32)
    condition = cond.astype(jnp.float32)
    cs = jax.nn.silu(condition).astype(jnp.bfloat16)
    ada = jnp.dot(cs, f_ada, preferred_element_type=jnp.float32) + f_bada.astype(jnp.float32)
    shift1, scale1, gate1, shift2, scale2, gate2 = jnp.split(ada, 6, axis=-1)
    n1, rstd1 = layer_norm(tokens)
    m1 = (n1 * (1.0 + scale1[:, None]) + shift1[:, None]).astype(jnp.bfloat16)
    qkv = project(m1, f_qkv)
    bias_qv = f_bqv.astype(jnp.float32)
    query = (qkv[..., :width] + bias_qv[:width]).astype(jnp.bfloat16)
    key = qkv[..., width : 2 * width].astype(jnp.bfloat16)
    value = (qkv[..., 2 * width :] + bias_qv[width:]).astype(jnp.bfloat16)
    shape_blocks = (blocks, per_block, length, HEADS, head_size)
    q_blocks = query.reshape(shape_blocks)
    k_blocks = key.reshape(shape_blocks)
    v_blocks = value.reshape(shape_blocks)
    att_blocks, logsum = lax.map(attend, (q_blocks, k_blocks, v_blocks))
    attended = att_blocks.reshape(count, length, width)
    branch = project(attended, f_wo) + f_bo.astype(jnp.float32)
    x1 = tokens + gate1[:, None] * branch
    n2, rstd2 = layer_norm(x1)
    m2 = (n2 * (1.0 + scale2[:, None]) + shift2[:, None]).astype(jnp.bfloat16)
    hidden = project(m2, f_w1) + f_b1.astype(jnp.float32)
    gelu_out, gelu_vjp = jax.vjp(lambda t: jax.nn.gelu(t, approximate=True), hidden)
    gelu_low = gelu_out.astype(jnp.bfloat16)
    ffn = project(gelu_low, f_w2) + f_b2.astype(jnp.float32)
    block_out = (x1 + gate2[:, None] * ffn).astype(jnp.bfloat16)
    again = (
        lax.all_gather(w_ada, "shard", axis=0, tiled=True),
        lax.all_gather(w_qkv, "shard", axis=0, tiled=True),
        lax.all_gather(w_o, "shard", axis=0, tiled=True),
        lax.all_gather(w_1, "shard", axis=0, tiled=True),
        lax.all_gather(w_2, "shard", axis=0, tiled=True),
    )
    g_ada, g_qkv, g_wo, g_w1, g_w2 = again
    cotangent = grad_out.astype(jnp.float32)
    grad_ffn = (cotangent * gate2[:, None]).astype(jnp.bfloat16)
    d_gate2 = jnp.sum(cotangent * ffn, axis=1)
    gw_2 = weight_grad(gelu_low, grad_ffn)
    gb_2 = jnp.sum(grad_ffn.astype(jnp.float32), axis=(0, 1))
    grad_gelu = jnp.einsum("lse,de->lsd", grad_ffn, g_w2, preferred_element_type=jnp.float32)
    grad_hidden = gelu_vjp(grad_gelu)[0].astype(jnp.bfloat16)
    gw_1 = weight_grad(m2, grad_hidden)
    gb_1 = jnp.sum(grad_hidden.astype(jnp.float32), axis=(0, 1))
    grad_m2 = jnp.einsum("lse,de->lsd", grad_hidden, g_w1, preferred_element_type=jnp.float32)
    d_scale2 = jnp.sum(grad_m2 * n2, axis=1)
    d_shift2 = jnp.sum(grad_m2, axis=1)
    grad_x1 = cotangent + norm_back(n2, rstd2, grad_m2 * (1.0 + scale2[:, None]))
    grad_branch = (grad_x1 * gate1[:, None]).astype(jnp.bfloat16)
    d_gate1 = jnp.sum(grad_x1 * branch, axis=1)
    gw_o = weight_grad(attended, grad_branch)
    gb_o = jnp.sum(grad_branch.astype(jnp.float32), axis=(0, 1))
    grad_att = jnp.einsum(
        "lse,de->lsd", grad_branch, g_wo, preferred_element_type=jnp.float32
    ).astype(jnp.bfloat16)
    dq, dk, dv = lax.map(
        attend_back, (q_blocks, k_blocks, v_blocks, logsum, grad_att.reshape(shape_blocks))
    )
    grad_qkv = jnp.concatenate(
        [
            dq.reshape(count, length, width),
            dk.reshape(count, length, width),
            dv.reshape(count, length, width),
        ],
        axis=-1,
    )
    gw_qkv = weight_grad(m1, grad_qkv)
    column_sums = jnp.sum(grad_qkv.astype(jnp.float32), axis=(0, 1))
    gb_qv = jnp.concatenate([column_sums[:width], column_sums[2 * width :]])
    grad_m1 = jnp.einsum("lse,de->lsd", grad_qkv, g_qkv, preferred_element_type=jnp.float32)
    d_scale1 = jnp.sum(grad_m1 * n1, axis=1)
    d_shift1 = jnp.sum(grad_m1, axis=1)
    grad_tokens = grad_x1 + norm_back(n1, rstd1, grad_m1 * (1.0 + scale1[:, None]))
    grad_ada = jnp.concatenate(
        [d_shift1, d_scale1, d_gate1, d_shift2, d_scale2, d_gate2], axis=-1
    ).astype(jnp.bfloat16)
    gw_ada = jnp.dot(cs.T, grad_ada, preferred_element_type=jnp.float32)
    gb_ada = jnp.sum(grad_ada.astype(jnp.float32), axis=0)
    grad_cs = jnp.dot(grad_ada, g_ada.T, preferred_element_type=jnp.float32)
    silu_grad = jax.vjp(jax.nn.silu, condition)[1](grad_cs)[0]
    partial_value = (
        lax.psum_scatter(
            gw_ada.astype(jnp.bfloat16), "shard", scatter_dimension=0, tiled=True
        ).astype(jnp.float32),
        lax.psum_scatter(
            gb_ada.astype(jnp.bfloat16), "shard", scatter_dimension=0, tiled=True
        ).astype(jnp.float32),
        lax.psum_scatter(
            gw_qkv.astype(jnp.bfloat16), "shard", scatter_dimension=0, tiled=True
        ).astype(jnp.float32),
        lax.psum_scatter(
            gb_qv.astype(jnp.bfloat16), "shard", scatter_dimension=0, tiled=True
        ).astype(jnp.float32),
        lax.psum_scatter(
            gw_o.astype(jnp.bfloat16), "shard", scatter_dimension=0, tiled=True
        ).astype(jnp.float32),
        lax.psum_scatter(
            gb_o.astype(jnp.bfloat16), "shard", scatter_dimension=0, tiled=True
        ).astype(jnp.float32),
        lax.psum_scatter(
            gw_1.astype(jnp.bfloat16), "shard", scatter_dimension=0, tiled=True
        ).astype(jnp.float32),
        lax.psum_scatter(
            gb_1.astype(jnp.bfloat16), "shard", scatter_dimension=0, tiled=True
        ).astype(jnp.float32),
        lax.psum_scatter(
            gw_2.astype(jnp.bfloat16), "shard", scatter_dimension=0, tiled=True
        ).astype(jnp.float32),
        lax.psum_scatter(
            gb_2.astype(jnp.bfloat16), "shard", scatter_dimension=0, tiled=True
        ).astype(jnp.float32),
    )
    summed = (
        lax.psum(partial_value[0].astype(jnp.bfloat16), "rep").astype(jnp.float32),
        lax.psum(partial_value[1].astype(jnp.bfloat16), "rep").astype(jnp.float32),
        lax.psum(partial_value[2].astype(jnp.bfloat16), "rep").astype(jnp.float32),
        lax.psum(partial_value[3].astype(jnp.bfloat16), "rep").astype(jnp.float32),
        lax.psum(partial_value[4].astype(jnp.bfloat16), "rep").astype(jnp.float32),
        lax.psum(partial_value[5].astype(jnp.bfloat16), "rep").astype(jnp.float32),
        lax.psum(partial_value[6].astype(jnp.bfloat16), "rep").astype(jnp.float32),
        lax.psum(partial_value[7].astype(jnp.bfloat16), "rep").astype(jnp.float32),
        lax.psum(partial_value[8].astype(jnp.bfloat16), "rep").astype(jnp.float32),
        lax.psum(partial_value[9].astype(jnp.bfloat16), "rep").astype(jnp.float32),
    )
    return (
        block_out,
        grad_tokens,
        silu_grad,
        summed[0],
        summed[1],
        summed[2],
        summed[3],
        summed[4],
        summed[5],
        summed[6],
        summed[7],
        summed[8],
        summed[9],
    )


def solution(mesh):
    in_specs = (
        P(("rep", "shard"), None, None),
        P(("rep", "shard"), None),
        P("shard", None),
        P("shard"),
        P("shard", None),
        P("shard"),
        P("shard", None),
        P("shard"),
        P("shard", None),
        P("shard"),
        P("shard", None),
        P("shard"),
        P(("rep", "shard"), None, None),
    )
    out_specs = (
        P(("rep", "shard"), None, None),
        P(("rep", "shard"), None, None),
        P(("rep", "shard"), None),
        P("shard", None),
        P("shard"),
        P("shard", None),
        P("shard"),
        P("shard", None),
        P("shard"),
        P("shard", None),
        P("shard"),
        P("shard", None),
        P("shard"),
    )
    return jax.shard_map(
        on_device, mesh=mesh, in_specs=in_specs, out_specs=out_specs, check_vma=False
    )
```

profile of v0, /device:TPU:0, one launch (start us, length us, event | category | flops | bytes accessed | tf_op | source)
XLA Modules:
  0.0 424.8 jit_solution(18000375624998559178)
XLA Ops:
  13.5 6.1 %all-gather = bf16[4,1,384]{2,1,0:T(2,128)(2,1)S(1)} all-gather(bf16[1,1,384]{2,1,0:T(2,128)(2,1)S(1)} %reshape.148), channel_id=1, replica_groups=mesh['rep'=8,'shard'=4] {'shard'}, dimensions={0}, use_global_device_ids=true | all-gather | bytes 3840 | tf_op jit(solution)/shard_map/all_gather | solution.py:82
  23.6 12.3 %all-reduce.12 = (bf16[2304]{0:T(1024)(128)(2,1)S(1)}, bf16[768]{0:T(1024)(128)(2,1)S(1)}, bf16[384]{0:T(512)(128)(2,1)S(1)}, bf16[384]{0:T(512)(128)(2,1)S(1)}) all-reduce(bf16[2304]{0:T(1024)(128)(2,1)S(1)} %dynamic-update-slice, bf16[768]{0:T(1024)(128)(2,1)S(1)} %dynamic-update-slice.1, ...), channel_id=1, replica_groups=mesh['rep'=8,'shard'=4] {'shard'}, use_global_device_ids=true, to_apply=%add | all-reduce | flops 3840 | bytes 15360
  39.2 5.9 %all_gather.39 = bf16[384,384]{1,0:T(8,128)(2,1)S(1)} all-gather(bf16[96,384]{1,0:T(8,128)(2,1)S(1)} %copy-done.16), channel_id=1, replica_groups=mesh['rep'=8,'shard'=4] {'shard'}, dimensions={0}, use_global_device_ids=true | all-gather | bytes 368640 | tf_op jit(solution)/shard_map/all_gather | solution.py:79
  45.1 11.3 %all_gather.37 = bf16[384,1152]{1,0:T(8,128)(2,1)S(1)} all-gather(bf16[96,1152]{1,0:T(8,128)(2,1)S(1)} %copy-done.15), channel_id=1, replica_groups=mesh['rep'=8,'shard'=4] {'shard'}, dimensions={0}, use_global_device_ids=true | all-gather | bytes 1105920 | tf_op jit(solution)/shard_map/all_gather | solution.py:77
  74.2 18.9 %while.26 = (s32[]{:T(128)}, bf16[4,2,256,6,64]{2,4,3,1,0:T(8,128)(2,1)}, f32[4,2,6,256,1]{3,2,1,4,0:T(8,128)S(1)}, bf16[4,2,256,6,64]{2,4,3,1,0:T(8,128)(2,1)},...) while((s32[]{:T(128)}, ...), condition=%wide.region_5.6_spmd, body=%wide.region_2.5_spmd.sunk | while | flops 208598016 | bytes 11122777 | solution.py:103
  93.1 4.6 %fusion.115 = (f32[8,256]{1,0:T(8,128)S(1)}, f32[8,256,384]{2,1,0:T(8,128)S(1)}, f32[8,256,384]{2,1,0:T(8,128)}) fusion(f32[384]{0:T(512)S(1)} %convert_element_type.177, f32[8,384]{1,0:T(8,128)S(1)} %get-tuple-element.197, bf16[8,256,384]{2,1,0:T(8,128)(2,1)S(1)} %copy-done, bf16[8,256,384]{1,2,0:T(8,128)(2,1)} %bitcast.178, ...), kind=kOutput, calls=%fused_computation.164 | convolution fusion | flops 607909888 | bytes 9754112 | tf_op jit(solution)/shard_map/lsd,de->lse/dot_general | solution.py:24
  100.7 11.0 %multiply_convert_fusion.1 = (bf16[8,256,1536]{2,1,0:T(8,128)(2,1)}, f32[8,256,1536]{2,1,0:T(8,128)}) fusion(f32[1536]{0:T(1024)} %reshape.150, bf16[384,1536]{1,0:T(8,128)(2,1)} %all-gather.7.cloned.1.call-done, f32[8,256,384]{2,1,0:T(8,128)} %copy-done.1, f32[8,384]{1,0:T(8,128)} %get-tuple-element.193, f32[8,384]{1,0:T(8,128)} %get-tuple-element.194, ...), kind=kOutput, calls=%fused_computation.69 | convolution fusion | flops 2451308544 | bytes 23246848 | tf_op jit(solution)/shard_map/lsd,de->lse/dot_general | solution.py:24
  111.7 14.8 %fusion.120 = (bf16[1536]{0:T(1024)(128)(2,1)}, bf16[8,256,1536]{2,1,0:T(8,128)(2,1)S(1)}) fusion(f32[8,256,1536]{2,1,0:T(8,128)} %get-tuple-element.206, f32[1536]{0:T(1024)} %reshape.150, bf16[1536,384]{1,0:T(8,128)(2,1)} %all-gather.9.cloned.1.call-done, bf16[8,256,384]{2,1,0:T(8,128)(2,1)} %param.29, f32[8,384]{1,0:T(8,128)} %get-tuple-element.192), kind=kOutput, calls=%fused_computation.169 | convolution fusion | flops 2487482880 | bytes 21648384 | tf_op jit(solution)/shard_map/lse,de->lsd/dot_general | solution.py:127
  126.6 3.6 fusion.92
  133.4 6.0 %fusion.79 = (bf16[8,384]{1,0:T(8,128)(2,1)}, bf16[8,256,384]{2,1,0:T(8,128)(2,1)}, bf16[8,384]{1,0:T(8,128)(2,1)}, f32[8,256]{1,0:T(8,128)S(1)}, f32[8,256]{1,0:T(8,128)S(1)}, /*index=5*/bf16[8,384]{1,0:T(8,128)(2,1)}) fusion(bf16[8,256,384]{2,1,0:T(8,128)(2,1)S(1)} %copy-done.13, f32[384]{0:T(512)S(1)} %copy-done.36, f32[8,256,384]{2,1,0:T(8,128)S(1)} %copy-done.2, ...), kind=kOutput, calls=%fused_computation.94 | convolution fusion | flops 2428488704 | bytes 16985600 | tf_op jit(solution)/shard_map/lsd,de->lse/dot_general | solution.py:24
  139.4 4.1 fusion.114
  146.4 3.7 convolution_convert_fusion.1
  156.8 37.3 %while.27 = (s32[]{:T(128)}, bf16[4,2,256,6,64]{2,4,3,1,0:T(8,128)(2,1)}, bf16[4,2,256,6,64]{2,4,3,1,0:T(8,128)(2,1)}, bf16[4,2,256,6,64]{2,4,3,1,0:T(8,128)(2,1...) while((s32[]{:T(128)}, ...), condition=%wide.region_12.13_spmd, body=%wide.region_10.12_spmd.sunk | while | flops 513733632 | bytes 33916044 | solution.py:142
  201.1 6.1 %fusion.82 = bf16[384,1152]{1,0:T(8,128)(2,1)} fusion(bf16[8,256,384]{2,1,0:T(8,128)(2,1)S(1)} %copy-done, f32[8,384]{1,0:T(8,128)S(1)} %copy-done.24, f32[8,384]{1,0:T(8,128)S(1)} %get-tuple-element.196, f32[8,256]{1,0:T(8,128)S(1)} %add_rsqrt_fusion.1, f32[8,256]{1,0:T(8,128)S(1)} %broadcast_multiply_fusion.5, bf16[8,256,384]{2,1,0:T(8,128)(2,1)} %copy.85, ...), kind=kOutput, calls=%fused_computation.111 | convolution fusion | flops 1831256064 | bytes 7217152 | tf_op jit(solution)/shard_map/lsd,lse->de/dot_general | solution.py:28
  207.3 7.6 %fusion.83 = bf16[384,1536]{1,0:T(8,128)(2,1)} fusion(bf16[8,256,1536]{2,1,0:T(8,128)(2,1)} %copy-done.39, f32[8,256,384]{2,1,0:T(8,128)} %copy-done.1, f32[8,384]{1,0:T(8,128)S(1)} %copy-done.29, f32[8,384]{1,0:T(8,128)S(1)} %copy-done.22, f32[8,256]{1,0:T(8,128)S(1)} %copy-done.26, f32[8,256]{1,0:T(8,128)S(1)} %broadcast_multiply_fusion.4), kind=kOutput, calls=%fused_computation.112 | convolution fusion | flops 2420441088 | bytes 10657792 | tf_op jit(solution)/shard_map/lsd,lse->de/dot_general | solution.py:28
  215.3 8.0 %fusion.84 = bf16[1536,384]{1,0:T(8,128)(2,1)} fusion(bf16[8,256,1536]{2,1,0:T(8,128)(2,1)} %get-tuple-element.205, bf16[8,256,384]{2,1,0:T(8,128)(2,1)} %param.29, f32[8,384]{1,0:T(8,128)S(1)} %copy-done.20), kind=kOutput, calls=%fused_computation.113 | convolution fusion | flops 2418868224 | bytes 9056256 | tf_op jit(solution)/shard_map/lsd,lse->de/dot_general | solution.py:28
  223.4 6.2 %fusion.76 = (bf16[8,384]{1,0:T(8,128)(2,1)S(1)}, f32[8,256]{1,0:T(8,128)S(1)}, f32[8,256]{1,0:T(8,128)S(1)}, bf16[8,384]{1,0:T(8,128)(2,1)S(1)}, f32[8,256,384]{2,1,0:T(8,128)S(1)}) fusion(bf16[8,256,384]{2,1,0:T(8,128)(2,1)S(1)} %copy-done, f32[8,256]{1,0:T(8,128)S(1)} %add_rsqrt_fusion.1, f32[8,256]{1,0:T(8,128)S(1)} %broadcast_multiply_fusion.5, ...), kind=kOutput, calls=%fused_computation.91 | convolution fusion | flops 1833949184 | bytes 10379264 | tf_op jit(solution)/shard_map/lse,de->lsd/dot_general | solution.py:156
  229.7 3.1 multiply_reduce_fusion.3
  235.0 24.6 %reduce-scatter.12.cloned.1.call-done = bf16[96,1536]{1,0:T(8,128)(2,1)} async-done(((bf16[384,1536]{1,0:T(8,128)(2,1)}), bf16[96,1536]{1,0:T(8,128)(2,1)}) %reduce-scatter.12.cloned.1.call-update) | async-done | bytes 294928 | tf_op jit(solution)/shard_map/reduce_scatter | solution.py:186
  259.6 28.5 %reduce-scatter.14.cloned.1.call-done = bf16[384,384]{1,0:T(8,128)(2,1)} async-done(((bf16[1536,384]{1,0:T(8,128)(2,1)}), bf16[384,384]{1,0:T(8,128)(2,1)}) %reduce-scatter.14.cloned.1.call-update) | async-done | bytes 294928 | tf_op jit(solution)/shard_map/reduce_scatter | solution.py:192
  288.0 32.0 %reduce-scatter.6.cloned.1.call-done = bf16[96,2304]{1,0:T(8,128)(2,1)} async-done(((bf16[384,2304]{1,0:T(8,128)(2,1)}), bf16[96,2304]{1,0:T(8,128)(2,1)}) %reduce-scatter.6.cloned.1.call-update) | async-done | bytes 442384 | tf_op jit(solution)/shard_map/reduce_scatter | solution.py:168
  325.0 10.5 %all-reduce.11 = (bf16[2304]{0:T(1024)(128)(2,1)S(1)}, bf16[768]{0:T(1024)(128)(2,1)S(1)}, bf16[384]{0:T(512)(128)(2,1)S(1)}, bf16[1536]{0:T(1024)(128)(2,1)S(1)}, bf16[384]{0:T(512)(128)(2,1)S(1)}) all-reduce(bf16[2304]{0:T(1024)(128)(2,1)S(1)} %reduce_sum.215, ...), channel_id=3, replica_groups=mesh['rep'=8,'shard'=4] {'shard'}, use_global_device_ids=true, to_apply=%region_24.25.clone | all-reduce | flops 5376 | bytes 21504
  335.9 22.2 %all-reduce.9 = (bf16[576]{0:T(1024)(128)(2,1)S(1)}, bf16[192]{0:T(256)(128)(2,1)S(1)}, bf16[96]{0:T(256)(128)(2,1)S(1)}, bf16[384]{0:T(512)(128)(2,1)S(1)}, bf16[96]{0:T(256)(128)(2,1)S(1)}) all-reduce(bf16[576]{0:T(1024)(128)(2,1)S(1)} %dynamic-slice.5, ...), channel_id=1, replica_groups=mesh['rep'=8,'shard'=4] {'rep'}, use_global_device_ids=true, to_apply=%region_25.26 | all-reduce | flops 1344 | bytes 5376 | tf_op jit(solution)/shard_map/psum | solution.py:201
  362.1 48.0 %all-reduce.15.cloned.1.call-done = (bf16[96,2304]{1,0:T(8,128)(2,1)}, bf16[96,1152]{1,0:T(8,128)(2,1)}, bf16[96,384]{1,0:T(8,128)(2,1)}, bf16[96,1536]{1,0:T(8,128)(2,1)}, bf16[384,384]{1,0:T(8,128)(2,1)}) async-done(((bf16[96,2304]{1,0:T(8,128)(2,1)}, bf16[96,1152]{1,0:T(8,128)(2,1)}, bf16[96,384]{1,0:T(8,128)(2,1)}, bf16[96,1536]{1,0:T(8,128)(2,1)}, bf16[384,384]{1,0:T(8,128)(2,1)}), ...) | async-done | bytes 1327120 | tf_op jit(solution)/shard_map/psum | solution.py:200
  (226 shorter events, 125.2 us)
Async XLA Ops:
  7.2 31.1 %copy-start = (bf16[8,256,384]{2,1,0:T(8,128)(2,1)S(1)}, bf16[8,256,384]{2,1,0:T(8,128)(2,1)}, u32[]{:S(2)}) copy-start(bf16[8,256,384]{2,1,0:T(8,128)(2,1)} %param.17) | copy-start | bytes 4718596
  7.2 32.0 %copy-start.16 = (bf16[96,384]{1,0:T(8,128)(2,1)S(1)}, bf16[96,384]{1,0:T(8,128)(2,1)}, u32[]{:S(2)}) copy-start(bf16[96,384]{1,0:T(8,128)(2,1)} %param.23) | copy-start | bytes 221188
  7.2 37.9 %copy-start.15 = (bf16[96,1152]{1,0:T(8,128)(2,1)S(1)}, bf16[96,1152]{1,0:T(8,128)(2,1)}, u32[]{:S(2)}) copy-start(bf16[96,1152]{1,0:T(8,128)(2,1)} %param.21) | copy-start | bytes 663556
  7.2 49.2 %copy-start.17 = (bf16[8,384]{1,0:T(8,128)(2,1)S(1)}, bf16[8,384]{1,0:T(8,128)(2,1)}, u32[]{:S(2)}) copy-start(bf16[8,384]{1,0:T(8,128)(2,1)} %param.18) | copy-start | bytes 18436
  7.2 49.2 %all-gather.5.cloned.1.call-start = ((), (), s32[]{:S(2)}) async-start(), calls=%async_computation.5 | async-start | bytes 2211840 | tf_op jit(solution)/shard_map/all_gather | solution.py:75
  8.0 92.7 %all-gather.7.cloned.1.call-start = ((), (), s32[]{:S(2)}) async-start(), calls=%async_computation.6 | async-start | bytes 1474560 | tf_op jit(solution)/shard_map/all_gather | solution.py:81
  8.7 103.0 %all-gather.9.cloned.1.call-start = ((), (), s32[]{:S(2)}) async-start(), calls=%async_computation.7 | async-start | bytes 1474560 | tf_op jit(solution)/shard_map/all_gather | solution.py:83
  9.4 225.5 %reduce-scatter.10.cloned.1.call-start = ((), (), s32[]{:S(2)}) async-start(), calls=%async_computation.10 | async-start | bytes 368640 | tf_op jit(solution)/shard_map/reduce_scatter | solution.py:180
  35.9 57.2 %copy-start.27 = (f32[384]{0:T(512)}, f32[384]{0:T(512)S(1)}, u32[]{:S(2)}) copy-start(f32[384]{0:T(512)S(1)} %convert_element_type.177) | copy-start | bytes 4612
  111.7 14.8 %copy-start.38 = (bf16[384,1536]{1,0:T(8,128)(2,1)S(1)}, bf16[384,1536]{1,0:T(8,128)(2,1)}, u32[]{:S(2)}) copy-start(bf16[384,1536]{1,0:T(8,128)(2,1)} %all-gather.7.cloned.1.call-done) | copy-start | bytes 3538948
  126.6 6.8 %copy-start.40 = (bf16[8,256,1536]{2,1,0:T(8,128)(2,1)S(1)}, bf16[8,256,1536]{2,1,0:T(8,128)(2,1)}, u32[]{:S(2)}) copy-start(bf16[8,256,1536]{2,1,0:T(8,128)(2,1)} %get-tuple-element.205) | copy-start | bytes 18874372
  150.1 84.9 %reduce-scatter.8.cloned.1.call-start = ((), (), s32[]{:S(2)}) async-start(), calls=%async_computation.9 | async-start | bytes 1105920 | tf_op jit(solution)/shard_map/reduce_scatter | solution.py:174
  207.3 8.1 %copy-start.20 = (f32[8,384]{1,0:T(8,128)S(1)}, f32[8,384]{1,0:T(8,128)}, u32[]{:S(2)}) copy-start(f32[8,384]{1,0:T(8,128)} %get-tuple-element.192) | copy-start | bytes 36868
  207.3 52.3 %reduce-scatter.12.cloned.1.call-start = ((), (), s32[]{:S(2)}) async-start(), calls=%async_computation.11 | async-start | bytes 1474560 | tf_op jit(solution)/shard_map/reduce_scatter | solution.py:186
  215.0 8.4 %copy-start.10 = (bf16[8,256,384]{2,1,0:T(8,128)(2,1)S(1)}, bf16[8,256,384]{2,1,0:T(8,128)(2,1)}, u32[]{:S(2)}) copy-start(bf16[8,256,384]{2,1,0:T(8,128)(2,1)} %copy.85) | copy-start | bytes 4718596
  215.0 73.0 %reduce-scatter.14.cloned.1.call-start = ((), (), s32[]{:S(2)}) async-start(), calls=%async_computation.12 | async-start | bytes 1474560 | tf_op jit(solution)/shard_map/reduce_scatter | solution.py:192
  223.3 96.7 %reduce-scatter.6.cloned.1.call-start = ((), (), s32[]{:S(2)}) async-start(), calls=%async_computation.8 | async-start | bytes 2211840 | tf_op jit(solution)/shard_map/reduce_scatter | solution.py:168
  232.8 89.9 %copy-start.11 = (bf16[8,256,384]{2,1,0:T(8,128)(2,1)S(1)}, bf16[8,256,384]{2,1,0:T(8,128)(2,1)}, u32[]{:S(2)}) copy-start(bf16[8,256,384]{2,1,0:T(8,128)(2,1)} %copy.85) | copy-start | bytes 4718596
  234.8 90.2 %copy-start.33 = (bf16[384]{0:T(512)(128)(2,1)S(1)}, bf16[384]{0:T(512)(128)(2,1)}, u32[]{:S(2)}) copy-start(bf16[384]{0:T(512)(128)(2,1)} %get-tuple-element.172) | copy-start | bytes 2308
  234.8 90.2 %copy-start.34 = (bf16[384]{0:T(512)(128)(2,1)S(1)}, bf16[384]{0:T(512)(128)(2,1)}, u32[]{:S(2)}) copy-start(bf16[384]{0:T(512)(128)(2,1)} %get-tuple-element.191) | copy-start | bytes 2308
  234.8 90.2 %copy-start.35 = (bf16[1536]{0:T(1024)(128)(2,1)S(1)}, bf16[1536]{0:T(1024)(128)(2,1)}, u32[]{:S(2)}) copy-start(bf16[1536]{0:T(1024)(128)(2,1)} %get-tuple-element.208) | copy-start | bytes 9220
  234.9 126.0 %copy-start.6 = (bf16[384,2304]{1,0:T(8,128)(2,1)S(1)}, bf16[384,2304]{1,0:T(8,128)(2,1)}, u32[]{:S(2)}) copy-start(bf16[384,2304]{1,0:T(8,128)(2,1)} %all-gather.5.cloned.1.call-done) | copy-start | bytes 5308420
  234.9 175.2 %all-reduce.15.cloned.1.call-start = ((), (), s32[]{:S(2)}) async-start(), calls=%async_computation.13 | async-start | bytes 2654208 | tf_op jit(solution)/shard_map/psum | solution.py:200
  410.1 7.1 %copy-start.14 = (bf16[384,384]{1,0:T(8,128)(2,1)S(1)}, bf16[384,384]{1,0:T(8,128)(2,1)}, u32[]{:S(2)}) copy-start(bf16[384,384]{1,0:T(8,128)(2,1)} %get-tuple-element.162) | copy-start | bytes 884740
  (29 other events, 119.7 us)
Sparse Core Ops, SparseCore 0:
  9.6 23.5 all-gather.4
  34.8 18.9 all-gather.6
  55.4 17.1 all-gather.8
  150.2 20.4 reduce-scatter.9
  207.4 23.9 reduce-scatter.7
  233.8 25.7 reduce-scatter.11
  262.3 25.7 reduce-scatter.13
  290.6 29.3 reduce-scatter.5
  324.6 85.3 all-reduce.14
where the time goes:
time: 429 us; the launch traced here: 425 us
  waiting for transfers between devices  135 us (31%)
  matrix products  132 us (31%)
  blocking collectives  68.3 us (16%)
  local copies, waits for them, and re-layouts  35.9 us (8%)
  other arithmetic  33 us (8%)
  between operations  19.2 us (4%)
    psum x1, waiting for transfers between devices, on_device(): lax.psum(partial_value[0].astype(jnp.bfloat16), 'rep').astype(jnp.float32)  48 us
    reduce_scatter x1, waiting for transfers between devices, on_device(): lax.psum_scatter(gw_ada.astype(jnp.bfloat16), 'shard', scatter_dimension=...  32 us
    reduce_scatter x1, waiting for transfers between devices, on_device(): lax.psum_scatter(gw_2.astype(jnp.bfloat16), 'shard', scatter_dimension=0,...  28.5 us
    dot_general x4, matrix products, project(): jnp.einsum('lsd,de->lse', left, right, preferred_element_type=jnp.float32)  24.6 us
    reduce_scatter x1, waiting for transfers between devices, on_device(): lax.psum_scatter(gw_1.astype(jnp.bfloat16), 'shard', scatter_dimension=0,...  24.6 us
    dot_general x4, matrix products, weight_grad(): jnp.einsum('lsd,lse->de', left, right, preferred_element_type=jnp.float32)  23.4 us
    unnamed x2, blocking collectives  22.9 us
    psum x1, blocking collectives, on_device(): lax.psum(partial_value[1].astype(jnp.bfloat16), 'rep').astype(jnp.float32)  22.2 us
  transfers between devices with their start and end apart: 9, of which 4 were waited for; matrix products, arithmetic and copies ran while one was open for 36% of the time, Pallas kernels for 0%

commit v1 on v0

v1 whole, which is shorter than its diff:
```python
import functools
import math

import jax
import jax.numpy as jnp
from jax import lax
from jax.experimental import pallas as pl
from jax.experimental.pallas import tpu as pltpu
from jax.sharding import PartitionSpec as P

HEADS = 6
F32 = jnp.float32
BF16 = jnp.bfloat16
EPS = 1e-06
GELU_C = math.sqrt(2.0 / math.pi)
GELU_A = 0.044715
VMEM_LIMIT = 56 * 1024 * 1024


def nn(a, b):
    return lax.dot_general(a, b, (((1,), (0,)), ((), ())), preferred_element_type=F32)


def nt(a, b):
    return lax.dot_general(a, b, (((1,), (1,)), ((), ())), preferred_element_type=F32)


def tn(a, b):
    return lax.dot_general(a, b, (((0,), (0,)), ((), ())), preferred_element_type=F32)


def norm_parts(x):
    centred = x - jnp.mean(x, axis=-1, keepdims=True)
    rstd = lax.rsqrt(jnp.mean(centred * centred, axis=-1, keepdims=True) + EPS)
    return centred * rstd, rstd


def norm_back(normed, rstd, grad):
    inner = jnp.mean(grad, axis=-1, keepdims=True)
    along = jnp.mean(grad * normed, axis=-1, keepdims=True)
    return rstd * (grad - inner - normed * along)


def piece_copies(mine, pieces, whole, sems):
    rows = pieces[0].shape[0]
    return [
        pltpu.make_async_copy(
            piece,
            whole.at[pl.ds(pl.multiple_of(jnp.bitwise_xor(mine, k) * rows, 32), rows)],
            sems.at[k],
        )
        for k, piece in enumerate(pieces)
    ]


def half_mask(shape, half):
    lane = lax.broadcasted_iota(jnp.int32, shape, len(shape) - 1)
    return (lane < shape[-1] // 2) if half == 0 else (lane >= shape[-1] // 2)


def attn_fwd(info, tok, cond, b_ada, b_qkv, *refs, per):
    wa, wq = refs[0:4], refs[4:8]
    ada_o, m1_o, qkv_o, p_o, att_o = refs[8:13]
    wa_s, wq_s, sem_a, sem_q = refs[13:]
    step = pl.program_id(0)
    width = tok.shape[-1]

    @pl.when(step == 0)
    def _():
        ca = piece_copies(info[0], wa, wa_s, sem_a)
        cq = piece_copies(info[0], wq, wq_s, sem_q)
        for copy in ca + cq:
            copy.start()
        c = cond[...].astype(F32)
        cs = (c / (1.0 + jnp.exp(-c))).astype(BF16)
        for copy in ca:
            copy.wait()
        ada_o[...] = nn(cs, wa_s[...]) + b_ada[...]
        for copy in cq:
            copy.wait()

    for l in range(per):
        row = pl.ds(step * per + l, 1)
        shift = ada_o[row, 0:width]
        scale = ada_o[row, width : 2 * width]
        n1, _ = norm_parts(tok[l].astype(F32))
        m1 = (n1 * (1.0 + scale) + shift).astype(BF16)
        m1_o[l] = m1
        qkv = (nn(m1, wq_s[...]) + b_qkv[...]).astype(BF16)
        qkv_o[l] = qkv
        for j in range(HEADS // 2):
            q = qkv[:, 128 * j : 128 * j + 128]
            k = qkv[:, width + 128 * j : width + 128 * j + 128]
            v = qkv[:, 2 * width + 128 * j : 2 * width + 128 * j + 128]
            both = []
            for h in range(2):
                km = jnp.where(half_mask(k.shape, h), k, jnp.zeros_like(k))
                s = nt(km, q)
                top = jnp.max(s, axis=0, keepdims=True)
                e = jnp.exp((s - top) * 0.125)
                total = jnp.sum(e, axis=0, keepdims=True)
                p = (e * (1.0 / total)).astype(BF16)
                p_o[l, 2 * j + h] = p
                both.append(tn(p, v))
            att = jnp.where(half_mask(both[0].shape, 0), both[0], both[1])
            att_o[l, :, 128 * j : 128 * j + 128] = att.astype(BF16)


def ffn_both(info, tok, att_i, dy_i, ada, cond, b_o, b_1, b_2, *refs, per, chunk):
    wo, w1, w2 = refs[0:4], refs[4:8], refs[8:12]
    out_o, dx1_o, datt_o, early_o, keep_a, send_a, keep_b, send_b = refs[12:20]
    wo_s, w1_s, w2_s, go_s, g1_s, g2_s, small_s, gb_s, sem_o, sem_1, sem_2 = refs[20:]
    step = pl.program_id(0)
    length, width = tok.shape[1:]
    hidden = w1_s.shape[1]

    @pl.when(step == 0)
    def _():
        copies = (
            piece_copies(info[0], wo, wo_s, sem_o)
            + piece_copies(info[0], w1, w1_s, sem_1)
            + piece_copies(info[0], w2, w2_s, sem_2)
        )
        for copy in copies:
            copy.start()
        go_s[...] = jnp.zeros_like(go_s)
        g1_s[...] = jnp.zeros_like(g1_s)
        g2_s[...] = jnp.zeros_like(g2_s)
        gb_s[...] = jnp.zeros_like(gb_s)
        c = cond[...].astype(F32)
        small_s[:, 4 * width : 5 * width] = c / (1.0 + jnp.exp(-c))
        for copy in copies:
            copy.wait()

    def rows_of(at):
        return jnp.stack(
            [ada[pl.ds(step * per + l, 1), at * width : (at + 1) * width] for l in range(per)]
        )

    def flat(v):
        return v.reshape(per * length, v.shape[-1])

    def deep(v):
        return v.reshape(per, length, v.shape[-1])

    gate1, shift2, scale2, gate2 = rows_of(2), rows_of(3), rows_of(4), rows_of(5)
    att = flat(att_i[...])
    branch = deep(nn(att, wo_s[...]) + b_o[...])
    x1 = tok[...].astype(F32) + gate1 * branch
    n2, rstd2 = norm_parts(x1)
    m2 = flat((n2 * (1.0 + scale2) + shift2).astype(BF16))
    dy = dy_i[...].astype(F32)
    df = flat((dy * gate2).astype(BF16))
    df_t = df.T
    m2_t = m2.T
    ffn = None
    dm2 = None
    for j in range(hidden // chunk):
        cols = slice(j * chunk, (j + 1) * chunk)
        h = nn(m2, w1_s[:, cols]) + b_1[:, cols]
        hh = h * h
        t = jnp.tanh(h * (GELU_C + (GELU_C * GELU_A) * hh))
        half_t = 0.5 + 0.5 * t
        g = (h * half_t).astype(BF16)
        slope = half_t + (0.5 * h) * (1.0 - t * t) * (GELU_C + (3.0 * GELU_C * GELU_A) * hh)
        part = nn(g, w2_s[cols, :])
        ffn = part if ffn is None else ffn + part
        g2_s[:, cols] += nn(df_t, g)
        dh32 = nt(df, w2_s[cols, :]) * slope
        dh = dh32.astype(BF16)
        gb_s[0:1, cols] += jnp.sum(dh.astype(F32), axis=0, keepdims=True)
        g1_s[:, cols] += nn(m2_t, dh)
        part = nt(dh, w1_s[:, cols])
        dm2 = part if dm2 is None else dm2 + part
    ffn = deep(ffn + b_2[...])
    dm2 = deep(dm2)
    out_o[...] = (x1 + gate2 * ffn).astype(BF16)
    gb_s[1:2, width : 2 * width] += jnp.sum(df.astype(F32), axis=0, keepdims=True)
    d_gate2 = jnp.sum(dy * ffn, axis=1)
    d_scale2 = jnp.sum(dm2 * n2, axis=1)
    d_shift2 = jnp.sum(dm2, axis=1)
    dx1 = dy + norm_back(n2, rstd2, dm2 * (1.0 + scale2))
    dx1_o[...] = dx1
    do = flat((dx1 * gate1).astype(BF16))
    d_gate1 = jnp.sum(dx1 * branch, axis=1)
    for l in range(per):
        row = pl.ds(step * per + l, 1)
        small_s[row, 0:width] = d_gate1[l : l + 1]
        small_s[row, width : 2 * width] = d_shift2[l : l + 1]
        small_s[row, 2 * width : 3 * width] = d_scale2[l : l + 1]
        small_s[row, 3 * width : 4 * width] = d_gate2[l : l + 1]
    gb_s[1:2, 0:width] += jnp.sum(do.astype(F32), axis=0, keepdims=True)
    go_s[...] += tn(att, do)
    datt_o[...] = deep(nt(do, wo_s[...]).astype(BF16))

    @pl.when(step == pl.num_programs(0) - 1)
    def _():
        early_o[0:8, :] = small_s[...].astype(BF16)
        early_o[8:16, :] = gb_s[...].astype(BF16)
        core = jnp.bitwise_and(info[0], 1)
        rows = width // 4
        g2_t = w2_s.shape[0] // 4
        for y in range(2):
            for which, (ra, rb) in enumerate(((keep_a, keep_b), (send_a, send_b))):
                shard = 2 * y + jnp.bitwise_xor(core, which)
                take = pl.ds(pl.multiple_of(shard * rows, 8), rows)
                ra[y, :, 0:width] = go_s[take, :].astype(BF16)
                ra[y, :, width : width + hidden] = g1_s[take, :].astype(BF16)
                at = pl.ds(pl.multiple_of(shard * g2_t, 128), g2_t)
                rb[y] = g2_s[:, at].astype(BF16)


def attn_bwd(info, tok, m1_i, qkv_i, p_i, datt_i, dx1_i, ada, cond, early, *refs, per):
    wa, wq = refs[0:4], refs[4:8]
    gtok_o, gcond_o, late_o, keep_o, send_o = refs[8:13]
    wa_s, wq_s, g_s, small_s, gb_s, sem_a, sem_q = refs[13:]
    step = pl.program_id(0)
    length, width = tok.shape[1:]

    @pl.when(step == 0)
    def _():
        ca = piece_copies(info[0], wa, wa_s, sem_a)
        cq = piece_copies(info[0], wq, wq_s, sem_q)
        for copy in cq + ca:
            copy.start()
        g_s[...] = jnp.zeros_like(g_s)
        gb_s[...] = jnp.zeros_like(gb_s)
        for copy in cq + ca:
            copy.wait()

    for l in range(per):
        row = pl.ds(step * per + l, 1)
        scale = ada[row, width : 2 * width]
        n1, rstd1 = norm_parts(tok[l].astype(F32))
        m1 = m1_i[l]
        grads = [[], [], []]
        for j in range(HEADS // 2):
            q = qkv_i[l, :, 128 * j : 128 * j + 128]
            k = qkv_i[l, :, width + 128 * j : width + 128 * j + 128]
            v = qkv_i[l, :, 2 * width + 128 * j : 2 * width + 128 * j + 128]
            datt = datt_i[l, :, 128 * j : 128 * j + 128]
            both = [[], [], []]
            for h in range(2):
                p = p_i[l, 2 * j + h]
                vm = jnp.where(half_mask(v.shape, h), v, jnp.zeros_like(v))
                both[2].append(nn(p, datt))
                dp = nt(vm, datt)
                p32 = p.astype(F32)
                pd = p32 * dp
                ds = (pd - p32 * jnp.sum(pd, axis=0, keepdims=True)).astype(BF16)
                both[1].append(nn(ds, q) * 0.125)
                both[0].append(tn(ds, k) * 0.125)
            for at in range(3):
                pair = both[at]
                grads[at].append(
                    jnp.where(half_mask(pair[0].shape, 0), pair[0], pair[1]).astype(BF16)
                )
        dqkv = jnp.concatenate(grads[0] + grads[1] + grads[2], axis=-1)
        g_s[...] += nn(m1.T, dqkv)
        sums = jnp.sum(dqkv.astype(F32), axis=0, keepdims=True)
        gb_s[0:1, 0:width] += sums[:, 0:width]
        gb_s[0:1, width : 2 * width] += sums[:, 2 * width : 3 * width]
        dm1 = nt(dqkv, wq_s[...])
        small_s[row, 0:width] = jnp.sum(dm1, axis=0, keepdims=True)
        small_s[row, width : 2 * width] = jnp.sum(dm1 * n1, axis=0, keepdims=True)
        gtok_o[l] = dx1_i[l] + norm_back(n1, rstd1, dm1 * (1.0 + scale))

    @pl.when(step == pl.num_programs(0) - 1)
    def _():
        late = small_s[...].astype(BF16)
        late_o[0:8, :] = late
        late_o[8:16, :] = gb_s[...].astype(BF16)
        dada = jnp.concatenate([late, early[0:8, 0 : 4 * width]], axis=-1)
        gcs = nt(dada, wa_s[...])
        c = cond[...].astype(F32)
        sig = 1.0 / (1.0 + jnp.exp(-c))
        gcond_o[...] = gcs * (sig * (1.0 + c * (1.0 - sig)))
        core = jnp.bitwise_and(info[0], 1)
        rows = width // 4
        for y in range(2):
            for which, ref in enumerate((keep_o, send_o)):
                shard = 2 * y + jnp.bitwise_xor(core, which)
                take = pl.ds(pl.multiple_of(shard * rows, 8), rows)
                ref[y] = g_s[take, :].astype(BF16)


def add_split(info, *refs):
    count = len(refs) // 6
    for n in range(count):
        keep, got = refs[n], refs[count + n]
        half = keep.shape[1] // 2
        for k in range(4):
            out = refs[2 * count + 4 * n + k]
            y = jnp.bitwise_xor(info[1], k >> 1)
            x = jnp.bitwise_xor(info[2], k & 1)
            take = pl.ds(pl.multiple_of(x * half, 16), half)
            out[...] = (keep[y, take, :].astype(F32) + got[y, take, :].astype(F32)).astype(BF16)


def tree_sum(values):
    while len(values) > 1:
        values = [values[2 * i] + values[2 * i + 1] for i in range(len(values) // 2)]
    return values[0]


def full(shape):
    return pl.BlockSpec(shape, lambda *_: (0,) * len(shape))


def call(body, info, operands, specs, outs, out_specs, scratch, grid, flops, traffic, exps=0):
    return pl.pallas_call(
        body,
        out_shape=outs,
        grid_spec=pltpu.PrefetchScalarGridSpec(
            num_scalar_prefetch=1,
            grid=grid,
            in_specs=specs,
            out_specs=out_specs,
            scratch_shapes=scratch,
        ),
        compiler_params=pltpu.CompilerParams(
            dimension_semantics=("arbitrary",) * len(grid), vmem_limit_bytes=VMEM_LIMIT
        ),
        cost_estimate=pl.CostEstimate(flops=flops, bytes_accessed=traffic, transcendentals=exps),
    )(info, *operands)


def on_device(
    latent_tokens, cond, w_ada, b_ada, w_qkv, b_qv, w_o, b_o, w_1, b_1, w_2, b_2, grad_out
):
    count, length, width = latent_tokens.shape
    hidden = w_1.shape[1]
    reps = lax.axis_size("rep")
    shards = lax.axis_size("shard")
    s = lax.axis_index("shard")
    r = lax.axis_index("rep")
    info = jnp.stack([s, s >> 1, r & 1, r >> 1]).astype(jnp.int32)

    def swap(v, shard_bits=0, rep_bits=0):
        pairs = [
            (i * shards + j, (i ^ rep_bits) * shards + (j ^ shard_bits))
            for i in range(reps)
            for j in range(shards)
        ]
        return lax.ppermute(v, ("rep", "shard"), pairs)

    def gather(v):
        far = swap(v, 2)
        return (v, swap(v, 1), far, swap(far, 1))

    def gather_row(v):
        a = gather(v.astype(BF16))
        core = (s & 1) == 0
        near = jnp.where(core, jnp.stack([a[0], a[1]]), jnp.stack([a[1], a[0]]))
        far = jnp.where(core, jnp.stack([a[2], a[3]]), jnp.stack([a[3], a[2]]))
        low = (s >> 1) == 0
        both = jnp.where(low, jnp.stack([near, far]), jnp.stack([far, near]))
        return both.reshape(1, -1).astype(F32)

    biases = gather_row(jnp.concatenate([b_ada, b_qv, b_o, b_1, b_2]))
    cuts, bias_rows, at = [b_ada, b_qv, b_o, b_1, b_2], [], 0
    table = biases.reshape(shards, -1)
    for b in cuts:
        bias_rows.append(table[:, at : at + b.shape[0]].reshape(1, -1))
        at += b.shape[0]
    f_bada, f_bqv, f_bo, f_b1, f_b2 = bias_rows
    b_qkv = jnp.concatenate(
        [f_bqv[:, :width], jnp.zeros((1, width), F32), f_bqv[:, width:]], axis=-1
    )
    p_ada, p_qkv = gather(w_ada), gather(w_qkv)
    w_o, w_1, w_2, _ = lax.optimization_barrier((w_o, w_1, w_2, p_qkv[2]))
    p_o, p_1, p_2 = gather(w_o), gather(w_1), gather(w_2)

    anyspec = pl.BlockSpec(memory_space=pl.ANY)
    dma4 = pltpu.SemaphoreType.DMA((4,))
    tokens = count * length

    per = 1
    lat = lambda *tail: pl.BlockSpec((per,) + tail, lambda i, _: (i,) + (0,) * len(tail))
    ada, m1, qkv, probs, att = call(
        functools.partial(attn_fwd, per=per),
        info,
        (latent_tokens, cond, f_bada, b_qkv) + p_ada + p_qkv,
        [lat(length, width), full(cond.shape), full(f_bada.shape), full(b_qkv.shape)]
        + [anyspec] * 8,
        [
            jax.ShapeDtypeStruct((count, 6 * width), F32),
            jax.ShapeDtypeStruct((count, length, width), BF16),
            jax.ShapeDtypeStruct((count, length, 3 * width), BF16),
            jax.ShapeDtypeStruct((count, HEADS, length, length), BF16),
            jax.ShapeDtypeStruct((count, length, width), BF16),
        ],
        [
            full((count, 6 * width)),
            lat(length, width),
            lat(length, 3 * width),
            lat(HEADS, length, length),
            lat(length, width),
        ],
        [
            pltpu.VMEM((width, 6 * width), BF16),
            pltpu.VMEM((width, 3 * width), BF16),
            dma4,
            dma4,
        ],
        (count // per,),
        8 * tokens * width * width + 8 * tokens * length * width,
        20 * tokens * width,
        tokens * length * HEADS,
    )

    per2 = 2 if count % 2 == 0 else 1
    lat2 = lambda *tail: pl.BlockSpec((per2,) + tail, lambda i, _: (i,) + (0,) * len(tail))
    quarter = width // 4
    block_out, dx1, datt, early, keep_a, send_a, keep_b, send_b = call(
        functools.partial(ffn_both, per=per2, chunk=512),
        info,
        (latent_tokens, att, grad_out, ada, cond, f_bo, f_b1, f_b2) + p_o + p_1 + p_2,
        [lat2(length, width)] * 3
        + [full(ada.shape), full(cond.shape), full(f_bo.shape), full(f_b1.shape), full(f_b2.shape)]
        + [anyspec] * 12,
        [
            jax.ShapeDtypeStruct((count, length, width), BF16),
            jax.ShapeDtypeStruct((count, length, width), F32),
            jax.ShapeDtypeStruct((count, length, width), BF16),
            jax.ShapeDtypeStruct((16, 5 * width), BF16),
        ]
        + [jax.ShapeDtypeStruct((2, quarter, width + hidden), BF16)] * 2
        + [jax.ShapeDtypeStruct((2, width, hidden // 4), BF16)] * 2,
        [lat2(length, width)] * 3
        + [full((16, 5 * width))]
        + [full((2, quarter, width + hidden))] * 2
        + [full((2, width, hidden // 4))] * 2,
        [
            pltpu.VMEM((width, width), BF16),
            pltpu.VMEM((width, hidden), BF16),
            pltpu.VMEM((hidden, width), BF16),
            pltpu.VMEM((width, width), F32),
            pltpu.VMEM((width, hidden), F32),
            pltpu.VMEM((width, hidden), F32),
            pltpu.VMEM((8, 5 * width), F32),
            pltpu.VMEM((8, 5 * width), F32),
            dma4,
            dma4,
            dma4,
        ],
        (count // per2,),
        12 * tokens * width * hidden + 6 * tokens * width * width,
        14 * tokens * width,
        tokens * hidden,
    )

    grad_tokens, grad_cond, late, keep_q, send_q = call(
        functools.partial(attn_bwd, per=per),
        info,
        (latent_tokens, m1, qkv, probs, datt, dx1, ada, cond, early) + p_ada + p_qkv,
        [
            lat(length, width),
            lat(length, width),
            lat(length, 3 * width),
            lat(HEADS, length, length),
            lat(length, width),
            lat(length, width),
            full(ada.shape),
            full(cond.shape),
            full(early.shape),
        ]
        + [anyspec] * 8,
        [
            jax.ShapeDtypeStruct((count, length, width), F32),
            jax.ShapeDtypeStruct((count, width), F32),
            jax.ShapeDtypeStruct((16, 2 * width), BF16),
        ]
        + [jax.ShapeDtypeStruct((2, quarter, 3 * width), BF16)] * 2,
        [lat(length, width), full((count, width)), full((16, 2 * width))]
        + [full((2, quarter, 3 * width))] * 2,
        [
            pltpu.VMEM((width, 6 * width), BF16),
            pltpu.VMEM((width, 3 * width), BF16),
            pltpu.VMEM((width, 3 * width), F32),
            pltpu.VMEM((8, 2 * width), F32),
            pltpu.VMEM((8, 2 * width), F32),
            dma4,
            dma4,
        ],
        (count // per,),
        12 * tokens * width * width + 16 * tokens * length * width,
        30 * tokens * width,
        0,
    )

    def reduce(keeps, sends):
        got = [swap(v, 1) for v in sends]
        outs = []
        for v in keeps:
            outs += [jax.ShapeDtypeStruct((v.shape[1] // 2, v.shape[2]), BF16)] * 4
        parts = call(
            add_split,
            info,
            tuple(keeps) + tuple(got),
            [full(v.shape) for v in list(keeps) + got],
            outs,
            [full(o.shape) for o in outs],
            [],
            (1,),
            0,
            sum(4 * v.size for v in keeps),
        )
        done = []
        for n in range(len(keeps)):
            own, to_x, to_y, to_d = parts[4 * n : 4 * n + 4]
            got4 = [own, swap(to_x, 0, 1), swap(to_y, 2, 0), swap(to_d, 2, 1)]
            total = tree_sum([v.astype(F32) for v in got4]).astype(BF16)
            ring = [total] + [swap(total, 0, 2 * k) for k in range(1, reps // 2)]
            total = tree_sum([v.astype(F32) for v in ring]).astype(BF16)
            other = swap(total, 0, 1)
            first = (r & 1) == 0
            whole = jnp.where(
                first, jnp.stack([total, other]), jnp.stack([other, total])
            ).astype(F32)
            done.append(whole.reshape(-1, total.shape[1]))
        return done

    def gather_all(v):
        zs = jnp.stack([v] + [swap(v, 0, 2 * k) for k in range(1, reps // 2)])
        four = jnp.stack([zs, swap(zs, 0, 1), swap(zs, 2, 0), swap(zs, 2, 1)])
        return four, swap(four, 1)

    def ada_grads(early4, late4):
        n_z = reps // 2
        n_dev = reps * shards

        def body(info, e0, e1, l0, l1, gw_o, gb_o, bias_o, e_s, l_s):
            for kc in range(2):
                e_ref, l_ref = ((e0, l0), (e1, l1))[kc]
                for kp in range(4):
                    for kz in range(n_z):
                        rep_at = jnp.bitwise_xor(info[3], kz) * 2 + jnp.bitwise_xor(
                            info[2], kp & 1
                        )
                        at = rep_at * 4 + jnp.bitwise_xor(info[0], 2 * (kp >> 1) + kc)
                        e_s[at] = e_ref[kp, kz].astype(F32)
                        l_s[at] = l_ref[kp, kz].astype(F32)
            cs = e_s[:, 0:8, 4 * width : 5 * width].reshape(8 * n_dev, width)
            cs_t = cs.T.astype(BF16)
            early_d = e_s[:, 0:8, 0 : 4 * width].reshape(8 * n_dev, 4 * width)
            late_d = l_s[:, 0:8, :].reshape(8 * n_dev, 2 * width)
            first = nn(cs_t, late_d.astype(BF16))
            second = nn(cs_t, early_d.astype(BF16))
            rows = width // 4
            for j in range(4):

                @pl.when(info[0] == j)
                def _():
                    gw_o[:, 0 : 2 * width] = first[j * rows : (j + 1) * rows]
                    gw_o[:, 2 * width : 6 * width] = second[j * rows : (j + 1) * rows]

            gb_o[:, 0 : 2 * width] = jnp.sum(late_d, axis=0, keepdims=True)
            gb_o[:, 2 * width : 6 * width] = jnp.sum(early_d, axis=0, keepdims=True)
            e_b = jnp.sum(e_s[:, 8:16, :], axis=0)
            l_b = jnp.sum(l_s[:, 8:16, :], axis=0)
            bias_o[:, 0 : 2 * width] = l_b[0:1]
            bias_o[:, 2 * width : 4 * width] = e_b[1:2, 0 : 2 * width]
            bias_o[:, 4 * width : 4 * width + hidden] = e_b[0:1, 0:hidden]

        ins = early4 + late4
        outs = [
            jax.ShapeDtypeStruct((quarter, 6 * width), F32),
            jax.ShapeDtypeStruct((1, 6 * width), F32),
            jax.ShapeDtypeStruct((1, 4 * width + hidden), F32),
        ]
        return call(
            body,
            info,
            ins,
            [full(v.shape) for v in ins],
            outs,
            [full(o.shape) for o in outs],
            [
                pltpu.VMEM((n_dev, 16, 5 * width), F32),
                pltpu.VMEM((n_dev, 16, 2 * width), F32),
            ],
            (1,),
            2 * 8 * n_dev * width * 6 * width,
            4 * n_dev * 16 * 7 * width,
        )

    gw_o1, gw_2t = reduce([keep_a, keep_b], [send_a, send_b])
    early4 = gather_all(early)
    (gw_qkv,) = reduce([keep_q], [send_q])
    late4 = gather_all(late)
    gw_ada, gb_ada, gb_rest = ada_grads(early4, late4)

    def mine(row, total):
        part = total // shards
        return lax.dynamic_slice(row.reshape(-1), (s * part,), (part,))

    return (
        block_out,
        grad_tokens,
        grad_cond,
        gw_ada,
        mine(gb_ada, 6 * width),
        gw_qkv,
        mine(gb_rest[:, 0 : 2 * width], 2 * width),
        gw_o1[:, 0:width],
        mine(gb_rest[:, 2 * width : 3 * width], width),
        gw_o1[:, width:],
        mine(gb_rest[:, 4 * width :], hidden),
        gw_2t.T,
        mine(gb_rest[:, 3 * width : 4 * width], width),
    )


def solution(mesh):
    lead = P(("rep", "shard"))
    part = P("shard")
    return jax.shard_map(
        on_device,
        mesh=mesh,
        in_specs=(lead, lead) + (part,) * 10 + (lead,),
        out_specs=(lead,) * 3 + (part,) * 10,
        check_vma=False,
    )
```

time: 429 us -> 243 us (0.57)
  matrix products: 132 us -> 0 us
  Pallas kernels: 0 us -> 92.8 us
  waiting for transfers between devices: 135 us -> 63.8 us
  blocking collectives: 68.3 us -> 0 us
  starting transfers between devices: 0.61 us -> 59.1 us
  other arithmetic: 33 us -> 6.75 us
  between operations: 19.2 us -> 1.18 us
  local copies, waits for them, and re-layouts: 35.9 us -> 18.5 us
    dot_general x43 -> x0, matrix products: 132 us -> none  [the longest x4 24.6 us: project(): jnp.einsum('lsd,de->lse', left, right, preferred_element_type=jnp.float32)]
    pallas_call x0 -> x6, Pallas kernels: none -> 92.8 us  [call(): pl.pallas_call(body, out_shape=outs, grid_spec=pltpu.PrefetchScalarGridSp...]
    reduce_scatter x5 -> x0, waiting for transfers between devices: 85.1 us -> none  [the longest x1 32 us: on_device(): lax.psum_scatter(gw_ada.astype(jnp.bfloat16), 'shard', scatter_dimension=...]
    ppermute x0 -> x56, waiting for transfers between devices: none -> 63.8 us  [swap(): return lax.ppermute(v, ('rep', 'shard'), pairs)]
    ppermute x0 -> x56, starting transfers between devices: none -> 59.1 us  [swap(): return lax.ppermute(v, ('rep', 'shard'), pairs)]
    psum x1 -> x0, waiting for transfers between devices: 48 us -> none  [on_device(): lax.psum(partial_value[0].astype(jnp.bfloat16), 'rep').astype(jnp.float32)]
    all_gather x3 -> x0, blocking collectives: 23.3 us -> none  [the longest x1 11.3 us: on_device(): lax.all_gather(w_qkv, 'shard', axis=0, tiled=True)]
    unnamed x2 -> x0, blocking collectives: 22.9 us -> none
  transfers between devices with their start and end apart: 9 -> 56, of which waited for: 4 -> 23; matrix products, arithmetic and copies ran while one was open for 36% -> 6% of each run, Pallas kernels for 0% -> 11%
where the time goes in v1:
time: 243 us; the launch traced here: 242 us
  Pallas kernels  92.8 us (38%)
  waiting for transfers between devices  63.8 us (26%)
  starting transfers between devices  59.1 us (24%)
  local copies, waits for them, and re-layouts  18.5 us (8%)
  other arithmetic  6.75 us (3%)
    pallas_call x6, Pallas kernels, call(): pl.pallas_call(body, out_shape=outs, grid_spec=pltpu.PrefetchScalarGridSp...  92.8 us
    ppermute x56, waiting for transfers between devices, swap(): return lax.ppermute(v, ('rep', 'shard'), pairs)  63.8 us
    ppermute x56, starting transfers between devices, swap(): return lax.ppermute(v, ('rep', 'shard'), pairs)  59.1 us
    unnamed x50, local copies, waits for them, and re-layouts  4.95 us
  transfers between devices with their start and end apart: 56, of which 23 were waited for; matrix products, arithmetic and copies ran while one was open for 6% of the time, Pallas kernels for 11%

profile of v1, /device:TPU:0, one launch (start us, length us, event | category | flops | bytes accessed | tf_op | source)
XLA Modules:
  0.0 242.1 jit_solution(17126905512854418720)
XLA Ops:
  0.6 3.5 %concatenate.34 = bf16[1344]{0:T(1024)(128)(2,1)S(1)} concatenate(bf16[576]{0:T(1024)(128)(2,1)} %param.16, bf16[192]{0:T(256)(128)(2,1)} %param.18, bf16[96]{0:T(256)(128)(2,1)} %param.20, bf16[384]{0:T(512)(128)(2,1)} %param.22, bf16[96]{0:T(256)(128)(2,1)} %param.24), dimensions={0} | concatenate | bytes 5376 | tf_op jit(solution)/shard_map/concatenate | solution.py:360
  4.1 3.0 %collective-permute-start.1 = (bf16[1344]{0:T(1024)(128)(2,1)S(1)}, bf16[1344]{0:T(1024)(128)(2,1)S(1)}, u32[]{:S(2)}, u32[]{:S(2)}) collective-permute-start(bf16[1344]{0:T(1024)(128)(2,1)S(1)} %concatenate.34), channel_id=1, source_target_pairs={{0,2},{1,3},{2,0},{3,1},{4,6},{5,7},{6,4},{7,5},{8,10},{9,11},{10,... | collective-permute-start | bytes 8072 | tf_op jit(solution)/shard_map/ppermute | solution.py:345
  11.8 12.9 %collective-permute-done.7.refs_6_ = bf16[96,1152]{1,0:T(8,128)(2,1)S(1)} collective-permute-done((bf16[96,1152]{1,0:T(8,128)(2,1)}, bf16[96,1152]{1,0:T(8,128)(2,1)S(1)}, u32[]{:S(2)}, u32[]{:S(2)}) %collective-permute-start.7) | collective-permute-done | bytes 221216 | tf_op jit(solution)/shard_map/ppermute | solution.py:345
  27.0 2.9 %collective-permute-done.10.refs_2_ = bf16[96,384]{1,0:T(8,128)(2,1)S(1)} collective-permute-done((bf16[96,384]{1,0:T(8,128)(2,1)}, bf16[96,384]{1,0:T(8,128)(2,1)S(1)}, u32[]{:S(2)}, u32[]{:S(2)}) %collective-permute-start.10) | collective-permute-done | bytes 73760 | tf_op jit(solution)/shard_map/ppermute | solution.py:345
  36.2 5.6 %collective-permute-done.16.refs_10_ = bf16[384,384]{1,0:T(8,128)(2,1)S(1)} collective-permute-done((bf16[384,384]{1,0:T(8,128)(2,1)}, bf16[384,384]{1,0:T(8,128)(2,1)S(1)}, u32[]{:S(2)}, u32[]{:S(2)}) %collective-permute-start.16) | collective-permute-done | bytes 294944 | tf_op jit(solution)/shard_map/ppermute | solution.py:345
  42.6 16.8 %shard_map.228 = (f32[8,2304]{1,0:T(8,128)}, bf16[8,256,384]{2,1,0:T(8,128)(2,1)}, bf16[8,256,1152]{2,1,0:T(8,128)(2,1)}, bf16[8,6,256,256]{3,2,1,0:T(8,128)(2,1)}, bf16[8,256,384]{2,1,0:T(8,128)(2,1)}) custom-call(s32[4]{0:T(128)} %pad_add_fusion.info, bf16[8,256,384]{2,1,0:T(8,128)(2,1)} %tok.5, bf16[8,384]{1,0:T(8,128)(2,1)} %cond.5, ...), custom_call_target="tpu_custom_call" | custom-call | flops 4026531840 | bytes 15728640 | tf_op jit(solution)/shard_map/pallas_call | solution.py:311
  60.5 35.3 %shard_map.229 = (bf16[8,256,384]{2,1,0:T(8,128)(2,1)}, f32[8,256,384]{2,1,0:T(8,128)}, bf16[8,256,384]{2,1,0:T(8,128)(2,1)}, bf16[16,1920]{1,0:T(8,128)(2,1)}, ...) custom-call(s32[4]{0:T(128)} %pad_add_fusion.info, ...), custom_call_target="tpu_custom_call" | custom-call | flops 16307453952 | bytes 11010048 | tf_op jit(solution)/shard_map/pallas_call | solution.py:311
  95.8 30.3 %shard_map.230 = (f32[8,256,384]{2,1,0:T(8,128)}, f32[8,384]{1,0:T(8,128)}, bf16[16,768]{1,0:T(8,128)(2,1)}, bf16[2,96,1152]{2,1,0:T(8,128)(2,1)}, bf16[2,96,1152]{2,1,0:T(8,128)(2,1)}) custom-call(s32[4]{0:T(128)} %pad_add_fusion.info, bf16[8,256,384]{2,1,0:T(8,128)(2,1)} %tok.5, bf16[8,256,384]{2,1,0:T(8,128)(2,1)} %get-tuple-element.55.m1_i, ...), custom_call_target="tpu_custom_call" | custom-call | flops 6845104128 | bytes 23592960 | tf_op jit(solution)/shard_map/pallas_call | solution.py:311
  128.3 2.6 %collective-permute-start.26 = (bf16[16,768]{1,0:T(8,128)(2,1)}, bf16[16,768]{1,0:T(8,128)(2,1)S(1)}, u32[]{:S(2)}, u32[]{:S(2)}) collective-permute-start(bf16[16,768]{1,0:T(8,128)(2,1)} %get-tuple-element.63), channel_id=1, source_target_pairs={{0,16},{1,17},{2,18},{3,19},{4,20},{5,21},{6,22},{7,23},{8,24},{9,... | collective-permute-start | bytes 73736 | tf_op jit(solution)/shard_map/ppermute | solution.py:345
  131.8 3.5 %collective-permute-start.19 = (bf16[16,1920]{1,0:T(8,128)(2,1)S(1)}, bf16[16,1920]{1,0:T(8,128)(2,1)S(1)}, u32[]{:S(2)}, u32[]{:S(2)}) collective-permute-start(bf16[16,1920]{1,0:T(8,128)(2,1)S(1)} %copy-done.8), channel_id=1, source_target_pairs={{0,16},{1,17},{2,18},{3,19},{4,20},{5,21},{6,22},{7,23},{8,24},{9,... | collective-permute-start | bytes 184328 | tf_op jit(solution)/shard_map/ppermute | solution.py:345
  138.4 2.6 %shard_map.232 = (bf16[48,1152]{1,0:T(8,128)(2,1)}, bf16[48,1152]{1,0:T(8,128)(2,1)}, bf16[48,1152]{1,0:T(8,128)(2,1)}, bf16[48,1152]{1,0:T(8,128)(2,1)}) custom-call(s32[4]{0:T(128)} %pad_add_fusion.info, bf16[2,96,1152]{2,1,0:T(8,128)(2,1)} %get-tuple-element.66.refs_0_, bf16[2,96,1152]{2,1,0:T(8,128)(2,1)} %copy-done.5), custom_call_target="tpu_custom_call" | custom-call | bytes 884736 | tf_op jit(solution)/shard_map/pallas_call | solution.py:311
  160.2 3.7 %collective-permute-done.37 = bf16[48,1152]{1,0:T(8,128)(2,1)S(1)} collective-permute-done((bf16[48,1152]{1,0:T(8,128)(2,1)S(1)}, bf16[48,1152]{1,0:T(8,128)(2,1)S(1)}, u32[]{:S(2)}, u32[]{:S(2)}) %collective-permute-start.37) | collective-permute-done | bytes 110624 | tf_op jit(solution)/shard_map/ppermute | solution.py:345
  163.9 2.5 %collective-permute-start.21 = (bf16[4,16,1920]{2,1,0:T(8,128)(2,1)S(1)}, bf16[4,16,1920]{2,1,0:T(8,128)(2,1)S(1)}, u32[]{:S(2)}, u32[]{:S(2)}) collective-permute-start(bf16[4,16,1920]{2,1,0:T(8,128)(2,1)S(1)} %get-tuple-element.86), channel_id=1, source_target_pairs={{0,4},{1,5},{2,6},{3,7},{4,0},{5,1},{6,2},{7,3},{8,12},{9,13},{10,... | collective-permute-start | bytes 737288 | tf_op jit(solution)/shard_map/ppermute | solution.py:345
  167.5 3.5 %collective-permute-done.23 = bf16[4,16,1920]{2,1,0:T(8,128)(2,1)S(1)} collective-permute-done((bf16[4,16,1920]{2,1,0:T(8,128)(2,1)S(1)}, bf16[4,16,1920]{2,1,0:T(8,128)(2,1)S(1)}, u32[]{:S(2)}, u32[]{:S(2)}) %collective-permute-start.23) | collective-permute-done | bytes 245792 | tf_op jit(solution)/shard_map/ppermute | solution.py:345
  171.0 3.4 %collective-permute-done.21 = bf16[4,16,1920]{2,1,0:T(8,128)(2,1)S(1)} collective-permute-done((bf16[4,16,1920]{2,1,0:T(8,128)(2,1)S(1)}, bf16[4,16,1920]{2,1,0:T(8,128)(2,1)S(1)}, u32[]{:S(2)}, u32[]{:S(2)}) %collective-permute-start.21) | collective-permute-done | bytes 245792 | tf_op jit(solution)/shard_map/ppermute | solution.py:345
  175.8 3.5 %shard_map.233 = (bf16[48,1920]{1,0:T(8,128)(2,1)}, bf16[48,1920]{1,0:T(8,128)(2,1)}, bf16[48,1920]{1,0:T(8,128)(2,1)}, bf16[48,1920]{1,0:T(8,128)(2,1)}, bf16[1...) custom-call(s32[4]{0:T(128)} %pad_add_fusion.info, ...), custom_call_target="tpu_custom_call" | custom-call | bytes 2654208 | tf_op jit(solution)/shard_map/pallas_call | solution.py:311
  183.7 2.5 %collective-permute-done.49 = bf16[192,384]{1,0:T(8,128)(2,1)S(1)} collective-permute-done((bf16[192,384]{1,0:T(8,128)(2,1)}, bf16[192,384]{1,0:T(8,128)(2,1)S(1)}, u32[]{:S(2)}, u32[]{:S(2)}) %collective-permute-start.49) | collective-permute-done | bytes 147488 | tf_op jit(solution)/shard_map/ppermute | solution.py:345
  187.2 2.6 %collective-permute-done.51 = bf16[192,384]{1,0:T(8,128)(2,1)S(1)} collective-permute-done((bf16[192,384]{1,0:T(8,128)(2,1)}, bf16[192,384]{1,0:T(8,128)(2,1)S(1)}, u32[]{:S(2)}, u32[]{:S(2)}) %collective-permute-start.51) | collective-permute-done | bytes 147488 | tf_op jit(solution)/shard_map/ppermute | solution.py:345
  200.1 6.4 %collective-permute-done.53 = bf16[192,384]{1,0:T(8,128)(2,1)S(1)} collective-permute-done((bf16[192,384]{1,0:T(8,128)(2,1)S(1)}, bf16[192,384]{1,0:T(8,128)(2,1)S(1)}, u32[]{:S(2)}, u32[]{:S(2)}) %collective-permute-start.53) | collective-permute-done | bytes 147488 | tf_op jit(solution)/shard_map/ppermute | solution.py:345
  207.3 2.8 %collective-permute-start.47 = (bf16[48,1920]{1,0:T(8,128)(2,1)S(1)}, bf16[48,1920]{1,0:T(8,128)(2,1)S(1)}, u32[]{:S(2)}, u32[]{:S(2)}) collective-permute-start(bf16[48,1920]{1,0:T(8,128)(2,1)S(1)} %add_convert_fusion.1), channel_id=1, source_target_pairs={{0,24},{1,25},{2,26},{3,27},{4,28},{5,29},{6,30},{7,31},{8,16},{9,... | collective-permute-start | bytes 552968 | tf_op jit(solution)/shard_map/ppermute | solution.py:345
  210.2 6.6 %collective-permute-start.55 = (bf16[192,384]{1,0:T(8,128)(2,1)S(1)}, bf16[192,384]{1,0:T(8,128)(2,1)S(1)}, u32[]{:S(2)}, u32[]{:S(2)}) collective-permute-start(bf16[192,384]{1,0:T(8,128)(2,1)S(1)} %add_convert_fusion.2), channel_id=1, source_target_pairs={{0,4},{1,5},{2,6},{3,7},{4,0},{5,1},{6,2},{7,3},{8,12},{9,13},{10,... | collective-permute-start | bytes 442376 | tf_op jit(solution)/shard_map/ppermute | solution.py:345
  216.8 5.2 %collective-permute-done.46 = bf16[48,1920]{1,0:T(8,128)(2,1)S(1)} collective-permute-done((bf16[48,1920]{1,0:T(8,128)(2,1)S(1)}, bf16[48,1920]{1,0:T(8,128)(2,1)S(1)}, u32[]{:S(2)}, u32[]{:S(2)}) %collective-permute-start.46) | collective-permute-done | bytes 184352 | tf_op jit(solution)/shard_map/ppermute | solution.py:345
  222.0 4.9 %collective-permute-start.48 = (bf16[48,1920]{1,0:T(8,128)(2,1)S(1)}, bf16[48,1920]{1,0:T(8,128)(2,1)}, u32[]{:S(2)}, u32[]{:S(2)}) collective-permute-start(bf16[48,1920]{1,0:T(8,128)(2,1)S(1)} %add_convert_fusion), channel_id=1, source_target_pairs={{0,4},{1,5},{2,6},{3,7},{4,0},{5,1},{6,2},{7,3},{8,12},{9,13},{10,... | collective-permute-start | bytes 552968 | tf_op jit(solution)/shard_map/ppermute | solution.py:345
  229.8 4.3 %shard_map.231 = (f32[96,2304]{1,0:T(8,128)}, f32[1,2304]{1,0:T(1,128)}, f32[1,3072]{1,0:T(1,128)}) custom-call(s32[4]{0:T(128)} %pad_add_fusion.info, bf16[4,4,16,1920]{3,2,1,0:T(8,128)(2,1)} %copy-done, bf16[4,4,16,1920]{3,2,1,0:T(8,128)(2,1)} %copy-done.2, bf16[4,4,16,768]{3,2,1,0:T(8,128)(2,1)} %copy-done.1, bf16[4,4,16,768]{3,2,1,0:T(8,128)(2,1)} %copy-done.6), custom_call_target="tpu_custom_call" | custom-call | flops 452984832 | bytes 5505024 | tf_op jit(solution)/shard_map/pallas_call | solution.py:311
  (191 shorter events, 70.3 us)
Async XLA Ops:
  7.1 22.8 %collective-permute-start.4 = (bf16[96,2304]{1,0:T(8,128)(2,1)}, bf16[96,2304]{1,0:T(8,128)(2,1)S(1)}, u32[]{:S(2)}, u32[]{:S(2)}) collective-permute-start(bf16[96,2304]{1,0:T(8,128)(2,1)} %refs_0_.4), channel_id=1, source_target_pairs={{0,2},{1,3},{2,0},{3,1},{4,6},{5,7},{6,4},{7,5},{8,10},{9,11},{10,... | collective-permute-start | bytes 1327112 | tf_op jit(solution)/shard_map/ppermute | solution.py:345
  7.2 27.3 %collective-permute-start.3 = (bf16[96,2304]{1,0:T(8,128)(2,1)}, bf16[96,2304]{1,0:T(8,128)(2,1)S(1)}, u32[]{:S(2)}, u32[]{:S(2)}) collective-permute-start(bf16[96,2304]{1,0:T(8,128)(2,1)} %refs_0_.4), channel_id=1, source_target_pairs={{0,1},{1,0},{2,3},{3,2},{4,5},{5,4},{6,7},{7,6},{8,9},{9,8},{10,11... | collective-permute-start | bytes 1327112 | tf_op jit(solution)/shard_map/ppermute | solution.py:345
  7.6 17.0 %collective-permute-start.7 = (bf16[96,1152]{1,0:T(8,128)(2,1)}, bf16[96,1152]{1,0:T(8,128)(2,1)S(1)}, u32[]{:S(2)}, u32[]{:S(2)}) collective-permute-start(bf16[96,1152]{1,0:T(8,128)(2,1)} %refs_4_.4), channel_id=1, source_target_pairs={{0,2},{1,3},{2,0},{3,1},{4,6},{5,7},{6,4},{7,5},{8,10},{9,11},{10,... | collective-permute-start | bytes 663560 | tf_op jit(solution)/shard_map/ppermute | solution.py:345
  10.0 15.1 %collective-permute-start.6 = (bf16[96,1152]{1,0:T(8,128)(2,1)}, bf16[96,1152]{1,0:T(8,128)(2,1)S(1)}, u32[]{:S(2)}, u32[]{:S(2)}) collective-permute-start(bf16[96,1152]{1,0:T(8,128)(2,1)} %refs_4_.4), channel_id=1, source_target_pairs={{0,1},{1,0},{2,3},{3,2},{4,5},{5,4},{6,7},{7,6},{8,9},{9,8},{10,11... | collective-permute-start | bytes 663560 | tf_op jit(solution)/shard_map/ppermute | solution.py:345
  25.2 11.0 %collective-permute-start.13 = (bf16[96,1536]{1,0:T(8,128)(2,1)}, bf16[96,1536]{1,0:T(8,128)(2,1)S(1)}, u32[]{:S(2)}, u32[]{:S(2)}) collective-permute-start(bf16[96,1536]{1,0:T(8,128)(2,1)} %refs_4_.3), channel_id=1, source_target_pairs={{0,2},{1,3},{2,0},{3,1},{4,6},{5,7},{6,4},{7,5},{8,10},{9,11},{10,... | collective-permute-start | bytes 884744 | tf_op jit(solution)/shard_map/ppermute | solution.py:345
  29.9 11.9 %collective-permute-start.16 = (bf16[384,384]{1,0:T(8,128)(2,1)}, bf16[384,384]{1,0:T(8,128)(2,1)S(1)}, u32[]{:S(2)}, u32[]{:S(2)}) collective-permute-start(bf16[384,384]{1,0:T(8,128)(2,1)} %refs_8_), channel_id=1, source_target_pairs={{0,2},{1,3},{2,0},{3,1},{4,6},{5,7},{6,4},{7,5},{8,10},{9,11},{10,... | collective-permute-start | bytes 884744 | tf_op jit(solution)/shard_map/ppermute | solution.py:345
  29.9 11.9 %collective-permute-start.5 = (bf16[96,2304]{1,0:T(8,128)(2,1)S(1)}, bf16[96,2304]{1,0:T(8,128)(2,1)S(1)}, u32[]{:S(2)}, u32[]{:S(2)}) collective-permute-start(bf16[96,2304]{1,0:T(8,128)(2,1)S(1)} %collective-permute-done.4.refs_2_), channel_id=1, source_target_pairs={{0,1},{1,0},{2,3},{3,2},{4,5},{5,4},{6,7},{7,6},{8,9},{9,8},{10,11... | collective-permute-start | bytes 1327112 | tf_op jit(solution)/shard_map/ppermute | solution.py:345
  34.2 25.3 %collective-permute-start.12 = (bf16[96,1536]{1,0:T(8,128)(2,1)}, bf16[96,1536]{1,0:T(8,128)(2,1)S(1)}, u32[]{:S(2)}, u32[]{:S(2)}) collective-permute-start(bf16[96,1536]{1,0:T(8,128)(2,1)} %refs_4_.3), channel_id=1, source_target_pairs={{0,1},{1,0},{2,3},{3,2},{4,5},{5,4},{6,7},{7,6},{8,9},{9,8},{10,11... | collective-permute-start | bytes 884744 | tf_op jit(solution)/shard_map/ppermute | solution.py:345
  34.5 25.0 %collective-permute-start.15 = (bf16[384,384]{1,0:T(8,128)(2,1)}, bf16[384,384]{1,0:T(8,128)(2,1)S(1)}, u32[]{:S(2)}, u32[]{:S(2)}) collective-permute-start(bf16[384,384]{1,0:T(8,128)(2,1)} %refs_8_), channel_id=1, source_target_pairs={{0,1},{1,0},{2,3},{3,2},{4,5},{5,4},{6,7},{7,6},{8,9},{9,8},{10,11... | collective-permute-start | bytes 884744 | tf_op jit(solution)/shard_map/ppermute | solution.py:345
  36.2 23.3 %collective-permute-start.11 = (bf16[96,384]{1,0:T(8,128)(2,1)S(1)}, bf16[96,384]{1,0:T(8,128)(2,1)S(1)}, u32[]{:S(2)}, u32[]{:S(2)}) collective-permute-start(bf16[96,384]{1,0:T(8,128)(2,1)S(1)} %collective-permute-done.10.refs_2_), channel_id=1, source_target_pairs={{0,1},{1,0},{2,3},{3,2},{4,5},{5,4},{6,7},{7,6},{8,9},{9,8},{10,11... | collective-permute-start | bytes 221192 | tf_op jit(solution)/shard_map/ppermute | solution.py:345
  41.8 17.7 %collective-permute-start.14 = (bf16[96,1536]{1,0:T(8,128)(2,1)S(1)}, bf16[96,1536]{1,0:T(8,128)(2,1)S(1)}, u32[]{:S(2)}, u32[]{:S(2)}) collective-permute-start(bf16[96,1536]{1,0:T(8,128)(2,1)S(1)} %collective-permute-done.13.refs_6_), channel_id=1, source_target_pairs={{0,1},{1,0},{2,3},{3,2},{4,5},{5,4},{6,7},{7,6},{8,9},{9,8},{10,11... | collective-permute-start | bytes 884744 | tf_op jit(solution)/shard_map/ppermute | solution.py:345
  41.8 17.7 %collective-permute-start.17 = (bf16[384,384]{1,0:T(8,128)(2,1)S(1)}, bf16[384,384]{1,0:T(8,128)(2,1)S(1)}, u32[]{:S(2)}, u32[]{:S(2)}) collective-permute-start(bf16[384,384]{1,0:T(8,128)(2,1)S(1)} %collective-permute-done.16.refs_10_), channel_id=1, source_target_pairs={{0,1},{1,0},{2,3},{3,2},{4,5},{5,4},{6,7},{7,6},{8,9},{9,8},{10,11... | collective-permute-start | bytes 884744 | tf_op jit(solution)/shard_map/ppermute | solution.py:345
  126.1 11.5 %collective-permute-start.32 = (bf16[2,96,1152]{2,1,0:T(8,128)(2,1)}, bf16[2,96,1152]{2,1,0:T(8,128)(2,1)S(1)}, u32[]{:S(2)}, u32[]{:S(2)}) collective-permute-start(bf16[2,96,1152]{2,1,0:T(8,128)(2,1)} %get-tuple-element.67), channel_id=1, source_target_pairs={{0,1},{1,0},{2,3},{3,2},{4,5},{5,4},{6,7},{7,6},{8,9},{9,8},{10,11... | collective-permute-start | bytes 1327112 | tf_op jit(solution)/shard_map/ppermute | solution.py:345
  131.8 10.7 %collective-permute-start.19 = (bf16[16,1920]{1,0:T(8,128)(2,1)S(1)}, bf16[16,1920]{1,0:T(8,128)(2,1)S(1)}, u32[]{:S(2)}, u32[]{:S(2)}) collective-permute-start(bf16[16,1920]{1,0:T(8,128)(2,1)S(1)} %copy-done.8), channel_id=1, source_target_pairs={{0,16},{1,17},{2,18},{3,19},{4,20},{5,21},{6,22},{7,23},{8,24},{9,... | collective-permute-start | bytes 184328 | tf_op jit(solution)/shard_map/ppermute | solution.py:345
  136.9 37.7 %collective-permute-start.40 = (bf16[2,96,1920]{2,1,0:T(8,128)(2,1)}, bf16[2,96,1920]{2,1,0:T(8,128)(2,1)S(1)}, u32[]{:S(2)}, u32[]{:S(2)}) collective-permute-start(bf16[2,96,1920]{2,1,0:T(8,128)(2,1)} %get-tuple-element.75), channel_id=1, source_target_pairs={{0,1},{1,0},{2,3},{3,2},{4,5},{5,4},{6,7},{7,6},{8,9},{9,8},{10,11... | collective-permute-start | bytes 2211848 | tf_op jit(solution)/shard_map/ppermute | solution.py:345
  137.7 36.9 %collective-permute-start.41 = (bf16[2,384,384]{2,1,0:T(8,128)(2,1)}, bf16[2,384,384]{2,1,0:T(8,128)(2,1)S(1)}, u32[]{:S(2)}, u32[]{:S(2)}) collective-permute-start(bf16[2,384,384]{2,1,0:T(8,128)(2,1)} %get-tuple-element.76), channel_id=1, source_target_pairs={{0,1},{1,0},{2,3},{3,2},{4,5},{5,4},{6,7},{7,6},{8,9},{9,8},{10,11... | collective-permute-start | bytes 1769480 | tf_op jit(solution)/shard_map/ppermute | solution.py:345
  167.5 60.6 %collective-permute-start.31 = (bf16[4,4,16,768]{3,2,1,0:T(8,128)(2,1)S(1)}, bf16[4,4,16,768]{3,2,1,0:T(8,128)(2,1)S(1)}, u32[]{:S(2)}, u32[]{:S(2)}) collective-permute-start(bf16[4,4,16,768]{3,2,1,0:T(8,128)(2,1)S(1)} %pad_maximum_fusion.1.l0), channel_id=1, source_target_pairs={{0,1},{1,0},{2,3},{3,2},{4,5},{5,4},{6,7},{7,6},{8,9},{9,8},{10,11... | collective-permute-start | bytes 1179656 | tf_op jit(solution)/shard_map/ppermute | solution.py:345
  174.5 53.6 %collective-permute-start.24 = (bf16[4,4,16,1920]{3,2,1,0:T(8,128)(2,1)S(1)}, bf16[4,4,16,1920]{3,2,1,0:T(8,128)(2,1)S(1)}, u32[]{:S(2)}, u32[]{:S(2)}) collective-permute-start(bf16[4,4,16,1920]{3,2,1,0:T(8,128)(2,1)S(1)} %pad_maximum_fusion.e0), channel_id=1, source_target_pairs={{0,1},{1,0},{2,3},{3,2},{4,5},{5,4},{6,7},{7,6},{8,9},{9,8},{10,11... | collective-permute-start | bytes 2949128 | tf_op jit(solution)/shard_map/ppermute | solution.py:345
  193.8 12.7 %collective-permute-start.53 = (bf16[192,384]{1,0:T(8,128)(2,1)S(1)}, bf16[192,384]{1,0:T(8,128)(2,1)S(1)}, u32[]{:S(2)}, u32[]{:S(2)}) collective-permute-start(bf16[192,384]{1,0:T(8,128)(2,1)S(1)} %add_convert_fusion.3), channel_id=1, source_target_pairs={{0,16},{1,17},{2,18},{3,19},{4,20},{5,21},{6,22},{7,23},{8,24},{9,... | collective-permute-start | bytes 442376 | tf_op jit(solution)/shard_map/ppermute | solution.py:345
  199.5 10.7 %collective-permute-start.45 = (bf16[48,1920]{1,0:T(8,128)(2,1)S(1)}, bf16[48,1920]{1,0:T(8,128)(2,1)S(1)}, u32[]{:S(2)}, u32[]{:S(2)}) collective-permute-start(bf16[48,1920]{1,0:T(8,128)(2,1)S(1)} %add_convert_fusion.1), channel_id=1, source_target_pairs={{0,8},{1,9},{2,10},{3,11},{4,12},{5,13},{6,14},{7,15},{8,0},{9,1},... | collective-permute-start | bytes 552968 | tf_op jit(solution)/shard_map/ppermute | solution.py:345
  206.6 15.4 %collective-permute-start.46 = (bf16[48,1920]{1,0:T(8,128)(2,1)S(1)}, bf16[48,1920]{1,0:T(8,128)(2,1)S(1)}, u32[]{:S(2)}, u32[]{:S(2)}) collective-permute-start(bf16[48,1920]{1,0:T(8,128)(2,1)S(1)} %add_convert_fusion.1), channel_id=1, source_target_pairs={{0,16},{1,17},{2,18},{3,19},{4,20},{5,21},{6,22},{7,23},{8,24},{9,... | collective-permute-start | bytes 552968 | tf_op jit(solution)/shard_map/ppermute | solution.py:345
  207.3 14.7 %collective-permute-start.47 = (bf16[48,1920]{1,0:T(8,128)(2,1)S(1)}, bf16[48,1920]{1,0:T(8,128)(2,1)S(1)}, u32[]{:S(2)}, u32[]{:S(2)}) collective-permute-start(bf16[48,1920]{1,0:T(8,128)(2,1)S(1)} %add_convert_fusion.1), channel_id=1, source_target_pairs={{0,24},{1,25},{2,26},{3,27},{4,28},{5,29},{6,30},{7,31},{8,16},{9,... | collective-permute-start | bytes 552968 | tf_op jit(solution)/shard_map/ppermute | solution.py:345
  210.2 16.7 %collective-permute-start.55 = (bf16[192,384]{1,0:T(8,128)(2,1)S(1)}, bf16[192,384]{1,0:T(8,128)(2,1)S(1)}, u32[]{:S(2)}, u32[]{:S(2)}) collective-permute-start(bf16[192,384]{1,0:T(8,128)(2,1)S(1)} %add_convert_fusion.2), channel_id=1, source_target_pairs={{0,4},{1,5},{2,6},{3,7},{4,0},{5,1},{6,2},{7,3},{8,12},{9,13},{10,... | collective-permute-start | bytes 442376 | tf_op jit(solution)/shard_map/ppermute | solution.py:345
  222.0 17.4 %collective-permute-start.48 = (bf16[48,1920]{1,0:T(8,128)(2,1)S(1)}, bf16[48,1920]{1,0:T(8,128)(2,1)}, u32[]{:S(2)}, u32[]{:S(2)}) collective-permute-start(bf16[48,1920]{1,0:T(8,128)(2,1)S(1)} %add_convert_fusion), channel_id=1, source_target_pairs={{0,4},{1,5},{2,6},{3,7},{4,0},{5,1},{6,2},{7,3},{8,12},{9,13},{10,... | collective-permute-start | bytes 552968 | tf_op jit(solution)/shard_map/ppermute | solution.py:345
  (56 other events, 472.5 us)

commit v2 on v1

v2 whole, which is shorter than its diff:
```python
import functools
import math

import jax
import jax.numpy as jnp
from jax import lax
from jax.experimental import pallas as pl
from jax.experimental.pallas import tpu as pltpu
from jax.sharding import PartitionSpec as P

HEADS = 6
F32 = jnp.float32
BF16 = jnp.bfloat16
EPS = 1e-06
GELU_C = math.sqrt(2.0 / math.pi)
GELU_A = 0.044715


def nn(a, b):
    return lax.dot_general(a, b, (((1,), (0,)), ((), ())), preferred_element_type=F32)


def nt(a, b):
    return lax.dot_general(a, b, (((1,), (1,)), ((), ())), preferred_element_type=F32)


def tn(a, b):
    return lax.dot_general(a, b, (((0,), (0,)), ((), ())), preferred_element_type=F32)


def norm_parts(x):
    centred = x - jnp.mean(x, axis=-1, keepdims=True)
    rstd = lax.rsqrt(jnp.mean(centred * centred, axis=-1, keepdims=True) + EPS)
    return centred * rstd, rstd


def norm_back(normed, rstd, grad):
    inner = jnp.mean(grad, axis=-1, keepdims=True)
    along = jnp.mean(grad * normed, axis=-1, keepdims=True)
    return rstd * (grad - inner - normed * along)


def piece_copies(mine, pieces, whole, sems):
    rows = pieces[0].shape[0]
    return [
        pltpu.make_async_copy(
            piece,
            whole.at[pl.ds(pl.multiple_of(jnp.bitwise_xor(mine, k) * rows, 32), rows)],
            sems.at[k],
        )
        for k, piece in enumerate(pieces)
    ]


def half_mask(shape, half):
    lane = lax.broadcasted_iota(jnp.int32, shape, len(shape) - 1)
    return (lane < shape[-1] // 2) if half == 0 else (lane >= shape[-1] // 2)


def condition(info, cond, b_ada, b_qv, b_o, b_1, b_2, *refs):
    cuts, share, packed = refs[0:4], refs[4], refs[5]
    c = cond[...].astype(F32)
    cs = c / (1.0 + jnp.exp(-c))
    cut = cs.shape[1] // 4
    for k, ref in enumerate(cuts):
        mine = jnp.bitwise_xor(info[0], k)
        ref[...] = sum(
            jnp.where(mine == j, cs[:, j * cut : (j + 1) * cut], 0.0) for j in range(4)
        ).astype(BF16)
    share[...] = jnp.zeros_like(share)
    n = b_ada.shape[0]
    row = b_ada[...].astype(F32).reshape(1, n)
    for j in range(4):

        @pl.when(info[0] == j)
        def _():
            share[:, j * n : (j + 1) * n] = row

    packed[...] = jnp.zeros_like(packed)
    for i, b in enumerate((b_qv, b_o, b_1, b_2)):
        packed[i : i + 1, 0 : b.shape[0]] = b[...].astype(F32).reshape(1, b.shape[0])


def ada_parts(info, c0, c1, c2, c3, w_ada, share, packed, *outs):
    for cut, out in zip((c0, c1, c2, c3), outs):
        n = w_ada.shape[1]
        out[:, 0:n] = nn(cut[...], w_ada[...]) + share[...]
        out[:, n:] = packed[...]


def bias_row(table, at, n):
    return jnp.concatenate([table[i, at : at + 1, 0:n] for i in range(4)], axis=1)


def attn_fwd(info, tok, *refs, per):
    parts, wq = refs[0:4], refs[4:8]
    m1_o, qkv_o, p_o, att_o, ada, table = refs[8:14]
    wq_s, bias_s, sem_q = refs[14:]
    step = pl.program_id(0)
    width = tok.shape[-1]

    @pl.when(step == 0)
    def _():
        cq = piece_copies(info[0], wq, wq_s, sem_q)
        for copy in cq:
            copy.start()
        ada[...] = sum(v[:, 0 : 6 * width] for v in parts)
        for k in range(4):
            table[jnp.bitwise_xor(info[0], k)] = parts[k][:, 6 * width :]
        row_qv = bias_row(table, 0, width // 2)
        bias_s[:, 0:width] = row_qv[:, 0:width]
        bias_s[:, width : 2 * width] = jnp.zeros((1, width), F32)
        bias_s[:, 2 * width : 3 * width] = row_qv[:, width : 2 * width]
        for copy in cq:
            copy.wait()

    qkvs, ss, ps, atts = {}, {}, {}, {}
    part = lambda l, at, j: qkvs[l][:, at + 128 * j : at + 128 * j + 128]

    def stage_q(l):
        row = pl.ds(step * per + l, 1)
        shift = ada[row, 0:width]
        scale = ada[row, width : 2 * width]
        n1, _ = norm_parts(tok[l].astype(F32))
        m1 = (n1 * (1.0 + scale) + shift).astype(BF16)
        m1_o[l] = m1
        qkvs[l] = (nn(m1, wq_s[...]) + bias_s[...]).astype(BF16)
        qkv_o[l] = qkvs[l]

    def stage_a(u):
        l, t = divmod(u, HEADS)
        j, h = t // 2, t % 2
        k = part(l, width, j)
        ss[u] = nt(jnp.where(half_mask(k.shape, h), k, jnp.zeros_like(k)), part(l, 0, j))

    def stage_b(u):
        l, t = divmod(u, HEADS)
        s = ss[u]
        top = jnp.max(s, axis=0, keepdims=True)
        e = jnp.exp((s - top) * 0.125)
        total = jnp.sum(e, axis=0, keepdims=True)
        ps[u] = (e * (1.0 / total)).astype(BF16)
        p_o[l, t] = ps[u]

    def stage_c(u):
        l, t = divmod(u, HEADS)
        j = t // 2
        atts[u] = tn(ps[u], part(l, 2 * width, j))
        if t % 2:
            att = jnp.where(half_mask(atts[u].shape, 0), atts[u - 1], atts[u])
            att_o[l, :, 128 * j : 128 * j + 128] = att.astype(BF16)

    n = HEADS * per
    stage_q(0)
    for u in range(n + 2):
        if u < n:
            stage_a(u)
        if u % HEADS == 1 and u // HEADS + 1 < per:
            stage_q(u // HEADS + 1)
        if 0 <= u - 1 < n:
            stage_b(u - 1)
        if 0 <= u - 2 < n:
            stage_c(u - 2)


def ffn_both(info, tok, att_i, dy_i, ada, cond, table, *refs, per, chunk):
    wo, w1, w2 = refs[0:4], refs[4:8], refs[8:12]
    out_o, dx1_o, datt_o, early_o, keep_o, send_o = refs[12:18]
    wo_s, w1_s, w2_s, go_s, g1_s, g2_s, small_s, gb_s, bo_s, b1_s, b2_s, sem_o, sem_1, sem_2 = refs[18:]
    step = pl.program_id(0)
    length, width = tok.shape[1:]
    hidden = w1_s.shape[1]

    @pl.when(step == 0)
    def _():
        copies = (
            piece_copies(info[0], wo, wo_s, sem_o)
            + piece_copies(info[0], w1, w1_s, sem_1)
            + piece_copies(info[0], w2, w2_s, sem_2)
        )
        for copy in copies:
            copy.start()
        go_s[...] = jnp.zeros_like(go_s)
        g1_s[...] = jnp.zeros_like(g1_s)
        g2_s[...] = jnp.zeros_like(g2_s)
        gb_s[...] = jnp.zeros_like(gb_s)
        bo_s[...] = bias_row(table, 1, width // 4)
        b1_s[...] = bias_row(table, 2, hidden // 4)
        b2_s[...] = bias_row(table, 3, width // 4)
        c = cond[...].astype(F32)
        small_s[:, 4 * width : 5 * width] = c / (1.0 + jnp.exp(-c))
        for copy in copies:
            copy.wait()

    def rows_of(at):
        return jnp.stack(
            [ada[pl.ds(step * per + l, 1), at * width : (at + 1) * width] for l in range(per)]
        )

    def flat(v):
        return v.reshape(per * length, v.shape[-1])

    def deep(v):
        return v.reshape(per, length, v.shape[-1])

    gate1, shift2, scale2, gate2 = rows_of(2), rows_of(3), rows_of(4), rows_of(5)
    att = flat(att_i[...])
    branch = deep(nn(att, wo_s[...]) + bo_s[...])
    x1 = tok[...].astype(F32) + gate1 * branch
    n2, rstd2 = norm_parts(x1)
    m2 = flat((n2 * (1.0 + scale2) + shift2).astype(BF16))
    dy = dy_i[...].astype(F32)
    df = flat((dy * gate2).astype(BF16))
    df_t = df.T
    m2_t = m2.T
    ffn = None
    dm2 = None
    for j in range(hidden // chunk):
        cols = slice(j * chunk, (j + 1) * chunk)
        h = nn(m2, w1_s[:, cols]) + b1_s[:, cols]
        hh = h * h
        t = jnp.tanh(h * (GELU_C + (GELU_C * GELU_A) * hh))
        half_t = 0.5 + 0.5 * t
        g = (h * half_t).astype(BF16)
        slope = half_t + (0.5 * h) * (1.0 - t * t) * (GELU_C + (3.0 * GELU_C * GELU_A) * hh)
        part = nn(g, w2_s[cols, :])
        ffn = part if ffn is None else ffn + part
        g2_s[:, cols] += nn(df_t, g)
        dh32 = nt(df, w2_s[cols, :]) * slope
        dh = dh32.astype(BF16)
        gb_s[0:1, cols] += jnp.sum(dh.astype(F32), axis=0, keepdims=True)
        g1_s[:, cols] += nn(m2_t, dh)
        part = nt(dh, w1_s[:, cols])
        dm2 = part if dm2 is None else dm2 + part
    ffn = deep(ffn + b2_s[...])
    dm2 = deep(dm2)
    out_o[...] = (x1 + gate2 * ffn).astype(BF16)
    gb_s[1:2, width : 2 * width] += jnp.sum(df.astype(F32), axis=0, keepdims=True)
    d_gate2 = jnp.sum(dy * ffn, axis=1)
    d_scale2 = jnp.sum(dm2 * n2, axis=1)
    d_shift2 = jnp.sum(dm2, axis=1)
    dx1 = dy + norm_back(n2, rstd2, dm2 * (1.0 + scale2))
    dx1_o[...] = dx1
    do = flat((dx1 * gate1).astype(BF16))
    d_gate1 = jnp.sum(dx1 * branch, axis=1)
    for l in range(per):
        row = pl.ds(step * per + l, 1)
        small_s[row, 0:width] = d_gate1[l : l + 1]
        small_s[row, width : 2 * width] = d_shift2[l : l + 1]
        small_s[row, 2 * width : 3 * width] = d_scale2[l : l + 1]
        small_s[row, 3 * width : 4 * width] = d_gate2[l : l + 1]
    gb_s[1:2, 0:width] += jnp.sum(do.astype(F32), axis=0, keepdims=True)
    go_s[...] += tn(att, do)
    datt_o[...] = deep(nt(do, wo_s[...]).astype(BF16))

    @pl.when(step == pl.num_programs(0) - 1)
    def _():
        for i in range(5):
            early_o[8 * i : 8 * i + 8, :] = small_s[:, i * width : (i + 1) * width].astype(BF16)
        pack = [gb_s[0:1, i * width : (i + 1) * width] for i in range(hidden // width)]
        pack += [gb_s[1:2, 0:width], gb_s[1:2, width : 2 * width]]
        pack += [jnp.zeros((1, width), F32)] * (8 - len(pack))
        early_o[40:48, :] = jnp.concatenate(pack, axis=0).astype(BF16)
        core = jnp.bitwise_and(info[0], 1)
        half = width // 8
        for y in range(2):
            for which, ref in enumerate((keep_o, send_o)):
                shard = 2 * y + jnp.bitwise_xor(core, which)
                for x in range(2):
                    take = pl.ds(pl.multiple_of(shard * 2 * half + x * half, 8), half)
                    wide = pl.ds(pl.multiple_of(shard * width, 128), width)
                    for z in range(4):
                        at = 2 * half * z
                        ref[y, x, at : at + half, :] = g1_s[
                            take, z * width : (z + 1) * width
                        ].astype(BF16)
                        rows = slice((4 * x + z) * half, (4 * x + z + 1) * half)
                        ref[y, x, at + half : at + 2 * half, :] = g2_s[rows, wide].astype(BF16)
                    ref[y, x, 8 * half : 9 * half, :] = go_s[take, :].astype(BF16)


def attn_bwd(info, tok, m1_i, qkv_i, p_i, datt_i, dx1_i, ada, *refs, per, base, last):
    wq, refs = refs[0:4], refs[4:]
    step = pl.program_id(0)
    length, width = tok.shape[1:]
    if last:
        _, g_i, small_i, gb_i = refs[0:4]
        gtok_o, late_o, keep_o, send_o = refs[4:8]
        wq_s, sem_q, g_s, small_s, gb_s = refs[8:]
    else:
        gtok_o, g_s, small_s, gb_s, wq_s, sem_q = refs

    @pl.when(step == 0)
    def _():
        copies = piece_copies(info[0], wq, wq_s, sem_q)
        for copy in copies:
            copy.start()
        if last:
            g_s[...] = g_i[...]
            small_s[...] = small_i[...]
            gb_s[...] = gb_i[...]
        else:
            g_s[...] = jnp.zeros_like(g_s)
            small_s[...] = jnp.zeros_like(small_s)
            gb_s[...] = jnp.zeros_like(gb_s)
        for copy in copies:
            copy.wait()

    part = lambda ref, l, at, j: ref[l, :, at + 128 * j : at + 128 * j + 128]
    dvs, dps, dss, dks, dqs, dqkvs, dm1s = {}, {}, {}, {}, {}, {}, {}

    def stage_a(u):
        l, t = divmod(u, HEADS)
        j, h = t // 2, t % 2
        v, datt = part(qkv_i, l, 2 * width, j), part(datt_i, l, 0, j)
        vm = jnp.where(half_mask(v.shape, h), v, jnp.zeros_like(v))
        dps[u] = nt(vm, datt)
        dvs[u] = nn(p_i[l, t], datt)

    def stage_b(u):
        l, t = divmod(u, HEADS)
        p32 = p_i[l, t].astype(F32)
        pd = p32 * dps[u]
        dss[u] = (pd - p32 * jnp.sum(pd, axis=0, keepdims=True)).astype(BF16)

    def stage_c(u):
        l, t = divmod(u, HEADS)
        j = t // 2
        dks[u] = nn(dss[u], part(qkv_i, l, 0, j)) * 0.125
        dqs[u] = tn(dss[u], part(qkv_i, l, width, j)) * 0.125

    def stage_f(l):
        grads = [
            jnp.where(half_mask(d[u].shape, 0), d[u], d[u + 1]).astype(BF16)
            for d in (dqs, dks, dvs)
            for u in range(l * HEADS, (l + 1) * HEADS, 2)
        ]
        dqkvs[l] = jnp.concatenate(grads, axis=-1)
        dm1s[l] = nt(dqkvs[l], wq_s[...])
        g_s[...] += nn(m1_i[l].T, dqkvs[l])

    def stage_g(l):
        dqkv, dm1 = dqkvs[l], dm1s[l]
        row = pl.ds(base + step * per + l, 1)
        scale = ada[row, width : 2 * width]
        n1, rstd1 = norm_parts(tok[l].astype(F32))
        sums = jnp.sum(dqkv.astype(F32), axis=0, keepdims=True)
        gb_s[0:1, :] += sums[:, 0:width]
        gb_s[1:2, :] += sums[:, 2 * width : 3 * width]
        small_s[row, 0:width] = jnp.sum(dm1, axis=0, keepdims=True)
        small_s[row, width : 2 * width] = jnp.sum(dm1 * n1, axis=0, keepdims=True)
        gtok_o[l] = dx1_i[l] + norm_back(n1, rstd1, dm1 * (1.0 + scale))

    n = HEADS * per
    for u in range(n + 2 + 0 + 0):
        if u < n:
            stage_a(u)
        if 0 <= u - 1 < n:
            stage_b(u - 1)
        if 0 <= u - 2 < n:
            stage_c(u - 2)
        f = u - 2 - 0
        if 0 <= f < n and f % HEADS == HEADS - 1:
            stage_f(f // HEADS)
        g = f - 0
        if 0 <= g < n and g % HEADS == HEADS - 1:
            stage_g(g // HEADS)

    if last:

        @pl.when(step == pl.num_programs(0) - 1)
        def _():
            for i in range(2):
                late_o[8 * i : 8 * i + 8, :] = small_s[:, i * width : (i + 1) * width].astype(BF16)
            late_o[16:24, :] = gb_s[...].astype(BF16)
            core = jnp.bitwise_and(info[0], 1)
            half = width // 8
            for y in range(2):
                for which, ref in enumerate((keep_o, send_o)):
                    shard = 2 * y + jnp.bitwise_xor(core, which)
                    for x in range(2):
                        take = pl.ds(pl.multiple_of(shard * 2 * half + x * half, 8), half)
                        ref[y, x] = g_s[take, :].astype(BF16)


def tree_sum(values):
    values = [v.astype(F32) for v in values]
    while len(values) > 1:
        values = [values[2 * i] + values[2 * i + 1] for i in range(len(values) // 2)]
    return values[0]


def ordered(values, me):
    bit = 1
    while bit < len(values):
        flip = (me & bit) != 0
        values = [jnp.where(flip, values[i ^ bit], values[i]) for i in range(len(values))]
        bit *= 2
    return values


def after(values, *deps):
    flat, tree = jax.tree.flatten(values)
    out = lax.optimization_barrier(tuple(flat) + tuple(deps))
    return jax.tree.unflatten(tree, out[: len(flat)])


def full(shape):
    return pl.BlockSpec(shape, lambda *_: (0,) * len(shape))


def call(body, info, operands, specs, outs, out_specs, scratch, grid, vmem, flops, traffic, exps=0, alias=None):
    return pl.pallas_call(
        body,
        out_shape=outs,
        input_output_aliases=alias or {},
        grid_spec=pltpu.PrefetchScalarGridSpec(
            num_scalar_prefetch=1,
            grid=grid,
            in_specs=specs,
            out_specs=out_specs,
            scratch_shapes=scratch,
        ),
        compiler_params=pltpu.CompilerParams(
            dimension_semantics=("arbitrary",) * len(grid), vmem_limit_bytes=vmem << 20
        ),
        cost_estimate=pl.CostEstimate(flops=flops, bytes_accessed=traffic, transcendentals=exps),
    )(info, *operands)


def on_device(
    latent_tokens, cond, w_ada, b_ada, w_qkv, b_qv, w_o, b_o, w_1, b_1, w_2, b_2, grad_out
):
    count, length, width = latent_tokens.shape
    hidden = w_1.shape[1]
    quarter, half = width // 4, width // 8
    reps = lax.axis_size("rep")
    shards = lax.axis_size("shard")
    s = lax.axis_index("shard")
    r = lax.axis_index("rep")
    y_at, x_at, z_at = s >> 1, r & 1, r >> 1
    n_z = reps // 2
    info = jnp.stack([s, y_at, x_at, z_at]).astype(jnp.int32)

    def swap(v, shard_bits=0, rep_bits=0):
        pairs = [
            (i * shards + j, (i ^ rep_bits) * shards + (j ^ shard_bits))
            for i in range(reps)
            for j in range(shards)
        ]
        return lax.ppermute(v, ("rep", "shard"), pairs)

    whole = lambda vs: [full(v.shape) for v in vs]
    ins = (cond, b_ada, b_qv, b_o, b_1, b_2)
    outs = [jax.ShapeDtypeStruct((count, quarter), BF16)] * 4 + [
        jax.ShapeDtypeStruct((1, 6 * width), F32),
        jax.ShapeDtypeStruct((8, width), F32),
    ]
    *cuts, share, packed = call(
        condition, info, ins, whole(ins), outs, whole(outs), [], (1,), 60, 0, 1 << 17
    )
    near_qkv, far_qkv = after((w_qkv, w_qkv), cuts[0])
    cuts = [cuts[0]] + [swap(cuts[k], k) for k in range(1, 4)]
    near_qkv, far_qkv = swap(near_qkv, 1), swap(far_qkv, 2)
    ffn_w = (w_o, w_1, w_2)
    near_w = [swap(v, 1) for v in after(ffn_w, cuts[1])]
    ins = tuple(cuts) + (w_ada, share, packed)
    outs = [jax.ShapeDtypeStruct((count, 7 * width), F32)] * 4
    parts = call(ada_parts, info, ins, whole(ins), outs, whole(outs), [], (1,), 60, 1 << 24, 1 << 20)
    sent = parts[0]
    p_qkv = (w_qkv, near_qkv, far_qkv, swap(far_qkv, 1))
    parts = [parts[0]] + [swap(parts[k], k) for k in range(1, 4)]
    far_w = [swap(v, 2) for v in after(ffn_w, sent)]

    anyspec = pl.BlockSpec(memory_space=pl.ANY)
    dma4 = pltpu.SemaphoreType.DMA((4,))
    tokens = count * length

    per = 2
    per3 = 1
    lat = lambda *tail: pl.BlockSpec((per,) + tail, lambda i, _: (i,) + (0,) * len(tail))
    m1, qkv, probs, att, ada, table = call(
        functools.partial(attn_fwd, per=per),
        info,
        (latent_tokens,) + tuple(parts) + p_qkv,
        [lat(length, width)] + [full(v.shape) for v in parts] + [anyspec] * 4,
        [
            jax.ShapeDtypeStruct((count, length, width), BF16),
            jax.ShapeDtypeStruct((count, length, 3 * width), BF16),
            jax.ShapeDtypeStruct((count, HEADS, length, length), BF16),
            jax.ShapeDtypeStruct((count, length, width), BF16),
            jax.ShapeDtypeStruct((count, 6 * width), F32),
            jax.ShapeDtypeStruct((4, 8, width), F32),
        ],
        [
            lat(length, width),
            lat(length, 3 * width),
            lat(HEADS, length, length),
            lat(length, width),
            full((count, 6 * width)),
            full((4, 8, width)),
        ],
        [pltpu.VMEM((width, 3 * width), BF16), pltpu.VMEM((1, 3 * width), F32), dma4],
        (count // per,),
        60,
        8 * tokens * width * width + 8 * tokens * length * width,
        20 * tokens * width,
        tokens * length * HEADS,
    )

    far_w = after(far_w, table)
    p_o, p_1, p_2 = ((v, near, far, swap(far, 1)) for v, near, far in zip(ffn_w, near_w, far_w))

    per2 = 2 if count % 2 == 0 else 1
    lat2 = lambda *tail: pl.BlockSpec((per2,) + tail, lambda i, _: (i,) + (0,) * len(tail))
    grads = (2, 2, 9 * half, width)
    block_out, dx1, datt, early, keep_f, send_f = call(
        functools.partial(ffn_both, per=per2, chunk=hidden),
        info,
        (latent_tokens, att, grad_out, ada, cond, table) + p_o + p_1 + p_2,
        [lat2(length, width)] * 3
        + [full(ada.shape), full(cond.shape), full(table.shape)]
        + [anyspec] * 12,
        [
            jax.ShapeDtypeStruct((count, length, width), BF16),
            jax.ShapeDtypeStruct((count, length, width), F32),
            jax.ShapeDtypeStruct((count, length, width), BF16),
            jax.ShapeDtypeStruct((48, width), BF16),
        ]
        + [jax.ShapeDtypeStruct(grads, BF16)] * 2,
        [lat2(length, width)] * 3 + [full((48, width))] + [full(grads)] * 2,
        [
            pltpu.VMEM((width, width), BF16),
            pltpu.VMEM((width, hidden), BF16),
            pltpu.VMEM((hidden, width), BF16),
            pltpu.VMEM((width, width), F32),
            pltpu.VMEM((width, hidden), F32),
            pltpu.VMEM((width, hidden), F32),
            pltpu.VMEM((8, 5 * width), F32),
            pltpu.VMEM((8, 5 * width), F32),
            pltpu.VMEM((1, width), F32),
            pltpu.VMEM((1, hidden), F32),
            pltpu.VMEM((1, width), F32),
            dma4,
            dma4,
            dma4,
        ],
        (count // per2,),
        60,
        12 * tokens * width * hidden + 6 * tokens * width * width,
        14 * tokens * width,
        tokens * hidden,
    )

    def chip_sum(keep, send):
        got = swap(send, 1)

        def part(y, x):
            both = [
                lax.dynamic_index_in_dim(
                    lax.dynamic_index_in_dim(v, y, 0, keepdims=False), x, 0, keepdims=False
                ).astype(F32)
                for v in (keep, got)
            ]
            return (both[0] + both[1]).astype(BF16)

        return [part(y_at ^ (k >> 1), x_at ^ (k & 1)) for k in range(4)]

    def backward(base, last, info, extra, extra_specs, outs, out_specs, scratch, alias):
        half_n = count // 2
        at = lambda *tail: pl.BlockSpec(
            (per3,) + tail, lambda i, _: (i + base // per3,) + (0,) * len(tail)
        )
        return call(
            functools.partial(attn_bwd, per=per3, base=base, last=last),
            info,
            (latent_tokens, m1, qkv, probs, datt, dx1, ada) + p_qkv + extra,
            [
                at(length, width),
                at(length, width),
                at(length, 3 * width),
                at(HEADS, length, length),
                at(length, width),
                at(length, width),
                full(ada.shape),
            ]
            + [anyspec] * 4
            + extra_specs,
            [jax.ShapeDtypeStruct((count, length, width), F32)] + outs,
            [at(length, width)] + out_specs,
            [pltpu.VMEM((width, 3 * width), BF16), dma4] + scratch,
            (half_n // per3,),
            60,
            6 * tokens * width * width + 5 * tokens * length * width,
            15 * tokens * width,
            0,
            alias,
        )

    acc = [(width, 3 * width), (8, 2 * width), (8, width)]
    acc_shapes = [jax.ShapeDtypeStruct(v, F32) for v in acc]
    acc_specs = [full(v) for v in acc]

    def over_plane(own, sends):
        return [own] + [swap(sends[k - 1], 2 * (k >> 1), k & 1) for k in range(1, 4)]

    def over_z(own, sends):
        return [own] + [swap(sends[k - 1], 0, 2 * k) for k in range(1, n_z)]

    first = x_at == 0

    def by_x(mine, yours):
        return jnp.where(first, mine, yours), jnp.where(first, yours, mine)

    def pair(v, shard_bits, rep_bits, second):
        other = swap(v, shard_bits, rep_bits)
        return jnp.concatenate(
            [jnp.where(second, other, v), jnp.where(second, v, other)], axis=0
        )

    def z_pair(v, bit):
        return pair(v, 0, 2 * bit, (z_at & bit) != 0)

    n_f = 9 * half
    n_e = early.shape[0]
    parts_f = chip_sum(keep_f, send_f)
    gtok, g_half, small_half, gb_half = backward(
        0, False, after(info, *parts_f), (), [], acc_shapes, acc_specs, [], None
    )
    got = over_plane(parts_f[0], parts_f[1:])
    early_g = z_pair(after(early, *parts_f), 2)
    bit = 4
    while bit < n_z:
        early_g = z_pair(early_g, bit)
        bit *= 2
    *got, early_g = after(got + [early_g], gb_half)
    total_f = tree_sum(got).astype(BF16)
    z_low = z_at & 3
    loads = [
        jnp.concatenate(
            [
                lax.dynamic_slice_in_dim(total_f, (z_low ^ (k & 3)) * 2 * half, 2 * half, 0),
                total_f[8 * half :],
            ],
            axis=0,
        )
        for k in range(n_z)
    ]
    early_g = pair(early_g, 0, 1, x_at == 1)
    send_shape = (2, 2, half, 3 * width)
    grad_tokens, late, keep_a, send_a = backward(
        count // 2,
        True,
        after(info, *loads),
        (gtok, g_half, small_half, gb_half),
        [anyspec] + acc_specs,
        [
            jax.ShapeDtypeStruct((24, width), BF16),
            jax.ShapeDtypeStruct(send_shape, BF16),
            jax.ShapeDtypeStruct(send_shape, BF16),
        ],
        [full((24, width)), full(send_shape), full(send_shape)],
        [pltpu.VMEM(v, F32) for v in acc],
        {12: 0},
    )
    *got, early_g = after(over_z(loads[0], loads[1:]) + [early_g], late)
    piece_f = tree_sum([v[: 2 * half] for v in got]).astype(BF16)
    out_f = tree_sum([v[2 * half : 3 * half] for v in got]).astype(BF16)

    parts_a = chip_sum(keep_a, send_a)
    n_l = late.shape[0]
    load = z_pair(jnp.concatenate([piece_f, late], axis=0), 1)
    early_g = z_pair(early_g, 1)
    got_a = over_plane(parts_a[0], parts_a[1:])
    load, early_g = after((load, early_g), *parts_a)
    bit = 2
    while bit < n_z:
        load = z_pair(load, bit)
        bit *= 2
    total_a, load, early_g = after((tree_sum(got_a).astype(BF16), load, early_g))
    ring_a = over_z(total_a, [total_a] * (n_z - 1))
    n_p = 2 * half + n_l
    blocks = [load[i * n_p : i * n_p + 2 * half] for i in range(4)]
    late_g = jnp.concatenate([load[i * n_p + 2 * half : (i + 1) * n_p] for i in range(n_z)], axis=0)
    mine_f = jnp.concatenate(blocks + [out_f], axis=0)
    yours_f = swap(mine_f, 0, 1)
    late_g = pair(late_g, 2, 0, y_at == 1)
    early_g = pair(early_g, 2, 0, y_at == 1)
    late_g = pair(late_g, 0, 1, x_at == 1)
    early_g = pair(early_g, 1, 0, (s & 1) == 1)
    late_g = pair(late_g, 1, 0, (s & 1) == 1)

    sides = by_x(mine_f, yours_f)
    deep = [side[: 8 * half].reshape(4, 2 * half, width) for side in sides]
    gw_1 = jnp.concatenate(
        [side[:, :half].transpose(1, 0, 2).reshape(half, hidden) for side in deep], axis=0
    ).astype(F32)
    gw_2 = jnp.concatenate(
        [side[:, half:].reshape(4 * half, width) for side in deep], axis=0
    ).T.astype(F32)
    gw_o = jnp.concatenate([side[8 * half :] for side in sides], axis=0).astype(F32)

    n_h = n_z // 2
    early_r = early_g.reshape(2, 2, 2, 2, n_h, n_e // 8, 8, width)
    early_r = early_r.transpose(0, 3, 1, 4, 2, 5, 6, 7).reshape(2, 2, 2, n_z, n_e // 8, 8, width)
    late_r = late_g.reshape(2, 2, 2, n_z, n_l // 8, 8, width)
    to_rows = lambda v, i: v[:, :, :, :, i].reshape(-1, width)
    cs_all = lax.dynamic_slice_in_dim(to_rows(early_r, 4), s * quarter, quarter, 1)
    d_late = jnp.concatenate([to_rows(late_r, i) for i in range(2)], axis=1)
    d_early = jnp.concatenate([to_rows(early_r, i) for i in range(4)], axis=1)
    contract = lambda v: lax.dot_general(
        cs_all, v, (((0,), (0,)), ((), ())), preferred_element_type=F32
    )
    gw_ada = jnp.concatenate([contract(d_late), contract(d_early)], axis=1)
    gb_ada = jnp.concatenate(
        [jnp.sum(d_late.astype(F32), axis=0), jnp.sum(d_early.astype(F32), axis=0)]
    )
    gb_early = jnp.sum(early_r[:, :, :, :, 5].astype(F32), axis=(0, 1, 2, 3))
    gb_late = jnp.sum(late_r[:, :, :, :, 2, :2].astype(F32), axis=(0, 1, 2, 3)).reshape(-1)

    def group(v, parts):
        v = lax.dynamic_index_in_dim(v, z_at, 3, keepdims=False)
        v = lax.dynamic_index_in_dim(v, x_at, 1, keepdims=False)
        return [v[:, :, i].transpose(1, 0, 2, 3).reshape(4 * 8, width) for i in range(parts)]

    dada = jnp.concatenate(group(late_r, 2) + group(early_r, 4), axis=1)
    dcs = lax.dot_general(dada, w_ada, (((1,), (1,)), ((), ())), preferred_element_type=F32)
    dcs = ordered([dcs[k * 8 : (k + 1) * 8] for k in range(4)], s)
    dcs = ordered([dcs[0]] + [swap(dcs[k], k) for k in range(1, 4)], s)
    c32 = cond.astype(F32)
    sig = 1.0 / (1.0 + jnp.exp(-c32))
    grad_cond = jnp.concatenate(dcs, axis=1) * (sig * (1.0 + c32 * (1.0 - sig)))

    def mine(row):
        part = row.shape[0] // shards
        return lax.dynamic_slice(row, (s * part,), (part,))

    *ring_a, gw_1, gw_2, gw_o = after(ring_a + [gw_1, gw_2, gw_o])
    mine_a = tree_sum(ring_a).astype(BF16)
    gw_qkv = jnp.concatenate(by_x(mine_a, swap(mine_a, 0, 1)), axis=0).astype(F32)

    return (
        block_out,
        grad_tokens,
        grad_cond,
        gw_ada,
        mine(gb_ada),
        gw_qkv,
        mine(gb_late),
        gw_o,
        mine(gb_early[hidden // width]),
        gw_1,
        mine(gb_early[: hidden // width].reshape(-1)),
        gw_2,
        mine(gb_early[hidden // width + 1]),
    )


def solution(mesh):
    lead = P(("rep", "shard"))
    part = P("shard")
    return jax.shard_map(
        on_device,
        mesh=mesh,
        in_specs=(lead, lead) + (part,) * 10 + (lead,),
        out_specs=(lead,) * 3 + (part,) * 10,
        check_vma=False,
    )
```

time: 243 us -> 193 us (0.79)
  starting transfers between devices: 59.1 us -> 43.1 us
  Pallas kernels: 92.8 us -> 76.9 us
  local copies, waits for them, and re-layouts: 18.5 us -> 5.7 us
  waiting for transfers between devices: 63.8 us -> 53.2 us
  other arithmetic: 6.75 us -> 11.4 us
    ppermute x56 -> x47, starting transfers between devices: 59.1 us -> 43.1 us  [swap(): return lax.ppermute(v, ('rep', 'shard'), pairs)]
    pallas_call x6, Pallas kernels: 92.8 us -> 76.9 us  [call(): pl.pallas_call(body, out_shape=outs, input_output_aliases=alias or {}, gr...]
    ppermute x56 -> x47, waiting for transfers between devices: 63.8 us -> 53.2 us  [swap(): return lax.ppermute(v, ('rep', 'shard'), pairs)]
    concatenate x2 -> x1, local copies, waits for them, and re-layouts: 3.47 us -> 0.01 us  [on_device(): dada = jnp.concatenate(group(late_r, 2) + group(early_r, 4), axis=1)]
    slice x9 -> x13, local copies, waits for them, and re-layouts: 3.76 us -> 0.37 us  [the longest x2 0.21 us: on_device(): to_rows = lambda v, i: v[:, :, :, :, i].reshape(-1, width)]
    unnamed x50 -> x56, local copies, waits for them, and re-layouts: 4.95 us -> 3.12 us
  transfers between devices with their start and end apart: 56 -> 47, of which waited for: 23 -> 17; matrix products, arithmetic and copies ran while one was open for 6% -> 5% of each run, Pallas kernels for 11% -> 22%
where the time goes in v2:
time: 193 us
  Pallas kernels  76.9 us (40%)
  waiting for transfers between devices  53.2 us (28%)
  starting transfers between devices  43.1 us (22%)
  other arithmetic  11.4 us (6%)
  local copies, waits for them, and re-layouts  5.7 us (3%)
    pallas_call x6, Pallas kernels, call(): pl.pallas_call(body, out_shape=outs, input_output_aliases=alias or {}, gr...  76.9 us
    ppermute x47, waiting for transfers between devices, swap(): return lax.ppermute(v, ('rep', 'shard'), pairs)  53.2 us
    ppermute x47, starting transfers between devices, swap(): return lax.ppermute(v, ('rep', 'shard'), pairs)  43.1 us
  transfers between devices with their start and end apart: 47, of which 17 were waited for; matrix products, arithmetic and copies ran while one was open for 5% of the time, Pallas kernels for 22%

profile of v2, /device:TPU:0, one launch (start us, length us, event | category | flops | bytes accessed | tf_op | source)
XLA Modules:
  0.0 192.5 jit_solution(7253294875753548885)
XLA Ops:
  1.3 2.2 %shard_map.228 = (bf16[8,96]{1,0:T(8,128)(2,1)}, bf16[8,96]{1,0:T(8,128)(2,1)}, bf16[8,96]{1,0:T(8,128)(2,1)}, bf16[8,96]{1,0:T(8,128)(2,1)}, f32[1,2304]{1,0:T(1,128)}, /*index=5*/f32[8,384]{1,0:T(8,128)}) custom-call(s32[4]{0:T(128)} %pad_add_fusion.info, bf16[8,384]{1,0:T(8,128)(2,1)} %cond.3, bf16[576]{0:T(1024)(128)(2,1)} %b_ada.1, bf16[192]{0:T(256)(128)(2,1)} %b_qv.1, ...), custom_call_target="tpu_custom_call" | custom-call | bytes 131072 | tf_op jit(solution)/shard_map/pallas_call | solution.py:413
  3.5 3.0 %collective-permute-start.7 = (bf16[96,1152]{1,0:T(8,128)(2,1)}, bf16[96,1152]{1,0:T(8,128)(2,1)S(1)}, u32[]{:S(2)}, u32[]{:S(2)}) collective-permute-start(bf16[96,1152]{1,0:T(8,128)(2,1)} %refs_0_.5), channel_id=1, source_target_pairs={{0,2},{1,3},{2,0},{3,1},{4,6},{5,7},{6,4},{7,5},{8,10},{9,11},{10,... | collective-permute-start | bytes 663560 | tf_op jit(solution)/shard_map/ppermute | solution.py:451
  6.4 5.7 %collective-permute-done.7.refs_6_.refs_2_ = bf16[96,1152]{1,0:T(8,128)(2,1)S(1)} collective-permute-done((bf16[96,1152]{1,0:T(8,128)(2,1)}, bf16[96,1152]{1,0:T(8,128)(2,1)S(1)}, u32[]{:S(2)}, u32[]{:S(2)}) %collective-permute-start.7) | collective-permute-done | bytes 221216 | tf_op jit(solution)/shard_map/ppermute | solution.py:451
  12.7 1.7 collective-permute-start.1
  14.4 2.0 %collective-permute-done.1.c2 = bf16[8,96]{1,0:T(8,128)(2,1)S(1)} collective-permute-done((bf16[8,96]{1,0:T(8,128)(2,1)}, bf16[8,96]{1,0:T(8,128)(2,1)S(1)}, u32[]{:S(2)}, u32[]{:S(2)}) %collective-permute-start.1) | collective-permute-done | bytes 1568 | tf_op jit(solution)/shard_map/ppermute | solution.py:451
  18.2 2.7 %shard_map.229 = (f32[8,2688]{1,0:T(8,128)}, f32[8,2688]{1,0:T(8,128)}, f32[8,2688]{1,0:T(8,128)}, f32[8,2688]{1,0:T(8,128)}) custom-call(s32[4]{0:T(128)} %pad_add_fusion.info, bf16[8,96]{1,0:T(8,128)(2,1)} %get-tuple-element.79.c0, bf16[8,96]{1,0:T(8,128)(2,1)} %copy-done.7, bf16[8,96]{1,0:T(8,128)(2,1)} %copy-done.8, bf16[8,96]{1,0:T(8,128)(2,1)} %copy-done.9, ...), custom_call_target="tpu_custom_call" | custom-call | flops 16777216 | bytes 1048576 | tf_op jit(solution)/shard_map/pallas_call | solution.py:413
  23.4 3.1 %collective-permute-done.4.refs_2_ = f32[8,2688]{1,0:T(8,128)S(1)} collective-permute-done((f32[8,2688]{1,0:T(8,128)}, f32[8,2688]{1,0:T(8,128)S(1)}, u32[]{:S(2)}, u32[]{:S(2)}) %collective-permute-start.4) | collective-permute-done | bytes 86048 | tf_op jit(solution)/shard_map/ppermute | solution.py:451
  29.3 13.9 %shard_map.230 = (bf16[8,256,384]{2,1,0:T(8,128)(2,1)}, bf16[8,256,1152]{2,1,0:T(8,128)(2,1)}, bf16[8,6,256,256]{3,2,1,0:T(8,128)(2,1)}, bf16[8,256,384]{2,1,0:T...) custom-call(s32[4]{0:T(128)} %pad_add_fusion.info, bf16[8,256,384]{2,1,0:T(8,128)(2,1)} %tok.7, ...), custom_call_target="tpu_custom_call" | custom-call | flops 4026531840 | bytes 15728640 | tf_op jit(solution)/shard_map/pallas_call | solution.py:413
  47.7 32.4 %shard_map.231 = (bf16[8,256,384]{2,1,0:T(8,128)(2,1)}, f32[8,256,384]{2,1,0:T(8,128)}, bf16[8,256,384]{2,1,0:T(8,128)(2,1)}, bf16[48,384]{1,0:T(8,128)(2,1)}, b...) custom-call(s32[4]{0:T(128)} %pad_add_fusion.info, bf16[8,256,384]{2,1,0:T(8,128)(2,1)} %tok.7, ...), custom_call_target="tpu_custom_call" | custom-call | flops 16307453952 | bytes 11010048 | tf_op jit(solution)/shard_map/pallas_call | solution.py:413
  80.5 2.9 %collective-permute-done.18 = bf16[2,2,432,384]{3,2,1,0:T(8,128)(2,1)S(1)} collective-permute-done((bf16[2,2,432,384]{3,2,1,0:T(8,128)(2,1)}, bf16[2,2,432,384]{3,2,1,0:T(8,128)(2,1)S(1)}, u32[]{:S(2)}, u32[]{:S(2)}) %collective-permute-start.18) | collective-permute-done | bytes 1327136 | tf_op jit(solution)/shard_map/ppermute | solution.py:451
  88.6 2.6 %collective-permute-start.22 = (bf16[48,384]{1,0:T(8,128)(2,1)S(1)}, bf16[48,384]{1,0:T(8,128)(2,1)S(1)}, u32[]{:S(2)}, u32[]{:S(2)}) collective-permute-start(bf16[48,384]{1,0:T(8,128)(2,1)S(1)} %copy-done.5), channel_id=1, source_target_pairs={{0,16},{1,17},{2,18},{3,19},{4,20},{5,21},{6,22},{7,23},{8,24},{9,... | collective-permute-start | bytes 110600 | tf_op jit(solution)/shard_map/ppermute | solution.py:451
  91.2 12.6 %shard_map.232 = (f32[8,256,384]{2,1,0:T(8,128)}, f32[384,1152]{1,0:T(8,128)}, f32[8,768]{1,0:T(8,128)}, f32[8,384]{1,0:T(8,128)}) custom-call(s32[4]{0:T(128)} %pad_add_fusion.info, bf16[8,256,384]{2,1,0:T(8,128)(2,1)} %tok.7, bf16[8,256,384]{2,1,0:T(8,128)(2,1)} %get-tuple-element.109.m1_i, bf16[8,256,1152]{2,1,0:T(8,128)(2,1)} %get-tuple-element.110.qkv_i, ...), custom_call_target="tpu_custom_call" | custom-call | flops 2818572288 | bytes 11796480 | tf_op jit(solution)/shard_map/pallas_call | solution.py:413
  105.9 2.1 %collective-permute-start.28 = (bf16[144,384]{1,0:T(8,128)(2,1)S(1)}, bf16[144,384]{1,0:T(8,128)(2,1)S(1)}, u32[]{:S(2)}, u32[]{:S(2)}) collective-permute-start(bf16[144,384]{1,0:T(8,128)(2,1)S(1)} %get-tuple-element.234), channel_id=1, source_target_pairs={{0,16},{1,17},{2,18},{3,19},{4,20},{5,21},{6,22},{7,23},{8,24},{9,... | collective-permute-start | bytes 331784 | tf_op jit(solution)/shard_map/ppermute | solution.py:451
  110.2 13.0 %shard_map.233 = (f32[8,256,384]{2,1,0:T(8,128)}, bf16[24,384]{1,0:T(8,128)(2,1)}, bf16[2,2,48,1152]{3,2,1,0:T(8,128)(2,1)}, bf16[2,2,48,1152]{3,2,1,0:T(8,128)(2,1)}) custom-call(s32[4]{0:T(128)} %pad_add_fusion.info, bf16[8,256,384]{2,1,0:T(8,128)(2,1)} %tok.7, bf16[8,256,384]{2,1,0:T(8,128)(2,1)} %get-tuple-element.109.m1_i, ...), custom_call_target="tpu_custom_call", output_to_operand_aliasing={{0}: (12, {})} | custom-call | flops 2818572288 | bytes 11796480 | tf_op jit(solution)/shard_map/pallas_call | solution.py:413
  126.2 3.3 %collective-permute-done.31 = bf16[120,384]{1,0:T(8,128)(2,1)S(1)} collective-permute-done((bf16[120,384]{1,0:T(8,128)(2,1)S(1)}, bf16[120,384]{1,0:T(8,128)(2,1)S(1)}, u32[]{:S(2)}, u32[]{:S(2)}) %collective-permute-start.31) | collective-permute-done | bytes 92192 | tf_op jit(solution)/shard_map/ppermute | solution.py:451
  135.6 2.9 %collective-permute-done.26 = bf16[48,1152]{1,0:T(8,128)(2,1)S(1)} collective-permute-done((bf16[48,1152]{1,0:T(8,128)(2,1)S(1)}, bf16[48,1152]{1,0:T(8,128)(2,1)S(1)}, u32[]{:S(2)}, u32[]{:S(2)}) %collective-permute-start.26) | collective-permute-done | bytes 110624 | tf_op jit(solution)/shard_map/ppermute | solution.py:451
  139.7 2.0 %collective-permute-start.33 = (bf16[240,384]{1,0:T(8,128)(2,1)S(1)}, bf16[240,384]{1,0:T(8,128)(2,1)S(1)}, u32[]{:S(2)}, u32[]{:S(2)}) collective-permute-start(bf16[240,384]{1,0:T(8,128)(2,1)S(1)} %pad_maximum_fusion.10), channel_id=1, source_target_pairs={{0,16},{1,17},{2,18},{3,19},{4,20},{5,21},{6,22},{7,23},{8,24},{9,... | collective-permute-start | bytes 552968 | tf_op jit(solution)/shard_map/ppermute | solution.py:451
  141.7 8.9 %collective-permute-done.33 = bf16[240,384]{1,0:T(8,128)(2,1)S(1)} collective-permute-done((bf16[240,384]{1,0:T(8,128)(2,1)S(1)}, bf16[240,384]{1,0:T(8,128)(2,1)S(1)}, u32[]{:S(2)}, u32[]{:S(2)}) %collective-permute-start.33) | collective-permute-done | bytes 184352 | tf_op jit(solution)/shard_map/ppermute | solution.py:451
  150.8 2.0 %collective-permute-start.43 = (bf16[48,1152]{1,0:T(8,128)(2,1)S(1)}, bf16[48,1152]{1,0:T(8,128)(2,1)S(1)}, u32[]{:S(2)}, u32[]{:S(2)}) collective-permute-start(bf16[48,1152]{1,0:T(8,128)(2,1)S(1)} %add_convert_fusion.6), channel_id=1, source_target_pairs={{0,16},{1,17},{2,18},{3,19},{4,20},{5,21},{6,22},{7,23},{8,24},{9,... | collective-permute-start | bytes 331784 | tf_op jit(solution)/shard_map/ppermute | solution.py:451
  152.7 2.4 %collective-permute-start.44 = (bf16[48,1152]{1,0:T(8,128)(2,1)S(1)}, bf16[48,1152]{1,0:T(8,128)(2,1)S(1)}, u32[]{:S(2)}, u32[]{:S(2)}) collective-permute-start(bf16[48,1152]{1,0:T(8,128)(2,1)S(1)} %add_convert_fusion.6), channel_id=1, source_target_pairs={{0,24},{1,25},{2,26},{3,27},{4,28},{5,29},{6,30},{7,31},{8,16},{9,... | collective-permute-start | bytes 331784 | tf_op jit(solution)/shard_map/ppermute | solution.py:451
  157.3 3.1 %collective-permute-done.34 = bf16[96,384]{1,0:T(8,128)(2,1)S(1)} collective-permute-done((bf16[96,384]{1,0:T(8,128)(2,1)S(1)}, bf16[96,384]{1,0:T(8,128)(2,1)S(1)}, u32[]{:S(2)}, u32[]{:S(2)}) %collective-permute-start.34) | collective-permute-done | bytes 73760 | tf_op jit(solution)/shard_map/ppermute | solution.py:451
  161.6 5.6 %collective-permute-done.35 = bf16[192,384]{1,0:T(8,128)(2,1)S(1)} collective-permute-done((bf16[192,384]{1,0:T(8,128)(2,1)S(1)}, bf16[192,384]{1,0:T(8,128)(2,1)S(1)}, u32[]{:S(2)}, u32[]{:S(2)}) %collective-permute-start.35) | collective-permute-done | bytes 147488 | tf_op jit(solution)/shard_map/ppermute | solution.py:451
  168.5 6.5 %collective-permute-done.45 = bf16[432,384]{1,0:T(8,128)(2,1)S(1)} collective-permute-done((bf16[432,384]{1,0:T(8,128)(2,1)S(1)}, bf16[432,384]{1,0:T(8,128)(2,1)S(1)}, u32[]{:S(2)}, u32[]{:S(2)}) %collective-permute-start.45) | collective-permute-done | bytes 331808 | tf_op jit(solution)/shard_map/ppermute | solution.py:451
  179.1 2.8 %collective-permute-done.46 = bf16[48,1152]{1,0:T(8,128)(2,1)} collective-permute-done((bf16[48,1152]{1,0:T(8,128)(2,1)S(1)}, bf16[48,1152]{1,0:T(8,128)(2,1)}, u32[]{:S(2)}, u32[]{:S(2)}) %collective-permute-start.46) | collective-permute-done | bytes 110624 | tf_op jit(solution)/shard_map/ppermute | solution.py:451
  (211 shorter events, 51.7 us)
Async XLA Ops:
  3.5 8.7 %collective-permute-start.7 = (bf16[96,1152]{1,0:T(8,128)(2,1)}, bf16[96,1152]{1,0:T(8,128)(2,1)S(1)}, u32[]{:S(2)}, u32[]{:S(2)}) collective-permute-start(bf16[96,1152]{1,0:T(8,128)(2,1)} %refs_0_.5), channel_id=1, source_target_pairs={{0,2},{1,3},{2,0},{3,1},{4,6},{5,7},{6,4},{7,5},{8,10},{9,11},{10,... | collective-permute-start | bytes 663560 | tf_op jit(solution)/shard_map/ppermute | solution.py:451
  6.4 22.1 %collective-permute-start.6 = (bf16[96,1152]{1,0:T(8,128)(2,1)}, bf16[96,1152]{1,0:T(8,128)(2,1)S(1)}, u32[]{:S(2)}, u32[]{:S(2)}) collective-permute-start(bf16[96,1152]{1,0:T(8,128)(2,1)} %refs_0_.5), channel_id=1, source_target_pairs={{0,1},{1,0},{2,3},{3,2},{4,5},{5,4},{6,7},{7,6},{8,9},{9,8},{10,11... | collective-permute-start | bytes 663560 | tf_op jit(solution)/shard_map/ppermute | solution.py:451
  12.1 16.4 %collective-permute-start.8 = (bf16[96,1152]{1,0:T(8,128)(2,1)S(1)}, bf16[96,1152]{1,0:T(8,128)(2,1)S(1)}, u32[]{:S(2)}, u32[]{:S(2)}) collective-permute-start(bf16[96,1152]{1,0:T(8,128)(2,1)S(1)} %collective-permute-done.7.refs_6_.refs_2_), channel_id=1, source_target_pairs={{0,1},{1,0},{2,3},{3,2},{4,5},{5,4},{6,7},{7,6},{8,9},{9,8},{10,11... | collective-permute-start | bytes 663560 | tf_op jit(solution)/shard_map/ppermute | solution.py:451
  22.8 20.5 %collective-permute-start.10 = (bf16[96,384]{1,0:T(8,128)(2,1)}, bf16[96,384]{1,0:T(8,128)(2,1)S(1)}, u32[]{:S(2)}, u32[]{:S(2)}) collective-permute-start(bf16[96,384]{1,0:T(8,128)(2,1)} %refs_0_.3), channel_id=1, source_target_pairs={{0,2},{1,3},{2,0},{3,1},{4,6},{5,7},{6,4},{7,5},{8,10},{9,11},{10,... | collective-permute-start | bytes 221192 | tf_op jit(solution)/shard_map/ppermute | solution.py:451
  26.5 16.8 %collective-permute-start.11 = (bf16[96,1536]{1,0:T(8,128)(2,1)}, bf16[96,1536]{1,0:T(8,128)(2,1)S(1)}, u32[]{:S(2)}, u32[]{:S(2)}) collective-permute-start(bf16[96,1536]{1,0:T(8,128)(2,1)} %refs_4_.3), channel_id=1, source_target_pairs={{0,2},{1,3},{2,0},{3,1},{4,6},{5,7},{6,4},{7,5},{8,10},{9,11},{10,... | collective-permute-start | bytes 884744 | tf_op jit(solution)/shard_map/ppermute | solution.py:451
  27.5 15.8 %collective-permute-start.12 = (bf16[384,384]{1,0:T(8,128)(2,1)}, bf16[384,384]{1,0:T(8,128)(2,1)S(1)}, u32[]{:S(2)}, u32[]{:S(2)}) collective-permute-start(bf16[384,384]{1,0:T(8,128)(2,1)} %refs_8_.1), channel_id=1, source_target_pairs={{0,2},{1,3},{2,0},{3,1},{4,6},{5,7},{6,4},{7,5},{8,10},{9,11},{10,... | collective-permute-start | bytes 884744 | tf_op jit(solution)/shard_map/ppermute | solution.py:451
  28.5 17.4 %collective-permute-start.14 = (bf16[96,1536]{1,0:T(8,128)(2,1)}, bf16[96,1536]{1,0:T(8,128)(2,1)S(1)}, u32[]{:S(2)}, u32[]{:S(2)}) collective-permute-start(bf16[96,1536]{1,0:T(8,128)(2,1)} %refs_4_.3), channel_id=1, source_target_pairs={{0,1},{1,0},{2,3},{3,2},{4,5},{5,4},{6,7},{7,6},{8,9},{9,8},{10,11... | collective-permute-start | bytes 884744 | tf_op jit(solution)/shard_map/ppermute | solution.py:451
  28.6 17.4 %collective-permute-start.16 = (bf16[384,384]{1,0:T(8,128)(2,1)}, bf16[384,384]{1,0:T(8,128)(2,1)S(1)}, u32[]{:S(2)}, u32[]{:S(2)}) collective-permute-start(bf16[384,384]{1,0:T(8,128)(2,1)} %refs_8_.1), channel_id=1, source_target_pairs={{0,1},{1,0},{2,3},{3,2},{4,5},{5,4},{6,7},{7,6},{8,9},{9,8},{10,11... | collective-permute-start | bytes 884744 | tf_op jit(solution)/shard_map/ppermute | solution.py:451
  85.0 18.8 %collective-permute-start.19 = (bf16[432,384]{1,0:T(8,128)(2,1)S(1)}, bf16[432,384]{1,0:T(8,128)(2,1)S(1)}, u32[]{:S(2)}, u32[]{:S(2)}) collective-permute-start(bf16[432,384]{1,0:T(8,128)(2,1)S(1)} %get-tuple-element.178), channel_id=1, source_target_pairs={{0,4},{1,5},{2,6},{3,7},{4,0},{5,1},{6,2},{7,3},{8,12},{9,13},{10,... | collective-permute-start | bytes 995336 | tf_op jit(solution)/shard_map/ppermute | solution.py:451
  86.6 17.3 %collective-permute-start.20 = (bf16[432,384]{1,0:T(8,128)(2,1)S(1)}, bf16[432,384]{1,0:T(8,128)(2,1)S(1)}, u32[]{:S(2)}, u32[]{:S(2)}) collective-permute-start(bf16[432,384]{1,0:T(8,128)(2,1)S(1)} %get-tuple-element.177), channel_id=1, source_target_pairs={{0,2},{1,3},{2,0},{3,1},{4,6},{5,7},{6,4},{7,5},{8,10},{9,11},{10,... | collective-permute-start | bytes 995336 | tf_op jit(solution)/shard_map/ppermute | solution.py:451
  87.8 16.1 %collective-permute-start.21 = (bf16[432,384]{1,0:T(8,128)(2,1)S(1)}, bf16[432,384]{1,0:T(8,128)(2,1)S(1)}, u32[]{:S(2)}, u32[]{:S(2)}) collective-permute-start(bf16[432,384]{1,0:T(8,128)(2,1)S(1)} %get-tuple-element.176), channel_id=1, source_target_pairs={{0,6},{1,7},{2,4},{3,5},{4,2},{5,3},{6,0},{7,1},{8,14},{9,15},{10,... | collective-permute-start | bytes 995336 | tf_op jit(solution)/shard_map/ppermute | solution.py:451
  88.6 15.2 %collective-permute-start.22 = (bf16[48,384]{1,0:T(8,128)(2,1)S(1)}, bf16[48,384]{1,0:T(8,128)(2,1)S(1)}, u32[]{:S(2)}, u32[]{:S(2)}) collective-permute-start(bf16[48,384]{1,0:T(8,128)(2,1)S(1)} %copy-done.5), channel_id=1, source_target_pairs={{0,16},{1,17},{2,18},{3,19},{4,20},{5,21},{6,22},{7,23},{8,24},{9,... | collective-permute-start | bytes 110600 | tf_op jit(solution)/shard_map/ppermute | solution.py:451
  104.2 19.0 %collective-permute-start.27 = (bf16[144,384]{1,0:T(8,128)(2,1)S(1)}, bf16[144,384]{1,0:T(8,128)(2,1)S(1)}, u32[]{:S(2)}, u32[]{:S(2)}) collective-permute-start(bf16[144,384]{1,0:T(8,128)(2,1)S(1)} %get-tuple-element.233), channel_id=1, source_target_pairs={{0,8},{1,9},{2,10},{3,11},{4,12},{5,13},{6,14},{7,15},{8,0},{9,1},... | collective-permute-start | bytes 331784 | tf_op jit(solution)/shard_map/ppermute | solution.py:451
  105.9 17.4 %collective-permute-start.28 = (bf16[144,384]{1,0:T(8,128)(2,1)S(1)}, bf16[144,384]{1,0:T(8,128)(2,1)S(1)}, u32[]{:S(2)}, u32[]{:S(2)}) collective-permute-start(bf16[144,384]{1,0:T(8,128)(2,1)S(1)} %get-tuple-element.234), channel_id=1, source_target_pairs={{0,16},{1,17},{2,18},{3,19},{4,20},{5,21},{6,22},{7,23},{8,24},{9,... | collective-permute-start | bytes 331784 | tf_op jit(solution)/shard_map/ppermute | solution.py:451
  108.0 15.2 %collective-permute-start.29 = (bf16[144,384]{1,0:T(8,128)(2,1)S(1)}, bf16[144,384]{1,0:T(8,128)(2,1)S(1)}, u32[]{:S(2)}, u32[]{:S(2)}) collective-permute-start(bf16[144,384]{1,0:T(8,128)(2,1)S(1)} %get-tuple-element.232), channel_id=1, source_target_pairs={{0,24},{1,25},{2,26},{3,27},{4,28},{5,29},{6,30},{7,31},{8,16},{9,... | collective-permute-start | bytes 331784 | tf_op jit(solution)/shard_map/ppermute | solution.py:451
  108.7 14.5 %collective-permute-start.30 = (bf16[96,384]{1,0:T(8,128)(2,1)S(1)}, bf16[96,384]{1,0:T(8,128)(2,1)S(1)}, u32[]{:S(2)}, u32[]{:S(2)}) collective-permute-start(bf16[96,384]{1,0:T(8,128)(2,1)S(1)} %pad_maximum_fusion.19), channel_id=1, source_target_pairs={{0,4},{1,5},{2,6},{3,7},{4,0},{5,1},{6,2},{7,3},{8,12},{9,13},{10,... | collective-permute-start | bytes 221192 | tf_op jit(solution)/shard_map/ppermute | solution.py:451
  124.8 7.1 %collective-permute-start.23 = (bf16[2,2,48,1152]{3,2,1,0:T(8,128)(2,1)}, bf16[2,2,48,1152]{3,2,1,0:T(8,128)(2,1)S(1)}, u32[]{:S(2)}, u32[]{:S(2)}) collective-permute-start(bf16[2,2,48,1152]{3,2,1,0:T(8,128)(2,1)} %get-tuple-element.125), channel_id=1, source_target_pairs={{0,1},{1,0},{2,3},{3,2},{4,5},{5,4},{6,7},{7,6},{8,9},{9,8},{10,11... | collective-permute-start | bytes 1327112 | tf_op jit(solution)/shard_map/ppermute | solution.py:451
  139.7 10.9 %collective-permute-start.33 = (bf16[240,384]{1,0:T(8,128)(2,1)S(1)}, bf16[240,384]{1,0:T(8,128)(2,1)S(1)}, u32[]{:S(2)}, u32[]{:S(2)}) collective-permute-start(bf16[240,384]{1,0:T(8,128)(2,1)S(1)} %pad_maximum_fusion.10), channel_id=1, source_target_pairs={{0,16},{1,17},{2,18},{3,19},{4,20},{5,21},{6,22},{7,23},{8,24},{9,... | collective-permute-start | bytes 552968 | tf_op jit(solution)/shard_map/ppermute | solution.py:451
  150.7 26.2 %collective-permute-start.42 = (bf16[48,1152]{1,0:T(8,128)(2,1)S(1)}, bf16[48,1152]{1,0:T(8,128)(2,1)S(1)}, u32[]{:S(2)}, u32[]{:S(2)}) collective-permute-start(bf16[48,1152]{1,0:T(8,128)(2,1)S(1)} %add_convert_fusion.6), channel_id=1, source_target_pairs={{0,8},{1,9},{2,10},{3,11},{4,12},{5,13},{6,14},{7,15},{8,0},{9,1},... | collective-permute-start | bytes 331784 | tf_op jit(solution)/shard_map/ppermute | solution.py:451
  150.8 26.1 %collective-permute-start.43 = (bf16[48,1152]{1,0:T(8,128)(2,1)S(1)}, bf16[48,1152]{1,0:T(8,128)(2,1)S(1)}, u32[]{:S(2)}, u32[]{:S(2)}) collective-permute-start(bf16[48,1152]{1,0:T(8,128)(2,1)S(1)} %add_convert_fusion.6), channel_id=1, source_target_pairs={{0,16},{1,17},{2,18},{3,19},{4,20},{5,21},{6,22},{7,23},{8,24},{9,... | collective-permute-start | bytes 331784 | tf_op jit(solution)/shard_map/ppermute | solution.py:451
  152.7 24.2 %collective-permute-start.44 = (bf16[48,1152]{1,0:T(8,128)(2,1)S(1)}, bf16[48,1152]{1,0:T(8,128)(2,1)S(1)}, u32[]{:S(2)}, u32[]{:S(2)}) collective-permute-start(bf16[48,1152]{1,0:T(8,128)(2,1)S(1)} %add_convert_fusion.6), channel_id=1, source_target_pairs={{0,24},{1,25},{2,26},{3,27},{4,28},{5,29},{6,30},{7,31},{8,16},{9,... | collective-permute-start | bytes 331784 | tf_op jit(solution)/shard_map/ppermute | solution.py:451
  156.0 12.4 %collective-permute-start.37 = (bf16[384,384]{1,0:T(8,128)(2,1)S(1)}, bf16[384,384]{1,0:T(8,128)(2,1)S(1)}, u32[]{:S(2)}, u32[]{:S(2)}) collective-permute-start(bf16[384,384]{1,0:T(8,128)(2,1)S(1)} %pad_maximum_fusion.7), channel_id=1, source_target_pairs={{0,2},{1,3},{2,0},{3,1},{4,6},{5,7},{6,4},{7,5},{8,10},{9,11},{10,... | collective-permute-start | bytes 884744 | tf_op jit(solution)/shard_map/ppermute | solution.py:451
  167.2 7.8 %collective-permute-start.45 = (bf16[432,384]{1,0:T(8,128)(2,1)S(1)}, bf16[432,384]{1,0:T(8,128)(2,1)S(1)}, u32[]{:S(2)}, u32[]{:S(2)}) collective-permute-start(bf16[432,384]{1,0:T(8,128)(2,1)S(1)} %fusion.12), channel_id=1, source_target_pairs={{0,4},{1,5},{2,6},{3,7},{4,0},{5,1},{6,2},{7,3},{8,12},{9,13},{10,... | collective-permute-start | bytes 995336 | tf_op jit(solution)/shard_map/ppermute | solution.py:451
  168.3 15.3 %collective-permute-start.36 = (bf16[384,384]{1,0:T(8,128)(2,1)S(1)}, bf16[384,384]{1,0:T(8,128)(2,1)S(1)}, u32[]{:S(2)}, u32[]{:S(2)}) collective-permute-start(bf16[384,384]{1,0:T(8,128)(2,1)S(1)} %pad_maximum_fusion.8), channel_id=1, source_target_pairs={{0,1},{1,0},{2,3},{3,2},{4,5},{5,4},{6,7},{7,6},{8,9},{9,8},{10,11... | collective-permute-start | bytes 884744 | tf_op jit(solution)/shard_map/ppermute | solution.py:451
  (46 other events, 195.4 us)

commit v3 on v2

--- a/solution.py
+++ b/solution.py
@@ -57,8 +57,8 @@
     return (lane < shape[-1] // 2) if half == 0 else (lane >= shape[-1] // 2)
 
 
-def condition(info, cond, b_ada, b_qv, b_o, b_1, b_2, *refs):
-    cuts, share, packed = refs[0:4], refs[4], refs[5]
+def condition(info, cond, b_ada, b_qv, b_o, b_1, b_2, w_o, w_1, w_2, *refs):
+    cuts, share, packed, tall = refs[0:4], refs[4], refs[5], refs[6]
     c = cond[...].astype(F32)
     cs = c / (1.0 + jnp.exp(-c))
     cut = cs.shape[1] // 4
@@ -79,6 +79,12 @@
     packed[...] = jnp.zeros_like(packed)
     for i, b in enumerate((b_qv, b_o, b_1, b_2)):
         packed[i : i + 1, 0 : b.shape[0]] = b[...].astype(F32).reshape(1, b.shape[0])
+    rows, width = w_o.shape
+    tall[0:rows] = w_o[...]
+    many = w_1.shape[1] // width
+    for i in range(many):
+        tall[(1 + i) * rows : (2 + i) * rows] = w_1[:, i * width : (i + 1) * width]
+    tall[(1 + many) * rows :] = w_2[...]
 
 
 def ada_parts(info, c0, c1, c2, c3, w_ada, share, packed, *outs):
@@ -164,20 +170,29 @@
 
 
 def ffn_both(info, tok, att_i, dy_i, ada, cond, table, *refs, per, chunk):
-    wo, w1, w2 = refs[0:4], refs[4:8], refs[8:12]
-    out_o, dx1_o, datt_o, early_o, keep_o, send_o = refs[12:18]
-    wo_s, w1_s, w2_s, go_s, g1_s, g2_s, small_s, gb_s, bo_s, b1_s, b2_s, sem_o, sem_1, sem_2 = refs[18:]
+    pieces = refs[0:4]
+    out_o, dx1_o, datt_o, early_o, keep_o, send_o = refs[4:10]
+    wo_s, w1_s, w2_s, go_s, g1_s, g2_s, small_s, gb_s, bo_s, b1_s, b2_s, sems = refs[10:]
     step = pl.program_id(0)
     length, width = tok.shape[1:]
     hidden = w1_s.shape[1]
 
     @pl.when(step == 0)
     def _():
-        copies = (
-            piece_copies(info[0], wo, wo_s, sem_o)
-            + piece_copies(info[0], w1, w1_s, sem_1)
-            + piece_copies(info[0], w2, w2_s, sem_2)
-        )
+        copies, n, rows = [], hidden // width + 2, width // 4
+        for k, piece in enumerate(pieces):
+            at = pl.multiple_of(jnp.bitwise_xor(info[0], k) * rows, 32)
+            at2 = pl.multiple_of(jnp.bitwise_xor(info[0], k) * (hidden // 4), 32)
+            places = [wo_s.at[pl.ds(at, rows)]]
+            places += [
+                w1_s.at[pl.ds(at, rows), i * width : (i + 1) * width] for i in range(n - 2)
+            ]
+            places += [w2_s.at[pl.ds(at2, hidden // 4)]]
+            start = 0
+            for i, place in enumerate(places):
+                source = piece.at[start : start + place.shape[0]]
+                copies.append(pltpu.make_async_copy(source, place, sems.at[n * k + i]))
+                start += place.shape[0]
         for copy in copies:
             copy.start()
         go_s[...] = jnp.zeros_like(go_s)
@@ -451,26 +466,26 @@
         return lax.ppermute(v, ("rep", "shard"), pairs)
 
     whole = lambda vs: [full(v.shape) for v in vs]
-    ins = (cond, b_ada, b_qv, b_o, b_1, b_2)
+    ins = (cond, b_ada, b_qv, b_o, b_1, b_2, w_o, w_1, w_2)
     outs = [jax.ShapeDtypeStruct((count, quarter), BF16)] * 4 + [
         jax.ShapeDtypeStruct((1, 6 * width), F32),
         jax.ShapeDtypeStruct((8, width), F32),
+        jax.ShapeDtypeStruct((quarter + quarter * hidden // width + hidden // 4, width), BF16),
     ]
-    *cuts, share, packed = call(
+    *cuts, share, packed, ffn_w = call(
         condition, info, ins, whole(ins), outs, whole(outs), [], (1,), 60, 0, 1 << 17
     )
-    near_qkv, far_qkv = after((w_qkv, w_qkv), cuts[0])
     cuts = [cuts[0]] + [swap(cuts[k], k) for k in range(1, 4)]
+    near_qkv, far_qkv = after((w_qkv, w_qkv), *cuts)
     near_qkv, far_qkv = swap(near_qkv, 1), swap(far_qkv, 2)
-    ffn_w = (w_o, w_1, w_2)
-    near_w = [swap(v, 1) for v in after(ffn_w, cuts[1])]
     ins = tuple(cuts) + (w_ada, share, packed)
     outs = [jax.ShapeDtypeStruct((count, 7 * width), F32)] * 4
     parts = call(ada_parts, info, ins, whole(ins), outs, whole(outs), [], (1,), 60, 1 << 24, 1 << 20)
     sent = parts[0]
     p_qkv = (w_qkv, near_qkv, far_qkv, swap(far_qkv, 1))
     parts = [parts[0]] + [swap(parts[k], k) for k in range(1, 4)]
-    far_w = [swap(v, 2) for v in after(ffn_w, sent)]
+    near_w = swap(after(ffn_w, sent), 1)
+    far_w = swap(after(ffn_w, *parts), 2)
 
     anyspec = pl.BlockSpec(memory_space=pl.ANY)
     dma4 = pltpu.SemaphoreType.DMA((4,))
@@ -509,7 +524,7 @@
     )
 
     far_w = after(far_w, table)
-    p_o, p_1, p_2 = ((v, near, far, swap(far, 1)) for v, near, far in zip(ffn_w, near_w, far_w))
+    p_ffn = (ffn_w, near_w, far_w, swap(far_w, 1))
 
     per2 = 2 if count % 2 == 0 else 1
     lat2 = lambda *tail: pl.BlockSpec((per2,) + tail, lambda i, _: (i,) + (0,) * len(tail))
@@ -517,10 +532,10 @@
     block_out, dx1, datt, early, keep_f, send_f = call(
         functools.partial(ffn_both, per=per2, chunk=hidden),
         info,
-        (latent_tokens, att, grad_out, ada, cond, table) + p_o + p_1 + p_2,
+        (latent_tokens, att, grad_out, ada, cond, table) + p_ffn,
         [lat2(length, width)] * 3
         + [full(ada.shape), full(cond.shape), full(table.shape)]
-        + [anyspec] * 12,
+        + [anyspec] * 4,
         [
             jax.ShapeDtypeStruct((count, length, width), BF16),
             jax.ShapeDtypeStruct((count, length, width), F32),
@@ -541,9 +556,7 @@
             pltpu.VMEM((1, width), F32),
             pltpu.VMEM((1, hidden), F32),
             pltpu.VMEM((1, width), F32),
-            dma4,
-            dma4,
-            dma4,
+            pltpu.SemaphoreType.DMA((4 * (hidden // width + 2),)),
         ],
         (count // per2,),
         60,
@@ -621,19 +634,19 @@
     def z_pair(v, bit):
         return pair(v, 0, 2 * bit, (z_at & bit) != 0)
 
-    n_f = 9 * half
-    n_e = early.shape[0]
+    n_f, n_e = 9 * half, early.shape[0]
+    early_z = over_z(early, [early] * (n_z - 1))
     parts_f = chip_sum(keep_f, send_f)
+    *early_z, first_part = after(early_z + parts_f[:1])
+    parts_f = [first_part] + parts_f[1:]
+    early_g = jnp.concatenate(ordered(early_z, z_at), axis=0)
+
+    got = over_plane(parts_f[0], parts_f[1:])
+    early_x = pair(early_g, 2, 0, y_at == 1)
     gtok, g_half, small_half, gb_half = backward(
         0, False, after(info, *parts_f), (), [], acc_shapes, acc_specs, [], None
     )
-    got = over_plane(parts_f[0], parts_f[1:])
-    early_g = z_pair(after(early, *parts_f), 2)
-    bit = 4
-    while bit < n_z:
-        early_g = z_pair(early_g, bit)
-        bit *= 2
-    *got, early_g = after(got + [early_g], gb_half)
+    *got, early_g = after(got + [early_x], gb_half)
     total_f = tree_sum(got).astype(BF16)
     z_low = z_at & 3
     loads = [
@@ -646,7 +659,9 @@
         )
         for k in range(n_z)
     ]
-    early_g = pair(early_g, 0, 1, x_at == 1)
+
+    got = over_z(loads[0], loads[1:])
+    early_y = pair(early_g, 0, 1, x_at == 1)
     send_shape = (2, 2, half, 3 * width)
     grad_tokens, late, keep_a, send_a = backward(
         count // 2,
@@ -663,31 +678,34 @@
         [pltpu.VMEM(v, F32) for v in acc],
         {12: 0},
     )
-    *got, early_g = after(over_z(loads[0], loads[1:]) + [early_g], late)
+    *got, early_g, keep_a, send_a, late = after(got + [early_y, keep_a, send_a, late])
     piece_f = tree_sum([v[: 2 * half] for v in got]).astype(BF16)
     out_f = tree_sum([v[2 * half : 3 * half] for v in got]).astype(BF16)
 
+    n_l = late.shape[0]
     parts_a = chip_sum(keep_a, send_a)
-    n_l = late.shape[0]
-    load = z_pair(jnp.concatenate([piece_f, late], axis=0), 1)
-    early_g = z_pair(early_g, 1)
-    got_a = over_plane(parts_a[0], parts_a[1:])
-    load, early_g = after((load, early_g), *parts_a)
-    bit = 2
-    while bit < n_z:
-        load = z_pair(load, bit)
-        bit *= 2
-    total_a, load, early_g = after((tree_sum(got_a).astype(BF16), load, early_g))
+    late_z = over_z(late, [late] * (n_z - 1))
+    first_f = swap(piece_f, 0, 2)
+    *phase, early_g, first_f = after(parts_a + late_z + [early_g, first_f])
+    parts_a, late_z = phase[:4], phase[4:]
+
+    late_g = jnp.concatenate(ordered(late_z, z_at), axis=0)
+    wide_rows = lambda v: jnp.concatenate(
+        [v[:, i * width : (i + 1) * width] for i in range(3)], axis=0
+    )
+    loads = [jnp.concatenate([wide_rows(v), late_g], axis=0) for v in parts_a]
+    got = over_plane(loads[0], loads[1:])
+    two_f = jnp.concatenate([piece_f, first_f], axis=0)
+    rest_f = swap(two_f, 0, 4)
+    early_c = pair(early_g, 1, 0, (s & 1) == 1)
+    *got, two_f, rest_f, early_g = after(got + [two_f, rest_f, early_c])
+
+    total_a = tree_sum([v[: 3 * half] for v in got]).astype(BF16)
+    late_g = jnp.concatenate(ordered([v[3 * half :] for v in got], 2 * y_at + x_at), axis=0)
     ring_a = over_z(total_a, [total_a] * (n_z - 1))
-    n_p = 2 * half + n_l
-    blocks = [load[i * n_p : i * n_p + 2 * half] for i in range(4)]
-    late_g = jnp.concatenate([load[i * n_p + 2 * half : (i + 1) * n_p] for i in range(n_z)], axis=0)
-    mine_f = jnp.concatenate(blocks + [out_f], axis=0)
+    blocks = [two_f[: 2 * half], two_f[2 * half :], rest_f[: 2 * half], rest_f[2 * half :]]
+    mine_f = jnp.concatenate(ordered(blocks, z_low) + [out_f], axis=0)
     yours_f = swap(mine_f, 0, 1)
-    late_g = pair(late_g, 2, 0, y_at == 1)
-    early_g = pair(early_g, 2, 0, y_at == 1)
-    late_g = pair(late_g, 0, 1, x_at == 1)
-    early_g = pair(early_g, 1, 0, (s & 1) == 1)
     late_g = pair(late_g, 1, 0, (s & 1) == 1)
 
     sides = by_x(mine_f, yours_f)
@@ -700,9 +718,7 @@
     ).T.astype(F32)
     gw_o = jnp.concatenate([side[8 * half :] for side in sides], axis=0).astype(F32)
 
-    n_h = n_z // 2
-    early_r = early_g.reshape(2, 2, 2, 2, n_h, n_e // 8, 8, width)
-    early_r = early_r.transpose(0, 3, 1, 4, 2, 5, 6, 7).reshape(2, 2, 2, n_z, n_e // 8, 8, width)
+    early_r = early_g.reshape(2, 2, 2, n_z, n_e // 8, 8, width).transpose(0, 2, 1, 3, 4, 5, 6)
     late_r = late_g.reshape(2, 2, 2, n_z, n_l // 8, 8, width)
     to_rows = lambda v, i: v[:, :, :, :, i].reshape(-1, width)
     cs_all = lax.dynamic_slice_in_dim(to_rows(early_r, 4), s * quarter, quarter, 1)
@@ -720,11 +736,14 @@
 
     def group(v, parts):
         v = lax.dynamic_index_in_dim(v, z_at, 3, keepdims=False)
-        v = lax.dynamic_index_in_dim(v, x_at, 1, keepdims=False)
+        v = lax.dynamic_index_in_dim(v, x_at, 2, keepdims=False)
         return [v[:, :, i].transpose(1, 0, 2, 3).reshape(4 * 8, width) for i in range(parts)]
 
     dada = jnp.concatenate(group(late_r, 2) + group(early_r, 4), axis=1)
     dcs = lax.dot_general(dada, w_ada, (((1,), (1,)), ((), ())), preferred_element_type=F32)
+    *ring_a, gw_1, gw_2, gw_o, gw_ada, dcs = after(ring_a + [gw_1, gw_2, gw_o, gw_ada, dcs])
+    mine_a = tree_sum(ring_a).astype(BF16)
+    yours_a = swap(mine_a, 0, 1)
     dcs = ordered([dcs[k * 8 : (k + 1) * 8] for k in range(4)], s)
     dcs = ordered([dcs[0]] + [swap(dcs[k], k) for k in range(1, 4)], s)
     c32 = cond.astype(F32)
@@ -735,9 +754,11 @@
         part = row.shape[0] // shards
         return lax.dynamic_slice(row, (s * part,), (part,))
 
-    *ring_a, gw_1, gw_2, gw_o = after(ring_a + [gw_1, gw_2, gw_o])
-    mine_a = tree_sum(ring_a).astype(BF16)
-    gw_qkv = jnp.concatenate(by_x(mine_a, swap(mine_a, 0, 1)), axis=0).astype(F32)
+    tall = jnp.concatenate(
+        [v.reshape(3, half, width).transpose(1, 0, 2).reshape(half, 3 * width) for v in by_x(mine_a, yours_a)],
+        axis=0,
+    )
+    gw_qkv = tall.astype(F32)
 
     return (
         block_out,

time: 193 us -> 172 us (0.89)
  waiting for transfers between devices: 53.2 us -> 34 us
  starting transfers between devices: 43.1 us -> 39.4 us
  local copies, waits for them, and re-layouts: 5.7 us -> 7.93 us
    ppermute x47 -> x43, waiting for transfers between devices: 53.2 us -> 34 us  [swap(): return lax.ppermute(v, ('rep', 'shard'), pairs)]
    ppermute x47 -> x43, starting transfers between devices: 43.1 us -> 39.4 us  [swap(): return lax.ppermute(v, ('rep', 'shard'), pairs)]
    unnamed x56 -> x58, local copies, waits for them, and re-layouts: 3.12 us -> 4.61 us
  transfers between devices with their start and end apart: 47 -> 43, of which waited for: 17 -> 16; matrix products, arithmetic and copies ran while one was open for 5% -> 8% of each run, Pallas kernels for 22% -> 25%
where the time goes in v3:
time: 172 us; the launch traced here: 171 us
  Pallas kernels  77.6 us (45%)
  starting transfers between devices  39.4 us (23%)
  waiting for transfers between devices  34 us (20%)
  other arithmetic  9.97 us (6%)
  local copies, waits for them, and re-layouts  7.93 us (5%)
    pallas_call x6, Pallas kernels, call(): pl.pallas_call(body, out_shape=outs, input_output_aliases=alias or {}, gr...  77.6 us
    ppermute x43, starting transfers between devices, swap(): return lax.ppermute(v, ('rep', 'shard'), pairs)  39.4 us
    ppermute x43, waiting for transfers between devices, swap(): return lax.ppermute(v, ('rep', 'shard'), pairs)  34 us
    unnamed x58, local copies, waits for them, and re-layouts  4.61 us
  transfers between devices with their start and end apart: 43, of which 16 were waited for; matrix products, arithmetic and copies ran while one was open for 8% of the time, Pallas kernels for 25%

profile of v3, /device:TPU:0, one launch (start us, length us, event | category | flops | bytes accessed | tf_op | source)
XLA Modules:
  0.0 171.2 jit_solution(7431735751629235899)
XLA Ops:
  1.3 2.9 %shard_map.228 = (bf16[8,96]{1,0:T(8,128)(2,1)}, bf16[8,96]{1,0:T(8,128)(2,1)}, bf16[8,96]{1,0:T(8,128)(2,1)}, bf16[8,96]{1,0:T(8,128)(2,1)}, f32[1,2304]{1,0:T(...) custom-call(s32[4]{0:T(128)} %pad_add_fusion.info, bf16[8,384]{1,0:T(8,128)(2,1)} %cond.3, bf16[576]{0:T(1024)(128)(2,1)} %b_ada.1, ...), custom_call_target="tpu_custom_call" | custom-call | bytes 131072 | tf_op jit(solution)/shard_map/pallas_call | solution.py:428
  4.7 2.5 %collective-permute-start.1 = (bf16[8,96]{1,0:T(8,128)(2,1)}, bf16[8,96]{1,0:T(8,128)(2,1)S(1)}, u32[]{:S(2)}, u32[]{:S(2)}) collective-permute-start(bf16[8,96]{1,0:T(8,128)(2,1)} %get-tuple-element.97), channel_id=1, source_target_pairs={{0,2},{1,3},{2,0},{3,1},{4,6},{5,7},{6,4},{7,5},{8,10},{9,11},{10,... | collective-permute-start | bytes 4616 | tf_op jit(solution)/shard_map/ppermute | solution.py:466
  7.3 1.6 collective-permute-done.1.c2
  11.0 2.7 %shard_map.229 = (f32[8,2688]{1,0:T(8,128)}, f32[8,2688]{1,0:T(8,128)}, f32[8,2688]{1,0:T(8,128)}, f32[8,2688]{1,0:T(8,128)}) custom-call(s32[4]{0:T(128)} %pad_add_fusion.info, bf16[8,96]{1,0:T(8,128)(2,1)} %get-tuple-element.95.c0, bf16[8,96]{1,0:T(8,128)(2,1)} %copy-done.8, bf16[8,96]{1,0:T(8,128)(2,1)} %copy-done.9, bf16[8,96]{1,0:T(8,128)(2,1)} %copy-done.10, ...), custom_call_target="tpu_custom_call" | custom-call | flops 16777216 | bytes 1048576 | tf_op jit(solution)/shard_map/pallas_call | solution.py:428
  15.6 5.1 %collective-permute-done.4.refs_2_ = f32[8,2688]{1,0:T(8,128)S(1)} collective-permute-done((f32[8,2688]{1,0:T(8,128)}, f32[8,2688]{1,0:T(8,128)S(1)}, u32[]{:S(2)}, u32[]{:S(2)}) %collective-permute-start.4) | collective-permute-done | bytes 86048 | tf_op jit(solution)/shard_map/ppermute | solution.py:466
  25.0 13.9 %shard_map.230 = (bf16[8,256,384]{2,1,0:T(8,128)(2,1)}, bf16[8,256,1152]{2,1,0:T(8,128)(2,1)}, bf16[8,6,256,256]{3,2,1,0:T(8,128)(2,1)}, bf16[8,256,384]{2,1,0:T...) custom-call(s32[4]{0:T(128)} %pad_add_fusion.info, bf16[8,256,384]{2,1,0:T(8,128)(2,1)} %tok.7, ...), custom_call_target="tpu_custom_call" | custom-call | flops 4026531840 | bytes 15728640 | tf_op jit(solution)/shard_map/pallas_call | solution.py:428
  39.2 2.0 %collective-permute-done.11.refs_3_ = bf16[864,384]{1,0:T(8,128)(2,1)S(1)} collective-permute-done((bf16[864,384]{1,0:T(8,128)(2,1)S(1)}, bf16[864,384]{1,0:T(8,128)(2,1)S(1)}, u32[]{:S(2)}, u32[]{:S(2)}) %collective-permute-start.11) | collective-permute-done | bytes 663584 | tf_op jit(solution)/shard_map/ppermute | solution.py:466
  42.0 32.5 %shard_map.231 = (bf16[8,256,384]{2,1,0:T(8,128)(2,1)}, f32[8,256,384]{2,1,0:T(8,128)}, bf16[8,256,384]{2,1,0:T(8,128)(2,1)}, bf16[48,384]{1,0:T(8,128)(2,1)}, b...) custom-call(s32[4]{0:T(128)} %pad_add_fusion.info, bf16[8,256,384]{2,1,0:T(8,128)(2,1)} %tok.7, ...), custom_call_target="tpu_custom_call" | custom-call | flops 16307453952 | bytes 11010048 | tf_op jit(solution)/shard_map/pallas_call | solution.py:428
  74.7 1.7 collective-permute-start.12
  76.4 2.6 %collective-permute-start.13 = (bf16[48,384]{1,0:T(8,128)(2,1)}, bf16[48,384]{1,0:T(8,128)(2,1)S(1)}, u32[]{:S(2)}, u32[]{:S(2)}) collective-permute-start(bf16[48,384]{1,0:T(8,128)(2,1)} %get-tuple-element.122), channel_id=1, source_target_pairs={{0,16},{1,17},{2,18},{3,19},{4,20},{5,21},{6,22},{7,23},{8,24},{9,... | collective-permute-start | bytes 110600 | tf_op jit(solution)/shard_map/ppermute | solution.py:466
  79.1 1.6 fusion.3
  82.2 2.8 %collective-permute-done.14 = bf16[48,384]{1,0:T(8,128)(2,1)S(1)} collective-permute-done((bf16[48,384]{1,0:T(8,128)(2,1)}, bf16[48,384]{1,0:T(8,128)(2,1)S(1)}, u32[]{:S(2)}, u32[]{:S(2)}) %collective-permute-start.14) | collective-permute-done | bytes 36896 | tf_op jit(solution)/shard_map/ppermute | solution.py:466
  89.8 12.6 %shard_map.232 = (f32[8,256,384]{2,1,0:T(8,128)}, f32[384,1152]{1,0:T(8,128)}, f32[8,768]{1,0:T(8,128)}, f32[8,384]{1,0:T(8,128)}) custom-call(s32[4]{0:T(128)} %pad_add_fusion.info, bf16[8,256,384]{2,1,0:T(8,128)(2,1)} %tok.7, bf16[8,256,384]{2,1,0:T(8,128)(2,1)} %get-tuple-element.124.m1_i, bf16[8,256,1152]{2,1,0:T(8,128)(2,1)} %get-tuple-element.125.qkv_i, ...), custom_call_target="tpu_custom_call" | custom-call | flops 2818572288 | bytes 11796480 | tf_op jit(solution)/shard_map/pallas_call | solution.py:428
  102.5 2.4 %collective-permute-done.19 = bf16[192,384]{1,0:T(8,128)(2,1)S(1)} collective-permute-done((bf16[192,384]{1,0:T(8,128)(2,1)S(1)}, bf16[192,384]{1,0:T(8,128)(2,1)S(1)}, u32[]{:S(2)}, u32[]{:S(2)}) %collective-permute-start.19) | collective-permute-done | bytes 147488 | tf_op jit(solution)/shard_map/ppermute | solution.py:466
  107.2 3.0 %collective-permute-start.22 = (bf16[144,384]{1,0:T(8,128)(2,1)S(1)}, bf16[144,384]{1,0:T(8,128)(2,1)S(1)}, u32[]{:S(2)}, u32[]{:S(2)}) collective-permute-start(bf16[144,384]{1,0:T(8,128)(2,1)S(1)} %get-tuple-element.263), channel_id=1, source_target_pairs={{0,24},{1,25},{2,26},{3,27},{4,28},{5,29},{6,30},{7,31},{8,16},{9,... | collective-permute-start | bytes 331784 | tf_op jit(solution)/shard_map/ppermute | solution.py:466
  110.3 13.0 %shard_map.233 = (f32[8,256,384]{2,1,0:T(8,128)}, bf16[24,384]{1,0:T(8,128)(2,1)}, bf16[2,2,48,1152]{3,2,1,0:T(8,128)(2,1)}, bf16[2,2,48,1152]{3,2,1,0:T(8,128)(2,1)}) custom-call(s32[4]{0:T(128)} %pad_add_fusion.info, bf16[8,256,384]{2,1,0:T(8,128)(2,1)} %tok.7, bf16[8,256,384]{2,1,0:T(8,128)(2,1)} %get-tuple-element.124.m1_i, ...), custom_call_target="tpu_custom_call", output_to_operand_aliasing={{0}: (12, {})} | custom-call | flops 2818572288 | bytes 11796480 | tf_op jit(solution)/shard_map/pallas_call | solution.py:428
  125.6 3.0 %collective-permute-start.27 = (bf16[24,384]{1,0:T(8,128)(2,1)S(1)}, bf16[24,384]{1,0:T(8,128)(2,1)S(1)}, u32[]{:S(2)}, u32[]{:S(2)}) collective-permute-start(bf16[24,384]{1,0:T(8,128)(2,1)S(1)} %copy-done.5), channel_id=1, source_target_pairs={{0,24},{1,25},{2,26},{3,27},{4,28},{5,29},{6,30},{7,31},{8,16},{9,... | collective-permute-start | bytes 55304 | tf_op jit(solution)/shard_map/ppermute | solution.py:466
  129.0 2.4 %collective-permute-done.27 = bf16[24,384]{1,0:T(8,128)(2,1)S(1)} collective-permute-done((bf16[24,384]{1,0:T(8,128)(2,1)S(1)}, bf16[24,384]{1,0:T(8,128)(2,1)S(1)}, u32[]{:S(2)}, u32[]{:S(2)}) %collective-permute-start.27) | collective-permute-done | bytes 18464 | tf_op jit(solution)/shard_map/ppermute | solution.py:466
  131.4 1.7 collective-permute-done.28
  137.5 8.7 %collective-permute-done.32 = bf16[192,384]{1,0:T(8,128)(2,1)S(1)} collective-permute-done((bf16[192,384]{1,0:T(8,128)(2,1)S(1)}, bf16[192,384]{1,0:T(8,128)(2,1)S(1)}, u32[]{:S(2)}, u32[]{:S(2)}) %collective-permute-start.32) | collective-permute-done | bytes 147488 | tf_op jit(solution)/shard_map/ppermute | solution.py:466
  146.3 2.1 %collective-permute-start.35 = (bf16[144,384]{1,0:T(8,128)(2,1)S(1)}, bf16[144,384]{1,0:T(8,128)(2,1)}, u32[]{:S(2)}, u32[]{:S(2)}) collective-permute-start(bf16[144,384]{1,0:T(8,128)(2,1)S(1)} %add_convert_fusion.6), channel_id=1, source_target_pairs={{0,16},{1,17},{2,18},{3,19},{4,20},{5,21},{6,22},{7,23},{8,24},{9,... | collective-permute-start | bytes 331784 | tf_op jit(solution)/shard_map/ppermute | solution.py:466
  148.5 2.2 %collective-permute-start.36 = (bf16[144,384]{1,0:T(8,128)(2,1)S(1)}, bf16[144,384]{1,0:T(8,128)(2,1)}, u32[]{:S(2)}, u32[]{:S(2)}) collective-permute-start(bf16[144,384]{1,0:T(8,128)(2,1)S(1)} %add_convert_fusion.6), channel_id=1, source_target_pairs={{0,24},{1,25},{2,26},{3,27},{4,28},{5,29},{6,30},{7,31},{8,16},{9,... | collective-permute-start | bytes 331784 | tf_op jit(solution)/shard_map/ppermute | solution.py:466
  151.4 1.6 collective-permute-start.37
  168.5 1.7 collective-permute-done.42
  (203 shorter events, 43.4 us)
Async XLA Ops:
  10.4 11.6 %collective-permute-start.7 = (bf16[96,1152]{1,0:T(8,128)(2,1)}, bf16[96,1152]{1,0:T(8,128)(2,1)S(1)}, u32[]{:S(2)}, u32[]{:S(2)}) collective-permute-start(bf16[96,1152]{1,0:T(8,128)(2,1)} %refs_0_.3), channel_id=1, source_target_pairs={{0,2},{1,3},{2,0},{3,1},{4,6},{5,7},{6,4},{7,5},{8,10},{9,11},{10,... | collective-permute-start | bytes 663560 | tf_op jit(solution)/shard_map/ppermute | solution.py:466
  13.9 6.8 %collective-permute-start.4 = (f32[8,2688]{1,0:T(8,128)}, f32[8,2688]{1,0:T(8,128)S(1)}, u32[]{:S(2)}, u32[]{:S(2)}) collective-permute-start(f32[8,2688]{1,0:T(8,128)} %get-tuple-element.103), channel_id=1, source_target_pairs={{0,2},{1,3},{2,0},{3,1},{4,6},{5,7},{6,4},{7,5},{8,10},{9,11},{10,... | collective-permute-start | bytes 258056 | tf_op jit(solution)/shard_map/ppermute | solution.py:466
  15.2 6.0 %collective-permute-start.5 = (f32[8,2688]{1,0:T(8,128)}, f32[8,2688]{1,0:T(8,128)S(1)}, u32[]{:S(2)}, u32[]{:S(2)}) collective-permute-start(f32[8,2688]{1,0:T(8,128)} %get-tuple-element.104), channel_id=1, source_target_pairs={{0,3},{1,2},{2,1},{3,0},{4,7},{5,6},{6,5},{7,4},{8,11},{9,10},{10,... | collective-permute-start | bytes 258056 | tf_op jit(solution)/shard_map/ppermute | solution.py:466
  21.2 17.8 %collective-permute-start.10 = (bf16[864,384]{1,0:T(8,128)(2,1)}, bf16[864,384]{1,0:T(8,128)(2,1)S(1)}, u32[]{:S(2)}, u32[]{:S(2)}) collective-permute-start(bf16[864,384]{1,0:T(8,128)(2,1)} %get-tuple-element.112.refs_0_), channel_id=1, source_target_pairs={{0,2},{1,3},{2,0},{3,1},{4,6},{5,7},{6,4},{7,5},{8,10},{9,11},{10,... | collective-permute-start | bytes 1990664 | tf_op jit(solution)/shard_map/ppermute | solution.py:466
  22.5 16.7 %collective-permute-start.9 = (bf16[864,384]{1,0:T(8,128)(2,1)}, bf16[864,384]{1,0:T(8,128)(2,1)S(1)}, u32[]{:S(2)}, u32[]{:S(2)}) collective-permute-start(bf16[864,384]{1,0:T(8,128)(2,1)} %get-tuple-element.112.refs_0_), channel_id=1, source_target_pairs={{0,1},{1,0},{2,3},{3,2},{4,5},{5,4},{6,7},{7,6},{8,9},{9,8},{10,11... | collective-permute-start | bytes 1990664 | tf_op jit(solution)/shard_map/ppermute | solution.py:466
  74.7 6.0 %collective-permute-start.12 = (bf16[48,384]{1,0:T(8,128)(2,1)}, bf16[48,384]{1,0:T(8,128)(2,1)S(1)}, u32[]{:S(2)}, u32[]{:S(2)}) collective-permute-start(bf16[48,384]{1,0:T(8,128)(2,1)} %get-tuple-element.122), channel_id=1, source_target_pairs={{0,8},{1,9},{2,10},{3,11},{4,12},{5,13},{6,14},{7,15},{8,0},{9,1},... | collective-permute-start | bytes 110600 | tf_op jit(solution)/shard_map/ppermute | solution.py:466
  79.0 6.0 %collective-permute-start.14 = (bf16[48,384]{1,0:T(8,128)(2,1)}, bf16[48,384]{1,0:T(8,128)(2,1)S(1)}, u32[]{:S(2)}, u32[]{:S(2)}) collective-permute-start(bf16[48,384]{1,0:T(8,128)(2,1)} %get-tuple-element.122), channel_id=1, source_target_pairs={{0,24},{1,25},{2,26},{3,27},{4,28},{5,29},{6,30},{7,31},{8,16},{9,... | collective-permute-start | bytes 110600 | tf_op jit(solution)/shard_map/ppermute | solution.py:466
  85.0 20.0 %collective-permute-start.16 = (bf16[432,384]{1,0:T(8,128)(2,1)S(1)}, bf16[432,384]{1,0:T(8,128)(2,1)S(1)}, u32[]{:S(2)}, u32[]{:S(2)}) collective-permute-start(bf16[432,384]{1,0:T(8,128)(2,1)S(1)} %get-tuple-element.216), channel_id=1, source_target_pairs={{0,4},{1,5},{2,6},{3,7},{4,0},{5,1},{6,2},{7,3},{8,12},{9,13},{10,... | collective-permute-start | bytes 995336 | tf_op jit(solution)/shard_map/ppermute | solution.py:466
  86.5 18.4 %collective-permute-start.17 = (bf16[432,384]{1,0:T(8,128)(2,1)S(1)}, bf16[432,384]{1,0:T(8,128)(2,1)S(1)}, u32[]{:S(2)}, u32[]{:S(2)}) collective-permute-start(bf16[432,384]{1,0:T(8,128)(2,1)S(1)} %get-tuple-element.215), channel_id=1, source_target_pairs={{0,2},{1,3},{2,0},{3,1},{4,6},{5,7},{6,4},{7,5},{8,10},{9,11},{10,... | collective-permute-start | bytes 995336 | tf_op jit(solution)/shard_map/ppermute | solution.py:466
  87.6 17.3 %collective-permute-start.18 = (bf16[432,384]{1,0:T(8,128)(2,1)S(1)}, bf16[432,384]{1,0:T(8,128)(2,1)S(1)}, u32[]{:S(2)}, u32[]{:S(2)}) collective-permute-start(bf16[432,384]{1,0:T(8,128)(2,1)S(1)} %get-tuple-element.214), channel_id=1, source_target_pairs={{0,6},{1,7},{2,4},{3,5},{4,2},{5,3},{6,0},{7,1},{8,14},{9,15},{10,... | collective-permute-start | bytes 995336 | tf_op jit(solution)/shard_map/ppermute | solution.py:466
  88.5 16.3 %collective-permute-start.19 = (bf16[192,384]{1,0:T(8,128)(2,1)S(1)}, bf16[192,384]{1,0:T(8,128)(2,1)S(1)}, u32[]{:S(2)}, u32[]{:S(2)}) collective-permute-start(bf16[192,384]{1,0:T(8,128)(2,1)S(1)} %pad_maximum_fusion.13), channel_id=1, source_target_pairs={{0,2},{1,3},{2,0},{3,1},{4,6},{5,7},{6,4},{7,5},{8,10},{9,11},{10,... | collective-permute-start | bytes 442376 | tf_op jit(solution)/shard_map/ppermute | solution.py:466
  105.2 18.1 %collective-permute-start.23 = (bf16[384,384]{1,0:T(8,128)(2,1)S(1)}, bf16[384,384]{1,0:T(8,128)(2,1)S(1)}, u32[]{:S(2)}, u32[]{:S(2)}) collective-permute-start(bf16[384,384]{1,0:T(8,128)(2,1)S(1)} %pad_maximum_fusion.6), channel_id=1, source_target_pairs={{0,4},{1,5},{2,6},{3,7},{4,0},{5,1},{6,2},{7,3},{8,12},{9,13},{10,... | collective-permute-start | bytes 884744 | tf_op jit(solution)/shard_map/ppermute | solution.py:466
  105.8 17.6 %collective-permute-start.20 = (bf16[144,384]{1,0:T(8,128)(2,1)S(1)}, bf16[144,384]{1,0:T(8,128)(2,1)S(1)}, u32[]{:S(2)}, u32[]{:S(2)}) collective-permute-start(bf16[144,384]{1,0:T(8,128)(2,1)S(1)} %get-tuple-element.264), channel_id=1, source_target_pairs={{0,8},{1,9},{2,10},{3,11},{4,12},{5,13},{6,14},{7,15},{8,0},{9,1},... | collective-permute-start | bytes 331784 | tf_op jit(solution)/shard_map/ppermute | solution.py:466
  105.9 17.6 %collective-permute-start.21 = (bf16[144,384]{1,0:T(8,128)(2,1)S(1)}, bf16[144,384]{1,0:T(8,128)(2,1)S(1)}, u32[]{:S(2)}, u32[]{:S(2)}) collective-permute-start(bf16[144,384]{1,0:T(8,128)(2,1)S(1)} %get-tuple-element.265), channel_id=1, source_target_pairs={{0,16},{1,17},{2,18},{3,19},{4,20},{5,21},{6,22},{7,23},{8,24},{9,... | collective-permute-start | bytes 331784 | tf_op jit(solution)/shard_map/ppermute | solution.py:466
  107.2 16.2 %collective-permute-start.22 = (bf16[144,384]{1,0:T(8,128)(2,1)S(1)}, bf16[144,384]{1,0:T(8,128)(2,1)S(1)}, u32[]{:S(2)}, u32[]{:S(2)}) collective-permute-start(bf16[144,384]{1,0:T(8,128)(2,1)S(1)} %get-tuple-element.263), channel_id=1, source_target_pairs={{0,24},{1,25},{2,26},{3,27},{4,28},{5,29},{6,30},{7,31},{8,16},{9,... | collective-permute-start | bytes 331784 | tf_op jit(solution)/shard_map/ppermute | solution.py:466
  125.6 5.8 %collective-permute-start.27 = (bf16[24,384]{1,0:T(8,128)(2,1)S(1)}, bf16[24,384]{1,0:T(8,128)(2,1)S(1)}, u32[]{:S(2)}, u32[]{:S(2)}) collective-permute-start(bf16[24,384]{1,0:T(8,128)(2,1)S(1)} %copy-done.5), channel_id=1, source_target_pairs={{0,24},{1,25},{2,26},{3,27},{4,28},{5,29},{6,30},{7,31},{8,16},{9,... | collective-permute-start | bytes 55304 | tf_op jit(solution)/shard_map/ppermute | solution.py:466
  133.5 12.6 %collective-permute-start.29 = (bf16[240,384]{1,0:T(8,128)(2,1)S(1)}, bf16[240,384]{1,0:T(8,128)(2,1)S(1)}, u32[]{:S(2)}, u32[]{:S(2)}) collective-permute-start(bf16[240,384]{1,0:T(8,128)(2,1)S(1)} %get-tuple-element.272), channel_id=1, source_target_pairs={{0,4},{1,5},{2,6},{3,7},{4,0},{5,1},{6,2},{7,3},{8,12},{9,13},{10,... | collective-permute-start | bytes 552968 | tf_op jit(solution)/shard_map/ppermute | solution.py:466
  135.1 11.0 %collective-permute-start.30 = (bf16[240,384]{1,0:T(8,128)(2,1)S(1)}, bf16[240,384]{1,0:T(8,128)(2,1)S(1)}, u32[]{:S(2)}, u32[]{:S(2)}) collective-permute-start(bf16[240,384]{1,0:T(8,128)(2,1)S(1)} %get-tuple-element.271), channel_id=1, source_target_pairs={{0,2},{1,3},{2,0},{3,1},{4,6},{5,7},{6,4},{7,5},{8,10},{9,11},{10,... | collective-permute-start | bytes 552968 | tf_op jit(solution)/shard_map/ppermute | solution.py:466
  136.3 9.9 %collective-permute-start.31 = (bf16[240,384]{1,0:T(8,128)(2,1)S(1)}, bf16[240,384]{1,0:T(8,128)(2,1)S(1)}, u32[]{:S(2)}, u32[]{:S(2)}) collective-permute-start(bf16[240,384]{1,0:T(8,128)(2,1)S(1)} %get-tuple-element.206), channel_id=1, source_target_pairs={{0,6},{1,7},{2,4},{3,5},{4,2},{5,3},{6,0},{7,1},{8,14},{9,15},{10,... | collective-permute-start | bytes 552968 | tf_op jit(solution)/shard_map/ppermute | solution.py:466
  137.1 9.1 %collective-permute-start.32 = (bf16[192,384]{1,0:T(8,128)(2,1)S(1)}, bf16[192,384]{1,0:T(8,128)(2,1)S(1)}, u32[]{:S(2)}, u32[]{:S(2)}) collective-permute-start(bf16[192,384]{1,0:T(8,128)(2,1)S(1)} %pad_maximum_fusion.14), channel_id=1, source_target_pairs={{0,16},{1,17},{2,18},{3,19},{4,20},{5,21},{6,22},{7,23},{8,24},{9,... | collective-permute-start | bytes 442376 | tf_op jit(solution)/shard_map/ppermute | solution.py:466
  146.3 15.9 %collective-permute-start.34 = (bf16[144,384]{1,0:T(8,128)(2,1)S(1)}, bf16[144,384]{1,0:T(8,128)(2,1)S(1)}, u32[]{:S(2)}, u32[]{:S(2)}) collective-permute-start(bf16[144,384]{1,0:T(8,128)(2,1)S(1)} %add_convert_fusion.6), channel_id=1, source_target_pairs={{0,8},{1,9},{2,10},{3,11},{4,12},{5,13},{6,14},{7,15},{8,0},{9,1},... | collective-permute-start | bytes 331784 | tf_op jit(solution)/shard_map/ppermute | solution.py:466
  146.3 15.9 %collective-permute-start.35 = (bf16[144,384]{1,0:T(8,128)(2,1)S(1)}, bf16[144,384]{1,0:T(8,128)(2,1)}, u32[]{:S(2)}, u32[]{:S(2)}) collective-permute-start(bf16[144,384]{1,0:T(8,128)(2,1)S(1)} %add_convert_fusion.6), channel_id=1, source_target_pairs={{0,16},{1,17},{2,18},{3,19},{4,20},{5,21},{6,22},{7,23},{8,24},{9,... | collective-permute-start | bytes 331784 | tf_op jit(solution)/shard_map/ppermute | solution.py:466
  148.5 13.7 %collective-permute-start.36 = (bf16[144,384]{1,0:T(8,128)(2,1)S(1)}, bf16[144,384]{1,0:T(8,128)(2,1)}, u32[]{:S(2)}, u32[]{:S(2)}) collective-permute-start(bf16[144,384]{1,0:T(8,128)(2,1)S(1)} %add_convert_fusion.6), channel_id=1, source_target_pairs={{0,24},{1,25},{2,26},{3,27},{4,28},{5,29},{6,30},{7,31},{8,16},{9,... | collective-permute-start | bytes 331784 | tf_op jit(solution)/shard_map/ppermute | solution.py:466
  151.4 8.9 %collective-permute-start.37 = (bf16[432,384]{1,0:T(8,128)(2,1)S(1)}, bf16[432,384]{1,0:T(8,128)(2,1)S(1)}, u32[]{:S(2)}, u32[]{:S(2)}) collective-permute-start(bf16[432,384]{1,0:T(8,128)(2,1)S(1)} %constant_dynamic-update-slice_fusion.28), channel_id=1, source_target_pairs={{0,4},{1,5},{2,6},{3,7},{4,0},{5,1},{6,2},{7,3},{8,12},{9,13},{10,... | collective-permute-start | bytes 995336 | tf_op jit(solution)/shard_map/ppermute | solution.py:466
  (37 other events, 126.1 us)

commit v4 on v3

--- a/solution.py
+++ b/solution.py
@@ -57,28 +57,7 @@
     return (lane < shape[-1] // 2) if half == 0 else (lane >= shape[-1] // 2)
 
 
-def condition(info, cond, b_ada, b_qv, b_o, b_1, b_2, w_o, w_1, w_2, *refs):
-    cuts, share, packed, tall = refs[0:4], refs[4], refs[5], refs[6]
-    c = cond[...].astype(F32)
-    cs = c / (1.0 + jnp.exp(-c))
-    cut = cs.shape[1] // 4
-    for k, ref in enumerate(cuts):
-        mine = jnp.bitwise_xor(info[0], k)
-        ref[...] = sum(
-            jnp.where(mine == j, cs[:, j * cut : (j + 1) * cut], 0.0) for j in range(4)
-        ).astype(BF16)
-    share[...] = jnp.zeros_like(share)
-    n = b_ada.shape[0]
-    row = b_ada[...].astype(F32).reshape(1, n)
-    for j in range(4):
-
-        @pl.when(info[0] == j)
-        def _():
-            share[:, j * n : (j + 1) * n] = row
-
-    packed[...] = jnp.zeros_like(packed)
-    for i, b in enumerate((b_qv, b_o, b_1, b_2)):
-        packed[i : i + 1, 0 : b.shape[0]] = b[...].astype(F32).reshape(1, b.shape[0])
+def pack(info, w_o, w_1, w_2, tall):
     rows, width = w_o.shape
     tall[0:rows] = w_o[...]
     many = w_1.shape[1] // width
@@ -87,11 +66,32 @@
     tall[(1 + many) * rows :] = w_2[...]
 
 
-def ada_parts(info, c0, c1, c2, c3, w_ada, share, packed, *outs):
-    for cut, out in zip((c0, c1, c2, c3), outs):
-        n = w_ada.shape[1]
-        out[:, 0:n] = nn(cut[...], w_ada[...]) + share[...]
-        out[:, n:] = packed[...]
+def ada_parts(info, c0, c1, c2, c3, w_ada, b_ada, b_qv, b_o, b_1, b_2, *refs):
+    outs, share, packed = refs[0:8], refs[8], refs[9]
+    share[...] = jnp.zeros_like(share)
+    packed[...] = jnp.zeros_like(packed)
+    n = b_ada.shape[0]
+    row = b_ada[...].astype(F32).reshape(1, n)
+    for j in range(4):
+
+        @pl.when(info[0] == j)
+        def _():
+            share[:, j * n : (j + 1) * n] = row
+
+    for i, b in enumerate((b_qv, b_o, b_1, b_2)):
+        packed[i : i + 1, 0 : b.shape[0]] = b[...].astype(F32).reshape(1, b.shape[0])
+    m = w_ada.shape[1] // 3
+    for cond, first, rest in zip((c0, c1, c2, c3), outs[0:4], outs[4:8]):
+        c = cond[...].astype(F32)
+        cs = c / (1.0 + jnp.exp(-c))
+        cut = cs.shape[1] // 4
+        mine = sum(
+            jnp.where(info[0] == j, cs[:, j * cut : (j + 1) * cut], 0.0) for j in range(4)
+        ).astype(BF16)
+        part = nn(mine, w_ada[...]) + share[...]
+        first[:, 0:m] = part[:, 0:m]
+        first[:, m:] = packed[...]
+        rest[...] = part[:, m:]
 
 
 def bias_row(table, at, n):
@@ -100,8 +100,8 @@
 
 def attn_fwd(info, tok, *refs, per):
     parts, wq = refs[0:4], refs[4:8]
-    m1_o, qkv_o, p_o, att_o, ada, table = refs[8:14]
-    wq_s, bias_s, sem_q = refs[14:]
+    m1_o, qkv_o, p_o, att_o, ada, table, wq_o = refs[8:15]
+    wq_s, bias_s, sem_q = refs[15:]
     step = pl.program_id(0)
     width = tok.shape[-1]
 
@@ -110,15 +110,16 @@
         cq = piece_copies(info[0], wq, wq_s, sem_q)
         for copy in cq:
             copy.start()
-        ada[...] = sum(v[:, 0 : 6 * width] for v in parts)
+        ada[...] = sum(v[:, 0 : 2 * width] for v in parts)
         for k in range(4):
-            table[jnp.bitwise_xor(info[0], k)] = parts[k][:, 6 * width :]
+            table[jnp.bitwise_xor(info[0], k)] = parts[k][:, 2 * width :]
         row_qv = bias_row(table, 0, width // 2)
         bias_s[:, 0:width] = row_qv[:, 0:width]
         bias_s[:, width : 2 * width] = jnp.zeros((1, width), F32)
         bias_s[:, 2 * width : 3 * width] = row_qv[:, width : 2 * width]
         for copy in cq:
             copy.wait()
+        wq_o[...] = wq_s[...]
 
     qkvs, ss, ps, atts = {}, {}, {}, {}
     part = lambda l, at, j: qkvs[l][:, at + 128 * j : at + 128 * j + 128]
@@ -169,10 +170,10 @@
             stage_c(u - 2)
 
 
-def ffn_both(info, tok, att_i, dy_i, ada, cond, table, *refs, per, chunk):
-    pieces = refs[0:4]
-    out_o, dx1_o, datt_o, early_o, keep_o, send_o = refs[4:10]
-    wo_s, w1_s, w2_s, go_s, g1_s, g2_s, small_s, gb_s, bo_s, b1_s, b2_s, sems = refs[10:]
+def ffn_both(info, tok, att_i, dy_i, cond, table, *refs, per, chunk):
+    ada_parts, pieces = refs[0:4], refs[4:8]
+    out_o, dx1_o, datt_o, early_o, keep_o, send_o = refs[8:14]
+    wo_s, w1_s, w2_s, go_s, g1_s, g2_s, small_s, gb_s, bo_s, b1_s, b2_s, ada, sems = refs[14:]
     step = pl.program_id(0)
     length, width = tok.shape[1:]
     hidden = w1_s.shape[1]
@@ -199,6 +200,7 @@
         g1_s[...] = jnp.zeros_like(g1_s)
         g2_s[...] = jnp.zeros_like(g2_s)
         gb_s[...] = jnp.zeros_like(gb_s)
+        ada[...] = sum(v[...] for v in ada_parts)
         bo_s[...] = bias_row(table, 1, width // 4)
         b1_s[...] = bias_row(table, 2, hidden // 4)
         b2_s[...] = bias_row(table, 3, width // 4)
@@ -218,7 +220,7 @@
     def deep(v):
         return v.reshape(per, length, v.shape[-1])
 
-    gate1, shift2, scale2, gate2 = rows_of(2), rows_of(3), rows_of(4), rows_of(5)
+    gate1, shift2, scale2, gate2 = rows_of(0), rows_of(1), rows_of(2), rows_of(3)
     att = flat(att_i[...])
     branch = deep(nn(att, wo_s[...]) + bo_s[...])
     x1 = tok[...].astype(F32) + gate1 * branch
@@ -234,10 +236,10 @@
         cols = slice(j * chunk, (j + 1) * chunk)
         h = nn(m2, w1_s[:, cols]) + b1_s[:, cols]
         hh = h * h
-        t = jnp.tanh(h * (GELU_C + (GELU_C * GELU_A) * hh))
-        half_t = 0.5 + 0.5 * t
+        u = h * (GELU_C + (GELU_C * GELU_A) * hh)
+        half_t = 0.5 + 0.5 * jnp.tanh(u)
         g = (h * half_t).astype(BF16)
-        slope = half_t + (0.5 * h) * (1.0 - t * t) * (GELU_C + (3.0 * GELU_C * GELU_A) * hh)
+        slope = half_t * (1.0 + (1.0 - half_t) * (6.0 * u - (4.0 * GELU_C) * h))
         part = nn(g, w2_s[cols, :])
         ffn = part if ffn is None else ffn + part
         g2_s[:, cols] += nn(df_t, g)
@@ -294,22 +296,18 @@
                     ref[y, x, 8 * half : 9 * half, :] = go_s[take, :].astype(BF16)
 
 
-def attn_bwd(info, tok, m1_i, qkv_i, p_i, datt_i, dx1_i, ada, *refs, per, base, last):
-    wq, refs = refs[0:4], refs[4:]
+def attn_bwd(info, tok, m1_i, qkv_i, p_i, datt_i, dx1_i, ada, wq_s, *refs, per, base, last):
     step = pl.program_id(0)
     length, width = tok.shape[1:]
     if last:
-        _, g_i, small_i, gb_i = refs[0:4]
-        gtok_o, late_o, keep_o, send_o = refs[4:8]
-        wq_s, sem_q, g_s, small_s, gb_s = refs[8:]
+        _, g_i, small_i, gb_i, early = refs[0:5]
+        gtok_o, late_o, keep_o, send_o = refs[5:9]
+        g_s, small_s, gb_s = refs[9:]
     else:
-        gtok_o, g_s, small_s, gb_s, wq_s, sem_q = refs
+        gtok_o, g_s, small_s, gb_s = refs
 
     @pl.when(step == 0)
     def _():
-        copies = piece_copies(info[0], wq, wq_s, sem_q)
-        for copy in copies:
-            copy.start()
         if last:
             g_s[...] = g_i[...]
             small_s[...] = small_i[...]
@@ -318,8 +316,6 @@
             g_s[...] = jnp.zeros_like(g_s)
             small_s[...] = jnp.zeros_like(small_s)
             gb_s[...] = jnp.zeros_like(gb_s)
-        for copy in copies:
-            copy.wait()
 
     part = lambda ref, l, at, j: ref[l, :, at + 128 * j : at + 128 * j + 128]
     dvs, dps, dss, dks, dqs, dqkvs, dm1s = {}, {}, {}, {}, {}, {}, {}
@@ -388,6 +384,7 @@
             for i in range(2):
                 late_o[8 * i : 8 * i + 8, :] = small_s[:, i * width : (i + 1) * width].astype(BF16)
             late_o[16:24, :] = gb_s[...].astype(BF16)
+            late_o[24:32, :] = early[32:40, :]
             core = jnp.bitwise_and(info[0], 1)
             half = width // 8
             for y in range(2):
@@ -396,6 +393,42 @@
                     for x in range(2):
                         take = pl.ds(pl.multiple_of(shard * 2 * half + x * half, 8), half)
                         ref[y, x] = g_s[take, :].astype(BF16)
+
+
+def join(info, keep, got, *refs):
+    late, outs = refs[:-4], refs[-4:]
+    half, width = keep.shape[2], late[0].shape[1]
+    n = late[0].shape[0]
+    for k, out in enumerate(outs):
+        y, x = jnp.bitwise_xor(info[1], k >> 1), jnp.bitwise_xor(info[2], k & 1)
+        total = (keep[y, x].astype(F32) + got[y, x].astype(F32)).astype(BF16)
+        for i in range(3):
+            out[i * half : (i + 1) * half] = total[:, i * width : (i + 1) * width]
+        for z, piece in enumerate(late):
+            at = pl.multiple_of(3 * half + n * jnp.bitwise_xor(info[3], z), 16)
+            out[pl.ds(at, n)] = piece[0:n]
+
+
+def finish(info, w_late, sum_late, w_early, sum_early, few, gw, gb_ada, gb_o, gb_1, gb_2, row):
+    cols, width = w_late.shape[1], few.shape[1]
+    gw[:, 0:cols] = w_late[...]
+    gw[:, cols:] = w_early[...]
+    row[0:1, 0:cols] = sum_late[...]
+    row[0:1, cols:] = sum_early[...]
+    n_a, n_o, n_1 = gb_ada.shape[0], gb_o.shape[0], gb_1.shape[0]
+    rest = 4 * n_1 // width
+    for i in range(rest):
+        row[1:2, i * width : (i + 1) * width] = few[i : i + 1]
+    row[2:3, 0:width] = few[rest : rest + 1]
+    row[3:4, 0:width] = few[rest + 1 : rest + 2]
+    for j in range(4):
+
+        @pl.when(info[0] == j)
+        def _():
+            gb_ada[...] = row[0, j * n_a : (j + 1) * n_a]
+            gb_1[...] = row[1, j * n_1 : (j + 1) * n_1]
+            gb_o[...] = row[2, j * n_o : (j + 1) * n_o]
+            gb_2[...] = row[3, j * n_o : (j + 1) * n_o]
 
 
 def tree_sum(values):
@@ -466,26 +499,29 @@
         return lax.ppermute(v, ("rep", "shard"), pairs)
 
     whole = lambda vs: [full(v.shape) for v in vs]
-    ins = (cond, b_ada, b_qv, b_o, b_1, b_2, w_o, w_1, w_2)
-    outs = [jax.ShapeDtypeStruct((count, quarter), BF16)] * 4 + [
-        jax.ShapeDtypeStruct((1, 6 * width), F32),
-        jax.ShapeDtypeStruct((8, width), F32),
+    conds = [cond] + [swap(cond, k) for k in range(1, 4)]
+    outs = [
         jax.ShapeDtypeStruct((quarter + quarter * hidden // width + hidden // 4, width), BF16),
     ]
-    *cuts, share, packed, ffn_w = call(
-        condition, info, ins, whole(ins), outs, whole(outs), [], (1,), 60, 0, 1 << 17
-    )
-    cuts = [cuts[0]] + [swap(cuts[k], k) for k in range(1, 4)]
-    near_qkv, far_qkv = after((w_qkv, w_qkv), *cuts)
+    ins = (w_o, w_1, w_2)
+    (ffn_w,) = call(pack, info, ins, whole(ins), outs, whole(outs), [], (1,), 60, 0, 1 << 20)
+    *conds, ffn_w = after(conds + [ffn_w])
+    near_qkv, far_qkv = after((w_qkv, w_qkv), *conds)
     near_qkv, far_qkv = swap(near_qkv, 1), swap(far_qkv, 2)
-    ins = tuple(cuts) + (w_ada, share, packed)
-    outs = [jax.ShapeDtypeStruct((count, 7 * width), F32)] * 4
-    parts = call(ada_parts, info, ins, whole(ins), outs, whole(outs), [], (1,), 60, 1 << 24, 1 << 20)
-    sent = parts[0]
+    near_w = swap(ffn_w, 1)
+    ins = tuple(conds) + (w_ada, b_ada, b_qv, b_o, b_1, b_2)
+    outs = [jax.ShapeDtypeStruct((count, 3 * width), F32)] * 4
+    outs += [jax.ShapeDtypeStruct((count, 4 * width), F32)] * 4
+    scratch = [pltpu.VMEM((1, 6 * width), F32), pltpu.VMEM((8, width), F32)]
+    parts = call(
+        ada_parts, info, ins, whole(ins), outs, whole(outs), scratch, (1,), 60, 1 << 24, 1 << 20
+    )
     p_qkv = (w_qkv, near_qkv, far_qkv, swap(far_qkv, 1))
+    parts, later = parts[:4], parts[4:]
     parts = [parts[0]] + [swap(parts[k], k) for k in range(1, 4)]
-    near_w = swap(after(ffn_w, sent), 1)
-    far_w = swap(after(ffn_w, *parts), 2)
+    *later, ffn_far = after(list(later) + [ffn_w], *parts)
+    later = [later[0]] + [swap(later[k], k) for k in range(1, 4)]
+    far_w = swap(ffn_far, 2)
 
     anyspec = pl.BlockSpec(memory_space=pl.ANY)
     dma4 = pltpu.SemaphoreType.DMA((4,))
@@ -494,7 +530,7 @@
     per = 2
     per3 = 1
     lat = lambda *tail: pl.BlockSpec((per,) + tail, lambda i, _: (i,) + (0,) * len(tail))
-    m1, qkv, probs, att, ada, table = call(
+    m1, qkv, probs, att, ada, table, wq_all = call(
         functools.partial(attn_fwd, per=per),
         info,
         (latent_tokens,) + tuple(parts) + p_qkv,
@@ -504,16 +540,18 @@
             jax.ShapeDtypeStruct((count, length, 3 * width), BF16),
             jax.ShapeDtypeStruct((count, HEADS, length, length), BF16),
             jax.ShapeDtypeStruct((count, length, width), BF16),
-            jax.ShapeDtypeStruct((count, 6 * width), F32),
+            jax.ShapeDtypeStruct((count, 2 * width), F32),
             jax.ShapeDtypeStruct((4, 8, width), F32),
+            jax.ShapeDtypeStruct((width, 3 * width), BF16),
         ],
         [
             lat(length, width),
             lat(length, 3 * width),
             lat(HEADS, length, length),
             lat(length, width),
-            full((count, 6 * width)),
+            full((count, 2 * width)),
             full((4, 8, width)),
+            full((width, 3 * width)),
         ],
         [pltpu.VMEM((width, 3 * width), BF16), pltpu.VMEM((1, 3 * width), F32), dma4],
         (count // per,),
@@ -523,7 +561,7 @@
         tokens * length * HEADS,
     )
 
-    far_w = after(far_w, table)
+    far_w, *later = after([far_w] + later, table)
     p_ffn = (ffn_w, near_w, far_w, swap(far_w, 1))
 
     per2 = 2 if count % 2 == 0 else 1
@@ -532,9 +570,10 @@
     block_out, dx1, datt, early, keep_f, send_f = call(
         functools.partial(ffn_both, per=per2, chunk=hidden),
         info,
-        (latent_tokens, att, grad_out, ada, cond, table) + p_ffn,
+        (latent_tokens, att, grad_out, cond, table) + tuple(later) + p_ffn,
         [lat2(length, width)] * 3
-        + [full(ada.shape), full(cond.shape), full(table.shape)]
+        + [full(cond.shape), full(table.shape)]
+        + [full(v.shape) for v in later]
         + [anyspec] * 4,
         [
             jax.ShapeDtypeStruct((count, length, width), BF16),
@@ -556,6 +595,7 @@
             pltpu.VMEM((1, width), F32),
             pltpu.VMEM((1, hidden), F32),
             pltpu.VMEM((1, width), F32),
+            pltpu.VMEM((count, 4 * width), F32),
             pltpu.SemaphoreType.DMA((4 * (hidden // width + 2),)),
         ],
         (count // per2,),
@@ -587,7 +627,7 @@
         return call(
             functools.partial(attn_bwd, per=per3, base=base, last=last),
             info,
-            (latent_tokens, m1, qkv, probs, datt, dx1, ada) + p_qkv + extra,
+            (latent_tokens, m1, qkv, probs, datt, dx1, ada, wq_all) + extra,
             [
                 at(length, width),
                 at(length, width),
@@ -596,12 +636,12 @@
                 at(length, width),
                 at(length, width),
                 full(ada.shape),
+                full(wq_all.shape),
             ]
-            + [anyspec] * 4
             + extra_specs,
             [jax.ShapeDtypeStruct((count, length, width), F32)] + outs,
             [at(length, width)] + out_specs,
-            [pltpu.VMEM((width, 3 * width), BF16), dma4] + scratch,
+            scratch,
             (half_n // per3,),
             60,
             6 * tokens * width * width + 5 * tokens * length * width,
@@ -635,18 +675,14 @@
         return pair(v, 0, 2 * bit, (z_at & bit) != 0)
 
     n_f, n_e = 9 * half, early.shape[0]
-    early_z = over_z(early, [early] * (n_z - 1))
     parts_f = chip_sum(keep_f, send_f)
-    *early_z, first_part = after(early_z + parts_f[:1])
-    parts_f = [first_part] + parts_f[1:]
-    early_g = jnp.concatenate(ordered(early_z, z_at), axis=0)
 
     got = over_plane(parts_f[0], parts_f[1:])
-    early_x = pair(early_g, 2, 0, y_at == 1)
+    early_y = pair(early, 2, 0, y_at == 1)
     gtok, g_half, small_half, gb_half = backward(
         0, False, after(info, *parts_f), (), [], acc_shapes, acc_specs, [], None
     )
-    *got, early_g = after(got + [early_x], gb_half)
+    *got, early_y = after(got + [early_y], gb_half)
     total_f = tree_sum(got).astype(BF16)
     z_low = z_at & 3
     loads = [
@@ -654,6 +690,7 @@
             [
                 lax.dynamic_slice_in_dim(total_f, (z_low ^ (k & 3)) * 2 * half, 2 * half, 0),
                 total_f[8 * half :],
+                early_y,
             ],
             axis=0,
         )
@@ -661,44 +698,60 @@
     ]
 
     got = over_z(loads[0], loads[1:])
-    early_y = pair(early_g, 0, 1, x_at == 1)
     send_shape = (2, 2, half, 3 * width)
     grad_tokens, late, keep_a, send_a = backward(
         count // 2,
         True,
         after(info, *loads),
-        (gtok, g_half, small_half, gb_half),
-        [anyspec] + acc_specs,
+        (gtok, g_half, small_half, gb_half, early),
+        [anyspec] + acc_specs + [full(early.shape)],
         [
-            jax.ShapeDtypeStruct((24, width), BF16),
+            jax.ShapeDtypeStruct((32, width), BF16),
             jax.ShapeDtypeStruct(send_shape, BF16),
             jax.ShapeDtypeStruct(send_shape, BF16),
         ],
-        [full((24, width)), full(send_shape), full(send_shape)],
+        [full((32, width)), full(send_shape), full(send_shape)],
         [pltpu.VMEM(v, F32) for v in acc],
-        {12: 0},
-    )
-    *got, early_g, keep_a, send_a, late = after(got + [early_y, keep_a, send_a, late])
+        {9: 0},
+    )
+    *got, keep_a, send_a, late = after(got + [keep_a, send_a, late])
+    early_g = jnp.concatenate(ordered([v[3 * half :] for v in got], z_at), axis=0)
     piece_f = tree_sum([v[: 2 * half] for v in got]).astype(BF16)
     out_f = tree_sum([v[2 * half : 3 * half] for v in got]).astype(BF16)
 
-    n_l = late.shape[0]
-    parts_a = chip_sum(keep_a, send_a)
-    late_z = over_z(late, [late] * (n_z - 1))
-    first_f = swap(piece_f, 0, 2)
-    *phase, early_g, first_f = after(parts_a + late_z + [early_g, first_f])
-    parts_a, late_z = phase[:4], phase[4:]
-
-    late_g = jnp.concatenate(ordered(late_z, z_at), axis=0)
-    wide_rows = lambda v: jnp.concatenate(
-        [v[:, i * width : (i + 1) * width] for i in range(3)], axis=0
-    )
-    loads = [jnp.concatenate([wide_rows(v), late_g], axis=0) for v in parts_a]
+    n_l, n_e = late.shape[0], early.shape[0]
+    got_a = swap(send_a, 1)
+    both = jnp.concatenate([late, piece_f], axis=0)
+    late_z = [late, swap(both, 0, 2)] + [swap(late, 0, 2 * k) for k in range(2, n_z)]
+    early_x = pair(early_g, 0, 1, x_at == 1)
+    got_a, *late_z, early_g = after([got_a] + late_z + [early_x])
+    first_f = late_z[1][n_l:]
+
+    ins = (keep_a, got_a) + tuple(late_z)
+    outs = [jax.ShapeDtypeStruct((3 * half + n_z * n_l, width), BF16)] * 4
+    loads = call(join, info, ins, whole(ins), outs, whole(outs), [], (1,), 16, 0, 1 << 20)
     got = over_plane(loads[0], loads[1:])
     two_f = jnp.concatenate([piece_f, first_f], axis=0)
     rest_f = swap(two_f, 0, 4)
-    early_c = pair(early_g, 1, 0, (s & 1) == 1)
-    *got, two_f, rest_f, early_g = after(got + [two_f, rest_f, early_c])
+    early_g = pair(early_g, 1, 0, (s & 1) == 1)
+
+    contract = lambda a, b: lax.dot_general(
+        a, b, (((0,), (0,)), ((), ())), preferred_element_type=F32
+    )
+    early_r = early_g.reshape(2, 2, n_z, 2, n_e // 8, 8, width)
+    to_rows = lambda v, i: v[..., i, :, :].reshape(-1, width)
+    cs_all = lax.dynamic_slice_in_dim(to_rows(early_r, 4), s * quarter, quarter, 1)
+    d_early = jnp.concatenate([to_rows(early_r, i) for i in range(4)], axis=1)
+    few = jnp.sum(early_r[..., 5, :, :].astype(F32), axis=(0, 1, 2, 3))
+    w_early, sum_early = contract(cs_all, d_early), jnp.sum(d_early.astype(F32), axis=0)
+    group_r = lax.dynamic_index_in_dim(early_r, z_at, 2, keepdims=False)
+    group_r = lax.dynamic_index_in_dim(group_r, x_at, 1, keepdims=False)
+    near_d = [
+        group_r[:, :, i].transpose(1, 0, 2, 3).reshape(4 * count, width) for i in range(4)
+    ]
+    *got, two_f, rest_f, w_early, sum_early, few = after(
+        got + [two_f, rest_f, w_early, sum_early, few]
+    )
 
     total_a = tree_sum([v[: 3 * half] for v in got]).astype(BF16)
     late_g = jnp.concatenate(ordered([v[3 * half :] for v in got], 2 * y_at + x_at), axis=0)
@@ -708,6 +761,46 @@
     yours_f = swap(mine_f, 0, 1)
     late_g = pair(late_g, 1, 0, (s & 1) == 1)
 
+    def mine(row):
+        part = row.shape[0] // shards
+        return lax.dynamic_slice(row, (s * part,), (part,))
+
+    late_r = late_g.reshape(2, 2, 2, n_z, n_l // 8, 8, width)
+    d_late = jnp.concatenate([to_rows(late_r, i) for i in range(2)], axis=1)
+    cs_all = lax.dynamic_slice_in_dim(to_rows(late_r, 3), s * quarter, quarter, 1)
+    w_late, sum_late = contract(cs_all, d_late), jnp.sum(d_late.astype(F32), axis=0)
+    gb_late = mine(jnp.sum(late_r[..., 2, :2, :].astype(F32), axis=(0, 1, 2, 3)).reshape(-1))
+    side_r = lax.dynamic_index_in_dim(late_r, x_at, 2, keepdims=False)
+    side_r = lax.dynamic_index_in_dim(side_r, z_at, 2, keepdims=False)
+    late_d = [side_r[:, :, i].transpose(1, 0, 2, 3).reshape(4 * 8, width) for i in range(2)]
+    ins = (w_late, sum_late.reshape(1, -1), w_early, sum_early.reshape(1, -1), few)
+    outs = [
+        jax.ShapeDtypeStruct(shape, F32)
+        for shape in (
+            (quarter, 6 * width),
+            (6 * width // 4,),
+            (quarter,),
+            (hidden // 4,),
+            (quarter,),
+        )
+    ]
+    gw_ada, gb_ada, gb_o, gb_1, gb_2 = call(
+        finish,
+        info,
+        ins,
+        whole(ins),
+        outs,
+        whole(outs),
+        [pltpu.VMEM((8, 6 * width), F32)],
+        (1,),
+        16,
+        0,
+        1 << 20,
+    )
+    grads_b = [gb_ada, gb_late, gb_o, gb_1, gb_2]
+    dada = jnp.concatenate(late_d + near_d, axis=1)
+    dcs = lax.dot_general(dada, w_ada, (((1,), (1,)), ((), ())), preferred_element_type=F32)
+    yours_f, gw_ada, gb_late, dcs = after((yours_f, gw_ada, gb_late, dcs))
     sides = by_x(mine_f, yours_f)
     deep = [side[: 8 * half].reshape(4, 2 * half, width) for side in sides]
     gw_1 = jnp.concatenate(
@@ -717,43 +810,16 @@
         [side[:, half:].reshape(4 * half, width) for side in deep], axis=0
     ).T.astype(F32)
     gw_o = jnp.concatenate([side[8 * half :] for side in sides], axis=0).astype(F32)
-
-    early_r = early_g.reshape(2, 2, 2, n_z, n_e // 8, 8, width).transpose(0, 2, 1, 3, 4, 5, 6)
-    late_r = late_g.reshape(2, 2, 2, n_z, n_l // 8, 8, width)
-    to_rows = lambda v, i: v[:, :, :, :, i].reshape(-1, width)
-    cs_all = lax.dynamic_slice_in_dim(to_rows(early_r, 4), s * quarter, quarter, 1)
-    d_late = jnp.concatenate([to_rows(late_r, i) for i in range(2)], axis=1)
-    d_early = jnp.concatenate([to_rows(early_r, i) for i in range(4)], axis=1)
-    contract = lambda v: lax.dot_general(
-        cs_all, v, (((0,), (0,)), ((), ())), preferred_element_type=F32
-    )
-    gw_ada = jnp.concatenate([contract(d_late), contract(d_early)], axis=1)
-    gb_ada = jnp.concatenate(
-        [jnp.sum(d_late.astype(F32), axis=0), jnp.sum(d_early.astype(F32), axis=0)]
-    )
-    gb_early = jnp.sum(early_r[:, :, :, :, 5].astype(F32), axis=(0, 1, 2, 3))
-    gb_late = jnp.sum(late_r[:, :, :, :, 2, :2].astype(F32), axis=(0, 1, 2, 3)).reshape(-1)
-
-    def group(v, parts):
-        v = lax.dynamic_index_in_dim(v, z_at, 3, keepdims=False)
-        v = lax.dynamic_index_in_dim(v, x_at, 2, keepdims=False)
-        return [v[:, :, i].transpose(1, 0, 2, 3).reshape(4 * 8, width) for i in range(parts)]
-
-    dada = jnp.concatenate(group(late_r, 2) + group(early_r, 4), axis=1)
-    dcs = lax.dot_general(dada, w_ada, (((1,), (1,)), ((), ())), preferred_element_type=F32)
-    *ring_a, gw_1, gw_2, gw_o, gw_ada, dcs = after(ring_a + [gw_1, gw_2, gw_o, gw_ada, dcs])
+    *ring_a, gw_1, gw_2, gw_o = after(ring_a + [gw_1, gw_2, gw_o])
     mine_a = tree_sum(ring_a).astype(BF16)
     yours_a = swap(mine_a, 0, 1)
+    dcs = after(dcs, mine_a)
     dcs = ordered([dcs[k * 8 : (k + 1) * 8] for k in range(4)], s)
     dcs = ordered([dcs[0]] + [swap(dcs[k], k) for k in range(1, 4)], s)
     c32 = cond.astype(F32)
     sig = 1.0 / (1.0 + jnp.exp(-c32))
     grad_cond = jnp.concatenate(dcs, axis=1) * (sig * (1.0 + c32 * (1.0 - sig)))
 
-    def mine(row):
-        part = row.shape[0] // shards
-        return lax.dynamic_slice(row, (s * part,), (part,))
-
     tall = jnp.concatenate(
         [v.reshape(3, half, width).transpose(1, 0, 2).reshape(half, 3 * width) for v in by_x(mine_a, yours_a)],
         axis=0,
@@ -765,15 +831,15 @@
         grad_tokens,
         grad_cond,
         gw_ada,
-        mine(gb_ada),
+        grads_b[0],
         gw_qkv,
-        mine(gb_late),
+        grads_b[1],
         gw_o,
-        mine(gb_early[hidden // width]),
+        grads_b[2],
         gw_1,
-        mine(gb_early[: hidden // width].reshape(-1)),
+        grads_b[3],
         gw_2,
-        mine(gb_early[hidden // width + 1]),
+        grads_b[4],
     )
 
 

time: 172 us -> 166 us (0.965)
  local copies, waits for them, and re-layouts: 7.93 us -> 3.35 us
  other arithmetic: 9.97 us -> 7.98 us
    unnamed x58 -> x50, local copies, waits for them, and re-layouts: 4.61 us -> 2.05 us
    dynamic_slice x4 -> x1, local copies, waits for them, and re-layouts: 2.49 us -> 0.64 us  [mine(): return lax.dynamic_slice(row, (s * part,), (part,))]
    ppermute x43 -> x42, starting transfers between devices: 39.4 us -> 40.6 us  [swap(): return lax.ppermute(v, ('rep', 'shard'), pairs)]
    ppermute x43 -> x42, waiting for transfers between devices: 34 us -> 33.4 us  [swap(): return lax.ppermute(v, ('rep', 'shard'), pairs)]
    pallas_call x6 -> x8, Pallas kernels: 77.6 us -> 77.8 us  [call(): pl.pallas_call(body, out_shape=outs, input_output_aliases=alias or {}, gr...]
  transfers between devices with their start and end apart: 43 -> 42, of which waited for: 16 -> 13; matrix products, arithmetic and copies ran while one was open for 8% -> 5% of each run, Pallas kernels for 25% -> 28%
where the time goes in v4:
time: 166 us; the launch traced here: 165 us
  Pallas kernels  77.8 us (47%)
  starting transfers between devices  40.6 us (24%)
  waiting for transfers between devices  33.4 us (20%)
  other arithmetic  7.98 us (5%)
  local copies, waits for them, and re-layouts  3.35 us (2%)
    pallas_call x8, Pallas kernels, call(): pl.pallas_call(body, out_shape=outs, input_output_aliases=alias or {}, gr...  77.8 us
    ppermute x42, starting transfers between devices, swap(): return lax.ppermute(v, ('rep', 'shard'), pairs)  40.6 us
    ppermute x42, waiting for transfers between devices, swap(): return lax.ppermute(v, ('rep', 'shard'), pairs)  33.4 us
  transfers between devices with their start and end apart: 42, of which 13 were waited for; matrix products, arithmetic and copies ran while one was open for 5% of the time, Pallas kernels for 28%

profile of v4, /device:TPU:0, one launch (start us, length us, event | category | flops | bytes accessed | tf_op | source)
XLA Modules:
  0.0 165.4 jit_solution(11821817849053012050)
XLA Ops:
  1.2 2.6 %collective-permute-start.1 = (bf16[8,384]{1,0:T(8,128)(2,1)}, bf16[8,384]{1,0:T(8,128)(2,1)S(1)}, u32[]{:S(2)}, u32[]{:S(2)}) collective-permute-start(bf16[8,384]{1,0:T(8,128)(2,1)} %cond.1), channel_id=1, source_target_pairs={{0,2},{1,3},{2,0},{3,1},{4,6},{5,7},{6,4},{7,5},{8,10},{9,11},{10,... | collective-permute-start | bytes 18440 | tf_op jit(solution)/shard_map/ppermute | solution.py:499
  4.4 2.7 %shard_map.228.refs_4_ = bf16[864,384]{1,0:T(8,128)(2,1)} custom-call(s32[4]{0:T(128)} %pad_add_fusion.info, bf16[96,384]{1,0:T(8,128)(2,1)} %w_o.1, bf16[96,1536]{1,0:T(8,128)(2,1)} %w_1.1, bf16[384,384]{1,0:T(8,128)(2,1)} %w_2.1), custom_call_target="tpu_custom_call" | custom-call | bytes 1048576 | tf_op jit(solution)/shard_map/pallas_call | solution.py:461
  7.1 1.8 %collective-permute-start.7 = (bf16[96,1152]{1,0:T(8,128)(2,1)}, bf16[96,1152]{1,0:T(8,128)(2,1)S(1)}, u32[]{:S(2)}, u32[]{:S(2)}) collective-permute-start(bf16[96,1152]{1,0:T(8,128)(2,1)} %refs_4_.1), channel_id=1, source_target_pairs={{0,2},{1,3},{2,0},{3,1},{4,6},{5,7},{6,4},{7,5},{8,10},{9,11},{10,... | collective-permute-start | bytes 663560 | tf_op jit(solution)/shard_map/ppermute | solution.py:499
  8.9 2.8 %shard_map.229 = (f32[8,1152]{1,0:T(8,128)}, f32[8,1152]{1,0:T(8,128)}, f32[8,1152]{1,0:T(8,128)}, f32[8,1152]{1,0:T(8,128)}, f32[8,1536]{1,0:T(8,128)}, /*index...) custom-call(s32[4]{0:T(128)} %pad_add_fusion.info, bf16[8,384]{1,0:T(8,128)(2,1)} %cond.1, ...), custom_call_target="tpu_custom_call" | custom-call | flops 16777216 | bytes 1048576 | tf_op jit(solution)/shard_map/pallas_call | solution.py:461
  13.7 2.7 %collective-permute-done.4.refs_2_ = f32[8,1152]{1,0:T(8,128)S(1)} collective-permute-done((f32[8,1152]{1,0:T(8,128)}, f32[8,1152]{1,0:T(8,128)S(1)}, u32[]{:S(2)}, u32[]{:S(2)}) %collective-permute-start.4) | collective-permute-done | bytes 36896 | tf_op jit(solution)/shard_map/ppermute | solution.py:499
  21.1 14.0 %shard_map.230 = (bf16[8,256,384]{2,1,0:T(8,128)(2,1)}, bf16[8,256,1152]{2,1,0:T(8,128)(2,1)}, bf16[8,6,256,256]{3,2,1,0:T(8,128)(2,1)}, bf16[8,256,384]{2,1,0:T...) custom-call(s32[4]{0:T(128)} %pad_add_fusion.info, bf16[8,256,384]{2,1,0:T(8,128)(2,1)} %tok.7, ...), custom_call_target="tpu_custom_call" | custom-call | flops 4026531840 | bytes 15728640 | tf_op jit(solution)/shard_map/pallas_call | solution.py:461
  35.9 1.8 %collective-permute-done.14.refs_7_ = bf16[864,384]{1,0:T(8,128)(2,1)S(1)} collective-permute-done((bf16[864,384]{1,0:T(8,128)(2,1)S(1)}, bf16[864,384]{1,0:T(8,128)(2,1)S(1)}, u32[]{:S(2)}, u32[]{:S(2)}) %collective-permute-start.14) | collective-permute-done | bytes 663584 | tf_op jit(solution)/shard_map/ppermute | solution.py:499
  38.5 32.1 %shard_map.231 = (bf16[8,256,384]{2,1,0:T(8,128)(2,1)}, f32[8,256,384]{2,1,0:T(8,128)}, bf16[8,256,384]{2,1,0:T(8,128)(2,1)}, bf16[48,384]{1,0:T(8,128)(2,1)}, b...) custom-call(s32[4]{0:T(128)} %pad_add_fusion.info, bf16[8,256,384]{2,1,0:T(8,128)(2,1)} %tok.7, ...), custom_call_target="tpu_custom_call" | custom-call | flops 16307453952 | bytes 11010048 | tf_op jit(solution)/shard_map/pallas_call | solution.py:461
  72.4 2.8 %collective-permute-done.19 = bf16[48,384]{1,0:T(8,128)(2,1)S(1)} collective-permute-done((bf16[48,384]{1,0:T(8,128)(2,1)}, bf16[48,384]{1,0:T(8,128)(2,1)S(1)}, u32[]{:S(2)}, u32[]{:S(2)}) %collective-permute-start.19) | collective-permute-done | bytes 36896 | tf_op jit(solution)/shard_map/ppermute | solution.py:499
  76.0 1.6 fusion.3
  77.6 1.6 collective-permute-start.16
  81.2 11.8 %shard_map.232 = (f32[8,256,384]{2,1,0:T(8,128)}, f32[384,1152]{1,0:T(8,128)}, f32[8,768]{1,0:T(8,128)}, f32[8,384]{1,0:T(8,128)}) custom-call(s32[4]{0:T(128)} %pad_add_fusion.info, bf16[8,256,384]{2,1,0:T(8,128)(2,1)} %tok.7, bf16[8,256,384]{2,1,0:T(8,128)(2,1)} %get-tuple-element.140.m1_i, bf16[8,256,1152]{2,1,0:T(8,128)(2,1)} %get-tuple-element.141.qkv_i, ...), custom_call_target="tpu_custom_call" | custom-call | flops 2818572288 | bytes 11796480 | tf_op jit(solution)/shard_map/pallas_call | solution.py:461
  92.9 1.8 %collective-permute-done.17 = bf16[432,384]{1,0:T(8,128)(2,1)S(1)} collective-permute-done((bf16[432,384]{1,0:T(8,128)(2,1)S(1)}, bf16[432,384]{1,0:T(8,128)(2,1)S(1)}, u32[]{:S(2)}, u32[]{:S(2)}) %collective-permute-start.17) | collective-permute-done | bytes 331808 | tf_op jit(solution)/shard_map/ppermute | solution.py:499
  95.1 1.6 collective-permute-start.20
  96.7 2.6 %collective-permute-start.21 = (bf16[240,384]{1,0:T(8,128)(2,1)S(1)}, bf16[240,384]{1,0:T(8,128)(2,1)S(1)}, u32[]{:S(2)}, u32[]{:S(2)}) collective-permute-start(bf16[240,384]{1,0:T(8,128)(2,1)S(1)} %get-tuple-element.276), channel_id=1, source_target_pairs={{0,16},{1,17},{2,18},{3,19},{4,20},{5,21},{6,22},{7,23},{8,24},{9,... | collective-permute-start | bytes 552968 | tf_op jit(solution)/shard_map/ppermute | solution.py:499
  99.5 12.2 %shard_map.233 = (f32[8,256,384]{2,1,0:T(8,128)}, bf16[32,384]{1,0:T(8,128)(2,1)}, bf16[2,2,48,1152]{3,2,1,0:T(8,128)(2,1)}, bf16[2,2,48,1152]{3,2,1,0:T(8,128)(2,1)}) custom-call(s32[4]{0:T(128)} %pad_add_fusion.info, bf16[8,256,384]{2,1,0:T(8,128)(2,1)} %tok.7, bf16[8,256,384]{2,1,0:T(8,128)(2,1)} %get-tuple-element.140.m1_i, ...), custom_call_target="tpu_custom_call", output_to_operand_aliasing={{0}: (9, {})} | custom-call | flops 2818572288 | bytes 11796480 | tf_op jit(solution)/shard_map/pallas_call | solution.py:461
  111.8 3.4 %collective-permute-start.25 = (bf16[32,384]{1,0:T(8,128)(2,1)}, bf16[32,384]{1,0:T(8,128)(2,1)S(1)}, u32[]{:S(2)}, u32[]{:S(2)}) collective-permute-start(bf16[32,384]{1,0:T(8,128)(2,1)} %get-tuple-element.169.refs_0_), channel_id=1, source_target_pairs={{0,16},{1,17},{2,18},{3,19},{4,20},{5,21},{6,22},{7,23},{8,24},{9,... | collective-permute-start | bytes 73736 | tf_op jit(solution)/shard_map/ppermute | solution.py:499
  116.6 1.5 collective-permute-start.27
  118.2 7.9 %collective-permute-done.27 = bf16[384,384]{1,0:T(8,128)(2,1)S(1)} collective-permute-done((bf16[384,384]{1,0:T(8,128)(2,1)S(1)}, bf16[384,384]{1,0:T(8,128)(2,1)S(1)}, u32[]{:S(2)}, u32[]{:S(2)}) %collective-permute-start.27) | collective-permute-done | bytes 294944 | tf_op jit(solution)/shard_map/ppermute | solution.py:499
  132.7 7.3 %collective-permute-done.31 = bf16[192,384]{1,0:T(8,128)(2,1)S(1)} collective-permute-done((bf16[192,384]{1,0:T(8,128)(2,1)S(1)}, bf16[192,384]{1,0:T(8,128)(2,1)S(1)}, u32[]{:S(2)}, u32[]{:S(2)}) %collective-permute-start.31) | collective-permute-done | bytes 147488 | tf_op jit(solution)/shard_map/ppermute | solution.py:499
  140.5 3.1 %collective-permute-start.36 = (bf16[144,384]{1,0:T(8,128)(2,1)S(1)}, bf16[144,384]{1,0:T(8,128)(2,1)S(1)}, u32[]{:S(2)}, u32[]{:S(2)}) collective-permute-start(bf16[144,384]{1,0:T(8,128)(2,1)S(1)} %add_convert_fusion.6), channel_id=1, source_target_pairs={{0,16},{1,17},{2,18},{3,19},{4,20},{5,21},{6,22},{7,23},{8,24},{9,... | collective-permute-start | bytes 331784 | tf_op jit(solution)/shard_map/ppermute | solution.py:499
  148.5 1.6 shard_map.235
  150.3 5.3 %collective-permute-done.33 = bf16[432,384]{1,0:T(8,128)(2,1)S(1)} collective-permute-done((bf16[432,384]{1,0:T(8,128)(2,1)S(1)}, bf16[432,384]{1,0:T(8,128)(2,1)S(1)}, u32[]{:S(2)}, u32[]{:S(2)}) %collective-permute-start.33) | collective-permute-done | bytes 331808 | tf_op jit(solution)/shard_map/ppermute | solution.py:499
  162.4 2.0 %collective-permute-done.41 = bf16[144,384]{1,0:T(8,128)(2,1)S(1)} collective-permute-done((bf16[144,384]{1,0:T(8,128)(2,1)S(1)}, bf16[144,384]{1,0:T(8,128)(2,1)S(1)}, u32[]{:S(2)}, u32[]{:S(2)}) %collective-permute-start.41) | collective-permute-done | bytes 110624 | tf_op jit(solution)/shard_map/ppermute | solution.py:499
  (184 shorter events, 35.8 us)
Async XLA Ops:
  7.1 10.9 %collective-permute-start.7 = (bf16[96,1152]{1,0:T(8,128)(2,1)}, bf16[96,1152]{1,0:T(8,128)(2,1)S(1)}, u32[]{:S(2)}, u32[]{:S(2)}) collective-permute-start(bf16[96,1152]{1,0:T(8,128)(2,1)} %refs_4_.1), channel_id=1, source_target_pairs={{0,2},{1,3},{2,0},{3,1},{4,6},{5,7},{6,4},{7,5},{8,10},{9,11},{10,... | collective-permute-start | bytes 663560 | tf_op jit(solution)/shard_map/ppermute | solution.py:499
  16.7 18.7 %collective-permute-start.9 = (bf16[864,384]{1,0:T(8,128)(2,1)}, bf16[864,384]{1,0:T(8,128)(2,1)S(1)}, u32[]{:S(2)}, u32[]{:S(2)}) collective-permute-start(bf16[864,384]{1,0:T(8,128)(2,1)} %shard_map.228.refs_4_), channel_id=1, source_target_pairs={{0,2},{1,3},{2,0},{3,1},{4,6},{5,7},{6,4},{7,5},{8,10},{9,11},{10,... | collective-permute-start | bytes 1990664 | tf_op jit(solution)/shard_map/ppermute | solution.py:499
  18.6 17.3 %collective-permute-start.13 = (bf16[864,384]{1,0:T(8,128)(2,1)}, bf16[864,384]{1,0:T(8,128)(2,1)S(1)}, u32[]{:S(2)}, u32[]{:S(2)}) collective-permute-start(bf16[864,384]{1,0:T(8,128)(2,1)} %shard_map.228.refs_4_), channel_id=1, source_target_pairs={{0,1},{1,0},{2,3},{3,2},{4,5},{5,4},{6,7},{7,6},{8,9},{9,8},{10,11... | collective-permute-start | bytes 1990664 | tf_op jit(solution)/shard_map/ppermute | solution.py:499
  18.6 16.4 %collective-permute-start.10 = (f32[8,1536]{1,0:T(8,128)}, f32[8,1536]{1,0:T(8,128)S(1)}, u32[]{:S(2)}, u32[]{:S(2)}) collective-permute-start(f32[8,1536]{1,0:T(8,128)} %get-tuple-element.127), channel_id=1, source_target_pairs={{0,1},{1,0},{2,3},{3,2},{4,5},{5,4},{6,7},{7,6},{8,9},{9,8},{10,11... | collective-permute-start | bytes 147464 | tf_op jit(solution)/shard_map/ppermute | solution.py:499
  19.5 15.9 %collective-permute-start.11 = (f32[8,1536]{1,0:T(8,128)}, f32[8,1536]{1,0:T(8,128)S(1)}, u32[]{:S(2)}, u32[]{:S(2)}) collective-permute-start(f32[8,1536]{1,0:T(8,128)} %get-tuple-element.128), channel_id=1, source_target_pairs={{0,2},{1,3},{2,0},{3,1},{4,6},{5,7},{6,4},{7,5},{8,10},{9,11},{10,... | collective-permute-start | bytes 147464 | tf_op jit(solution)/shard_map/ppermute | solution.py:499
  20.2 15.2 %collective-permute-start.12 = (f32[8,1536]{1,0:T(8,128)}, f32[8,1536]{1,0:T(8,128)S(1)}, u32[]{:S(2)}, u32[]{:S(2)}) collective-permute-start(f32[8,1536]{1,0:T(8,128)} %get-tuple-element.129), channel_id=1, source_target_pairs={{0,3},{1,2},{2,1},{3,0},{4,7},{5,6},{6,5},{7,4},{8,11},{9,10},{10,... | collective-permute-start | bytes 147464 | tf_op jit(solution)/shard_map/ppermute | solution.py:499
  77.6 15.3 %collective-permute-start.16 = (bf16[432,384]{1,0:T(8,128)(2,1)S(1)}, bf16[432,384]{1,0:T(8,128)(2,1)S(1)}, u32[]{:S(2)}, u32[]{:S(2)}) collective-permute-start(bf16[432,384]{1,0:T(8,128)(2,1)S(1)} %get-tuple-element.234), channel_id=1, source_target_pairs={{0,4},{1,5},{2,6},{3,7},{4,0},{5,1},{6,2},{7,3},{8,12},{9,13},{10,... | collective-permute-start | bytes 995336 | tf_op jit(solution)/shard_map/ppermute | solution.py:499
  79.2 15.6 %collective-permute-start.17 = (bf16[432,384]{1,0:T(8,128)(2,1)S(1)}, bf16[432,384]{1,0:T(8,128)(2,1)S(1)}, u32[]{:S(2)}, u32[]{:S(2)}) collective-permute-start(bf16[432,384]{1,0:T(8,128)(2,1)S(1)} %get-tuple-element.233), channel_id=1, source_target_pairs={{0,2},{1,3},{2,0},{3,1},{4,6},{5,7},{6,4},{7,5},{8,10},{9,11},{10,... | collective-permute-start | bytes 995336 | tf_op jit(solution)/shard_map/ppermute | solution.py:499
  80.6 14.2 %collective-permute-start.18 = (bf16[432,384]{1,0:T(8,128)(2,1)S(1)}, bf16[432,384]{1,0:T(8,128)(2,1)S(1)}, u32[]{:S(2)}, u32[]{:S(2)}) collective-permute-start(bf16[432,384]{1,0:T(8,128)(2,1)S(1)} %get-tuple-element.232), channel_id=1, source_target_pairs={{0,6},{1,7},{2,4},{3,5},{4,2},{5,3},{6,0},{7,1},{8,14},{9,15},{10,... | collective-permute-start | bytes 995336 | tf_op jit(solution)/shard_map/ppermute | solution.py:499
  95.1 16.7 %collective-permute-start.20 = (bf16[240,384]{1,0:T(8,128)(2,1)S(1)}, bf16[240,384]{1,0:T(8,128)(2,1)S(1)}, u32[]{:S(2)}, u32[]{:S(2)}) collective-permute-start(bf16[240,384]{1,0:T(8,128)(2,1)S(1)} %get-tuple-element.275), channel_id=1, source_target_pairs={{0,8},{1,9},{2,10},{3,11},{4,12},{5,13},{6,14},{7,15},{8,0},{9,1},... | collective-permute-start | bytes 552968 | tf_op jit(solution)/shard_map/ppermute | solution.py:499
  96.7 15.0 %collective-permute-start.21 = (bf16[240,384]{1,0:T(8,128)(2,1)S(1)}, bf16[240,384]{1,0:T(8,128)(2,1)S(1)}, u32[]{:S(2)}, u32[]{:S(2)}) collective-permute-start(bf16[240,384]{1,0:T(8,128)(2,1)S(1)} %get-tuple-element.276), channel_id=1, source_target_pairs={{0,16},{1,17},{2,18},{3,19},{4,20},{5,21},{6,22},{7,23},{8,24},{9,... | collective-permute-start | bytes 552968 | tf_op jit(solution)/shard_map/ppermute | solution.py:499
  99.3 12.5 %collective-permute-start.22 = (bf16[240,384]{1,0:T(8,128)(2,1)S(1)}, bf16[240,384]{1,0:T(8,128)(2,1)S(1)}, u32[]{:S(2)}, u32[]{:S(2)}) collective-permute-start(bf16[240,384]{1,0:T(8,128)(2,1)S(1)} %get-tuple-element.274), channel_id=1, source_target_pairs={{0,24},{1,25},{2,26},{3,27},{4,28},{5,29},{6,30},{7,31},{8,16},{9,... | collective-permute-start | bytes 552968 | tf_op jit(solution)/shard_map/ppermute | solution.py:499
  111.8 14.5 %collective-permute-start.25 = (bf16[32,384]{1,0:T(8,128)(2,1)}, bf16[32,384]{1,0:T(8,128)(2,1)S(1)}, u32[]{:S(2)}, u32[]{:S(2)}) collective-permute-start(bf16[32,384]{1,0:T(8,128)(2,1)} %get-tuple-element.169.refs_0_), channel_id=1, source_target_pairs={{0,16},{1,17},{2,18},{3,19},{4,20},{5,21},{6,22},{7,23},{8,24},{9,... | collective-permute-start | bytes 73736 | tf_op jit(solution)/shard_map/ppermute | solution.py:499
  115.1 11.1 %collective-permute-start.26 = (bf16[32,384]{1,0:T(8,128)(2,1)}, bf16[32,384]{1,0:T(8,128)(2,1)S(1)}, u32[]{:S(2)}, u32[]{:S(2)}) collective-permute-start(bf16[32,384]{1,0:T(8,128)(2,1)} %get-tuple-element.169.refs_0_), channel_id=1, source_target_pairs={{0,24},{1,25},{2,26},{3,27},{4,28},{5,29},{6,30},{7,31},{8,16},{9,... | collective-permute-start | bytes 73736 | tf_op jit(solution)/shard_map/ppermute | solution.py:499
  116.5 9.8 %collective-permute-start.23 = (bf16[2,2,48,1152]{3,2,1,0:T(8,128)(2,1)}, bf16[2,2,48,1152]{3,2,1,0:T(8,128)(2,1)S(1)}, u32[]{:S(2)}, u32[]{:S(2)}) collective-permute-start(bf16[2,2,48,1152]{3,2,1,0:T(8,128)(2,1)} %get-tuple-element.162), channel_id=1, source_target_pairs={{0,1},{1,0},{2,3},{3,2},{4,5},{5,4},{6,7},{7,6},{8,9},{9,8},{10,11... | collective-permute-start | bytes 1327112 | tf_op jit(solution)/shard_map/ppermute | solution.py:499
  116.6 9.5 %collective-permute-start.27 = (bf16[384,384]{1,0:T(8,128)(2,1)S(1)}, bf16[384,384]{1,0:T(8,128)(2,1)S(1)}, u32[]{:S(2)}, u32[]{:S(2)}) collective-permute-start(bf16[384,384]{1,0:T(8,128)(2,1)S(1)} %pad_maximum_fusion.10), channel_id=1, source_target_pairs={{0,4},{1,5},{2,6},{3,7},{4,0},{5,1},{6,2},{7,3},{8,12},{9,13},{10,... | collective-permute-start | bytes 884744 | tf_op jit(solution)/shard_map/ppermute | solution.py:499
  127.1 12.9 %collective-permute-start.28 = (bf16[272,384]{1,0:T(8,128)(2,1)S(1)}, bf16[272,384]{1,0:T(8,128)(2,1)S(1)}, u32[]{:S(2)}, u32[]{:S(2)}) collective-permute-start(bf16[272,384]{1,0:T(8,128)(2,1)S(1)} %get-tuple-element.174), channel_id=1, source_target_pairs={{0,4},{1,5},{2,6},{3,7},{4,0},{5,1},{6,2},{7,3},{8,12},{9,13},{10,... | collective-permute-start | bytes 626696 | tf_op jit(solution)/shard_map/ppermute | solution.py:499
  128.6 11.7 %collective-permute-start.29 = (bf16[272,384]{1,0:T(8,128)(2,1)S(1)}, bf16[272,384]{1,0:T(8,128)(2,1)S(1)}, u32[]{:S(2)}, u32[]{:S(2)}) collective-permute-start(bf16[272,384]{1,0:T(8,128)(2,1)S(1)} %get-tuple-element.175), channel_id=1, source_target_pairs={{0,2},{1,3},{2,0},{3,1},{4,6},{5,7},{6,4},{7,5},{8,10},{9,11},{10,... | collective-permute-start | bytes 626696 | tf_op jit(solution)/shard_map/ppermute | solution.py:499
  129.3 11.1 %collective-permute-start.30 = (bf16[272,384]{1,0:T(8,128)(2,1)S(1)}, bf16[272,384]{1,0:T(8,128)(2,1)S(1)}, u32[]{:S(2)}, u32[]{:S(2)}) collective-permute-start(bf16[272,384]{1,0:T(8,128)(2,1)S(1)} %get-tuple-element.176), channel_id=1, source_target_pairs={{0,6},{1,7},{2,4},{3,5},{4,2},{5,3},{6,0},{7,1},{8,14},{9,15},{10,... | collective-permute-start | bytes 626696 | tf_op jit(solution)/shard_map/ppermute | solution.py:499
  130.7 9.3 %collective-permute-start.31 = (bf16[192,384]{1,0:T(8,128)(2,1)S(1)}, bf16[192,384]{1,0:T(8,128)(2,1)S(1)}, u32[]{:S(2)}, u32[]{:S(2)}) collective-permute-start(bf16[192,384]{1,0:T(8,128)(2,1)S(1)} %pad_maximum_fusion.16), channel_id=1, source_target_pairs={{0,16},{1,17},{2,18},{3,19},{4,20},{5,21},{6,22},{7,23},{8,24},{9,... | collective-permute-start | bytes 442376 | tf_op jit(solution)/shard_map/ppermute | solution.py:499
  140.4 17.1 %collective-permute-start.35 = (bf16[144,384]{1,0:T(8,128)(2,1)S(1)}, bf16[144,384]{1,0:T(8,128)(2,1)S(1)}, u32[]{:S(2)}, u32[]{:S(2)}) collective-permute-start(bf16[144,384]{1,0:T(8,128)(2,1)S(1)} %add_convert_fusion.6), channel_id=1, source_target_pairs={{0,8},{1,9},{2,10},{3,11},{4,12},{5,13},{6,14},{7,15},{8,0},{9,1},... | collective-permute-start | bytes 331784 | tf_op jit(solution)/shard_map/ppermute | solution.py:499
  140.5 17.0 %collective-permute-start.36 = (bf16[144,384]{1,0:T(8,128)(2,1)S(1)}, bf16[144,384]{1,0:T(8,128)(2,1)S(1)}, u32[]{:S(2)}, u32[]{:S(2)}) collective-permute-start(bf16[144,384]{1,0:T(8,128)(2,1)S(1)} %add_convert_fusion.6), channel_id=1, source_target_pairs={{0,16},{1,17},{2,18},{3,19},{4,20},{5,21},{6,22},{7,23},{8,24},{9,... | collective-permute-start | bytes 331784 | tf_op jit(solution)/shard_map/ppermute | solution.py:499
  143.5 13.9 %collective-permute-start.37 = (bf16[144,384]{1,0:T(8,128)(2,1)S(1)}, bf16[144,384]{1,0:T(8,128)(2,1)S(1)}, u32[]{:S(2)}, u32[]{:S(2)}) collective-permute-start(bf16[144,384]{1,0:T(8,128)(2,1)S(1)} %add_convert_fusion.6), channel_id=1, source_target_pairs={{0,24},{1,25},{2,26},{3,27},{4,28},{5,29},{6,30},{7,31},{8,16},{9,... | collective-permute-start | bytes 331784 | tf_op jit(solution)/shard_map/ppermute | solution.py:499
  145.3 10.3 %collective-permute-start.33 = (bf16[432,384]{1,0:T(8,128)(2,1)S(1)}, bf16[432,384]{1,0:T(8,128)(2,1)S(1)}, u32[]{:S(2)}, u32[]{:S(2)}) collective-permute-start(bf16[432,384]{1,0:T(8,128)(2,1)S(1)} %fusion.8), channel_id=1, source_target_pairs={{0,4},{1,5},{2,6},{3,7},{4,0},{5,1},{6,2},{7,3},{8,12},{9,13},{10,... | collective-permute-start | bytes 995336 | tf_op jit(solution)/shard_map/ppermute | solution.py:499
  (39 other events, 163.0 us)

commit v5 on v4

--- a/solution.py
+++ b/solution.py
@@ -172,8 +172,8 @@
 
 def ffn_both(info, tok, att_i, dy_i, cond, table, *refs, per, chunk):
     ada_parts, pieces = refs[0:4], refs[4:8]
-    out_o, dx1_o, datt_o, early_o, keep_o, send_o = refs[8:14]
-    wo_s, w1_s, w2_s, go_s, g1_s, g2_s, small_s, gb_s, bo_s, b1_s, b2_s, ada, sems = refs[14:]
+    out_o, dx1_o, datt_o, early_o, cs_o, keep_o, send_o = refs[8:15]
+    wo_s, w1_s, w2_s, go_s, g1_s, g2_s, small_s, gb_s, bo_s, b1_s, b2_s, ada, sems = refs[15:]
     step = pl.program_id(0)
     length, width = tok.shape[1:]
     hidden = w1_s.shape[1]
@@ -205,7 +205,7 @@
         b1_s[...] = bias_row(table, 2, hidden // 4)
         b2_s[...] = bias_row(table, 3, width // 4)
         c = cond[...].astype(F32)
-        small_s[:, 4 * width : 5 * width] = c / (1.0 + jnp.exp(-c))
+        cs_o[...] = (c / (1.0 + jnp.exp(-c))).astype(BF16)
         for copy in copies:
             copy.wait()
 
@@ -272,12 +272,12 @@
 
     @pl.when(step == pl.num_programs(0) - 1)
     def _():
-        for i in range(5):
+        for i in range(4):
             early_o[8 * i : 8 * i + 8, :] = small_s[:, i * width : (i + 1) * width].astype(BF16)
         pack = [gb_s[0:1, i * width : (i + 1) * width] for i in range(hidden // width)]
         pack += [gb_s[1:2, 0:width], gb_s[1:2, width : 2 * width]]
         pack += [jnp.zeros((1, width), F32)] * (8 - len(pack))
-        early_o[40:48, :] = jnp.concatenate(pack, axis=0).astype(BF16)
+        early_o[32:40, :] = jnp.concatenate(pack, axis=0).astype(BF16)
         core = jnp.bitwise_and(info[0], 1)
         half = width // 8
         for y in range(2):
@@ -300,7 +300,7 @@
     step = pl.program_id(0)
     length, width = tok.shape[1:]
     if last:
-        _, g_i, small_i, gb_i, early = refs[0:5]
+        _, g_i, small_i, gb_i, cs = refs[0:5]
         gtok_o, late_o, keep_o, send_o = refs[5:9]
         g_s, small_s, gb_s = refs[9:]
     else:
@@ -384,7 +384,7 @@
             for i in range(2):
                 late_o[8 * i : 8 * i + 8, :] = small_s[:, i * width : (i + 1) * width].astype(BF16)
             late_o[16:24, :] = gb_s[...].astype(BF16)
-            late_o[24:32, :] = early[32:40, :]
+            late_o[24:32, :] = cs[...]
             core = jnp.bitwise_and(info[0], 1)
             half = width // 8
             for y in range(2):
@@ -500,15 +500,6 @@
 
     whole = lambda vs: [full(v.shape) for v in vs]
     conds = [cond] + [swap(cond, k) for k in range(1, 4)]
-    outs = [
-        jax.ShapeDtypeStruct((quarter + quarter * hidden // width + hidden // 4, width), BF16),
-    ]
-    ins = (w_o, w_1, w_2)
-    (ffn_w,) = call(pack, info, ins, whole(ins), outs, whole(outs), [], (1,), 60, 0, 1 << 20)
-    *conds, ffn_w = after(conds + [ffn_w])
-    near_qkv, far_qkv = after((w_qkv, w_qkv), *conds)
-    near_qkv, far_qkv = swap(near_qkv, 1), swap(far_qkv, 2)
-    near_w = swap(ffn_w, 1)
     ins = tuple(conds) + (w_ada, b_ada, b_qv, b_o, b_1, b_2)
     outs = [jax.ShapeDtypeStruct((count, 3 * width), F32)] * 4
     outs += [jax.ShapeDtypeStruct((count, 4 * width), F32)] * 4
@@ -516,7 +507,14 @@
     parts = call(
         ada_parts, info, ins, whole(ins), outs, whole(outs), scratch, (1,), 60, 1 << 24, 1 << 20
     )
+    near_qkv, far_qkv = after((w_qkv, w_qkv), *conds)
+    near_qkv, far_qkv = swap(near_qkv, 1), swap(far_qkv, 2)
     p_qkv = (w_qkv, near_qkv, far_qkv, swap(far_qkv, 1))
+    tall = quarter + quarter * hidden // width + hidden // 4
+    ins = after((w_o, w_1, w_2), parts[0])
+    outs = [jax.ShapeDtypeStruct((tall, width), BF16)]
+    (ffn_w,) = call(pack, info, ins, whole(ins), outs, whole(outs), [], (1,), 60, 0, 1 << 20)
+    near_w = swap(ffn_w, 1)
     parts, later = parts[:4], parts[4:]
     parts = [parts[0]] + [swap(parts[k], k) for k in range(1, 4)]
     *later, ffn_far = after(list(later) + [ffn_w], *parts)
@@ -567,7 +565,7 @@
     per2 = 2 if count % 2 == 0 else 1
     lat2 = lambda *tail: pl.BlockSpec((per2,) + tail, lambda i, _: (i,) + (0,) * len(tail))
     grads = (2, 2, 9 * half, width)
-    block_out, dx1, datt, early, keep_f, send_f = call(
+    block_out, dx1, datt, early, cs_own, keep_f, send_f = call(
         functools.partial(ffn_both, per=per2, chunk=hidden),
         info,
         (latent_tokens, att, grad_out, cond, table) + tuple(later) + p_ffn,
@@ -579,10 +577,11 @@
             jax.ShapeDtypeStruct((count, length, width), BF16),
             jax.ShapeDtypeStruct((count, length, width), F32),
             jax.ShapeDtypeStruct((count, length, width), BF16),
-            jax.ShapeDtypeStruct((48, width), BF16),
+            jax.ShapeDtypeStruct((40, width), BF16),
+            jax.ShapeDtypeStruct((count, width), BF16),
         ]
         + [jax.ShapeDtypeStruct(grads, BF16)] * 2,
-        [lat2(length, width)] * 3 + [full((48, width))] + [full(grads)] * 2,
+        [lat2(length, width)] * 3 + [full((40, width)), full((count, width))] + [full(grads)] * 2,
         [
             pltpu.VMEM((width, width), BF16),
             pltpu.VMEM((width, hidden), BF16),
@@ -590,7 +589,7 @@
             pltpu.VMEM((width, width), F32),
             pltpu.VMEM((width, hidden), F32),
             pltpu.VMEM((width, hidden), F32),
-            pltpu.VMEM((8, 5 * width), F32),
+            pltpu.VMEM((8, 4 * width), F32),
             pltpu.VMEM((8, 5 * width), F32),
             pltpu.VMEM((1, width), F32),
             pltpu.VMEM((1, hidden), F32),
@@ -657,8 +656,11 @@
     def over_plane(own, sends):
         return [own] + [swap(sends[k - 1], 2 * (k >> 1), k & 1) for k in range(1, 4)]
 
+    z_order = sorted(range(1, n_z), key=lambda k: (k & 3) % 3 if k & 3 else 4)
+
     def over_z(own, sends):
-        return [own] + [swap(sends[k - 1], 0, 2 * k) for k in range(1, n_z)]
+        got = {k: swap(sends[k - 1], 0, 2 * k) for k in z_order}
+        return [own] + [got[k] for k in range(1, n_z)]
 
     first = x_at == 0
 
@@ -703,8 +705,8 @@
         count // 2,
         True,
         after(info, *loads),
-        (gtok, g_half, small_half, gb_half, early),
-        [anyspec] + acc_specs + [full(early.shape)],
+        (gtok, g_half, small_half, gb_half, cs_own),
+        [anyspec] + acc_specs + [full(cs_own.shape)],
         [
             jax.ShapeDtypeStruct((32, width), BF16),
             jax.ShapeDtypeStruct(send_shape, BF16),
@@ -722,9 +724,8 @@
     n_l, n_e = late.shape[0], early.shape[0]
     got_a = swap(send_a, 1)
     both = jnp.concatenate([late, piece_f], axis=0)
-    late_z = [late, swap(both, 0, 2)] + [swap(late, 0, 2 * k) for k in range(2, n_z)]
-    early_x = pair(early_g, 0, 1, x_at == 1)
-    got_a, *late_z, early_g = after([got_a] + late_z + [early_x])
+    late_z = over_z(late, [both] + [late] * (n_z - 2))
+    got_a, *late_z, early_g = after([got_a] + late_z + [early_g])
     first_f = late_z[1][n_l:]
 
     ins = (keep_a, got_a) + tuple(late_z)
@@ -733,25 +734,8 @@
     got = over_plane(loads[0], loads[1:])
     two_f = jnp.concatenate([piece_f, first_f], axis=0)
     rest_f = swap(two_f, 0, 4)
-    early_g = pair(early_g, 1, 0, (s & 1) == 1)
-
-    contract = lambda a, b: lax.dot_general(
-        a, b, (((0,), (0,)), ((), ())), preferred_element_type=F32
-    )
-    early_r = early_g.reshape(2, 2, n_z, 2, n_e // 8, 8, width)
-    to_rows = lambda v, i: v[..., i, :, :].reshape(-1, width)
-    cs_all = lax.dynamic_slice_in_dim(to_rows(early_r, 4), s * quarter, quarter, 1)
-    d_early = jnp.concatenate([to_rows(early_r, i) for i in range(4)], axis=1)
-    few = jnp.sum(early_r[..., 5, :, :].astype(F32), axis=(0, 1, 2, 3))
-    w_early, sum_early = contract(cs_all, d_early), jnp.sum(d_early.astype(F32), axis=0)
-    group_r = lax.dynamic_index_in_dim(early_r, z_at, 2, keepdims=False)
-    group_r = lax.dynamic_index_in_dim(group_r, x_at, 1, keepdims=False)
-    near_d = [
-        group_r[:, :, i].transpose(1, 0, 2, 3).reshape(4 * count, width) for i in range(4)
-    ]
-    *got, two_f, rest_f, w_early, sum_early, few = after(
-        got + [two_f, rest_f, w_early, sum_early, few]
-    )
+    early_g = pair(early_g, 0, 1, x_at == 1)
+    *got, two_f, rest_f, early_g = after(got + [two_f, rest_f, early_g])
 
     total_a = tree_sum([v[: 3 * half] for v in got]).astype(BF16)
     late_g = jnp.concatenate(ordered([v[3 * half :] for v in got], 2 * y_at + x_at), axis=0)
@@ -759,15 +743,32 @@
     blocks = [two_f[: 2 * half], two_f[2 * half :], rest_f[: 2 * half], rest_f[2 * half :]]
     mine_f = jnp.concatenate(ordered(blocks, z_low) + [out_f], axis=0)
     yours_f = swap(mine_f, 0, 1)
-    late_g = pair(late_g, 1, 0, (s & 1) == 1)
+    n_rows = late_g.shape[0]
+    both_g = pair(jnp.concatenate([late_g, early_g], axis=0), 1, 0, (s & 1) == 1)
+    both_g = both_g.reshape(2, -1, width)
+    late_g, early_g = both_g[:, :n_rows], both_g[:, n_rows:]
 
     def mine(row):
         part = row.shape[0] // shards
         return lax.dynamic_slice(row, (s * part,), (part,))
 
+    contract = lambda a, b: lax.dot_general(
+        a, b, (((0,), (0,)), ((), ())), preferred_element_type=F32
+    )
+    early_r = early_g.reshape(2, 2, n_z, 2, n_e // 8, 8, width)
+    to_rows = lambda v, i: v[..., i, :, :].reshape(-1, width)
     late_r = late_g.reshape(2, 2, 2, n_z, n_l // 8, 8, width)
+    cs_all = lax.dynamic_slice_in_dim(to_rows(late_r, 3), s * quarter, quarter, 1)
+    cs_turned = cs_all.reshape(2, 2, 2, n_z, 8, quarter).transpose(0, 2, 3, 1, 4, 5)
+    d_early = jnp.concatenate([to_rows(early_r, i) for i in range(4)], axis=1)
+    few = jnp.sum(early_r[..., 4, :, :].astype(F32), axis=(0, 1, 2, 3))
+    w_early, sum_early = contract(cs_turned.reshape(-1, quarter), d_early), jnp.sum(d_early.astype(F32), axis=0)
+    group_r = lax.dynamic_index_in_dim(early_r, z_at, 2, keepdims=False)
+    group_r = lax.dynamic_index_in_dim(group_r, x_at, 1, keepdims=False)
+    near_d = [
+        group_r[:, :, i].transpose(1, 0, 2, 3).reshape(4 * count, width) for i in range(4)
+    ]
     d_late = jnp.concatenate([to_rows(late_r, i) for i in range(2)], axis=1)
-    cs_all = lax.dynamic_slice_in_dim(to_rows(late_r, 3), s * quarter, quarter, 1)
     w_late, sum_late = contract(cs_all, d_late), jnp.sum(d_late.astype(F32), axis=0)
     gb_late = mine(jnp.sum(late_r[..., 2, :2, :].astype(F32), axis=(0, 1, 2, 3)).reshape(-1))
     side_r = lax.dynamic_index_in_dim(late_r, x_at, 2, keepdims=False)
@@ -800,7 +801,10 @@
     grads_b = [gb_ada, gb_late, gb_o, gb_1, gb_2]
     dada = jnp.concatenate(late_d + near_d, axis=1)
     dcs = lax.dot_general(dada, w_ada, (((1,), (1,)), ((), ())), preferred_element_type=F32)
-    yours_f, gw_ada, gb_late, dcs = after((yours_f, gw_ada, gb_late, dcs))
+    mine_d, send_d = ordered([dcs[: 2 * count], dcs[2 * count :]], y_at)
+    far_d = swap(send_d, 2)
+    yours_f, gw_ada, gb_late, far_d = after((yours_f, gw_ada, gb_late, far_d))
+    *ring_a, yours_f = after(ring_a + [yours_f])
     sides = by_x(mine_f, yours_f)
     deep = [side[: 8 * half].reshape(4, 2 * half, width) for side in sides]
     gw_1 = jnp.concatenate(
@@ -810,12 +814,12 @@
         [side[:, half:].reshape(4 * half, width) for side in deep], axis=0
     ).T.astype(F32)
     gw_o = jnp.concatenate([side[8 * half :] for side in sides], axis=0).astype(F32)
-    *ring_a, gw_1, gw_2, gw_o = after(ring_a + [gw_1, gw_2, gw_o])
     mine_a = tree_sum(ring_a).astype(BF16)
     yours_a = swap(mine_a, 0, 1)
-    dcs = after(dcs, mine_a)
-    dcs = ordered([dcs[k * 8 : (k + 1) * 8] for k in range(4)], s)
-    dcs = ordered([dcs[0]] + [swap(dcs[k], k) for k in range(1, 4)], s)
+    dcs = jnp.concatenate(ordered([mine_d, after(far_d, mine_a)], y_at), axis=1)
+    mine_d, send_d = ordered([dcs[:count], dcs[count:]], s & 1)
+    dcs = ordered([mine_d, swap(send_d, 1)], s & 1)
+    dcs = [v[:, i * quarter : (i + 1) * quarter] for i in range(2) for v in dcs]
     c32 = cond.astype(F32)
     sig = 1.0 / (1.0 + jnp.exp(-c32))
     grad_cond = jnp.concatenate(dcs, axis=1) * (sig * (1.0 + c32 * (1.0 - sig)))

time: 166 us -> 160 us (0.964)
  waiting for transfers between devices: 33.4 us -> 28.8 us
  starting transfers between devices: 40.6 us -> 37.8 us
    ppermute x42 -> x40, waiting for transfers between devices: 33.4 us -> 28.8 us  [swap(): return lax.ppermute(v, ('rep', 'shard'), pairs)]
    ppermute x42 -> x40, starting transfers between devices: 40.6 us -> 37.8 us  [swap(): return lax.ppermute(v, ('rep', 'shard'), pairs)]
  transfers between devices with their start and end apart: 42 -> 40, of which waited for: 13 -> 15; matrix products, arithmetic and copies ran while one was open for 5% -> 6% of each run, Pallas kernels for 28% -> 29%
where the time goes in v5:
time: 160 us
  Pallas kernels  77.7 us (49%)
  starting transfers between devices  37.8 us (24%)
  waiting for transfers between devices  28.8 us (18%)
  other arithmetic  8.87 us (6%)
  local copies, waits for them, and re-layouts  4.63 us (3%)
    pallas_call x8, Pallas kernels, call(): pl.pallas_call(body, out_shape=outs, input_output_aliases=alias or {}, gr...  77.7 us
    ppermute x40, starting transfers between devices, swap(): return lax.ppermute(v, ('rep', 'shard'), pairs)  37.8 us
    ppermute x40, waiting for transfers between devices, swap(): return lax.ppermute(v, ('rep', 'shard'), pairs)  28.8 us
  transfers between devices with their start and end apart: 40, of which 15 were waited for; matrix products, arithmetic and copies ran while one was open for 6% of the time, Pallas kernels for 29%

profile of v5, /device:TPU:0, one launch (start us, length us, event | category | flops | bytes accessed | tf_op | source)
XLA Modules:
  0.0 159.8 jit_solution(14069091462999855898)
XLA Ops:
  1.2 2.6 %collective-permute-start.1 = (bf16[8,384]{1,0:T(8,128)(2,1)}, bf16[8,384]{1,0:T(8,128)(2,1)S(1)}, u32[]{:S(2)}, u32[]{:S(2)}) collective-permute-start(bf16[8,384]{1,0:T(8,128)(2,1)} %cond.1), channel_id=1, source_target_pairs={{0,2},{1,3},{2,0},{3,1},{4,6},{5,7},{6,4},{7,5},{8,10},{9,11},{10,... | collective-permute-start | bytes 18440 | tf_op jit(solution)/shard_map/ppermute | solution.py:499
  3.8 1.7 %collective-permute-done.1.c2 = bf16[8,384]{1,0:T(8,128)(2,1)S(1)} collective-permute-done((bf16[8,384]{1,0:T(8,128)(2,1)}, bf16[8,384]{1,0:T(8,128)(2,1)S(1)}, u32[]{:S(2)}, u32[]{:S(2)}) %collective-permute-start.1) | collective-permute-done | bytes 6176 | tf_op jit(solution)/shard_map/ppermute | solution.py:499
  8.3 2.9 %shard_map.228 = (f32[8,1152]{1,0:T(8,128)}, f32[8,1152]{1,0:T(8,128)}, f32[8,1152]{1,0:T(8,128)}, f32[8,1152]{1,0:T(8,128)}, f32[8,1536]{1,0:T(8,128)}, /*index...) custom-call(s32[4]{0:T(128)} %pad_add_fusion.info, bf16[8,384]{1,0:T(8,128)(2,1)} %cond.1, ...), custom_call_target="tpu_custom_call" | custom-call | flops 16777216 | bytes 1048576 | tf_op jit(solution)/shard_map/pallas_call | solution.py:461
  13.0 2.7 %shard_map.230.refs_4_ = bf16[864,384]{1,0:T(8,128)(2,1)} custom-call(s32[4]{0:T(128)} %pad_add_fusion.info, bf16[96,384]{1,0:T(8,128)(2,1)} %w_o, bf16[96,1536]{1,0:T(8,128)(2,1)} %w_1, bf16[384,384]{1,0:T(8,128)(2,1)} %w_2), custom_call_target="tpu_custom_call" | custom-call | bytes 1048576 | tf_op jit(solution)/shard_map/pallas_call | solution.py:461
  20.5 13.9 %shard_map.229 = (bf16[8,256,384]{2,1,0:T(8,128)(2,1)}, bf16[8,256,1152]{2,1,0:T(8,128)(2,1)}, bf16[8,6,256,256]{3,2,1,0:T(8,128)(2,1)}, bf16[8,256,384]{2,1,0:T...) custom-call(s32[4]{0:T(128)} %pad_add_fusion.info, bf16[8,256,384]{2,1,0:T(8,128)(2,1)} %tok.7, ...), custom_call_target="tpu_custom_call" | custom-call | flops 4026531840 | bytes 15728640 | tf_op jit(solution)/shard_map/pallas_call | solution.py:461
  35.5 1.8 %collective-permute-done.14.refs_7_ = bf16[864,384]{1,0:T(8,128)(2,1)S(1)} collective-permute-done((bf16[864,384]{1,0:T(8,128)(2,1)S(1)}, bf16[864,384]{1,0:T(8,128)(2,1)S(1)}, u32[]{:S(2)}, u32[]{:S(2)}) %collective-permute-start.14) | collective-permute-done | bytes 663584 | tf_op jit(solution)/shard_map/ppermute | solution.py:499
  38.1 32.1 %shard_map.231 = (bf16[8,256,384]{2,1,0:T(8,128)(2,1)}, f32[8,256,384]{2,1,0:T(8,128)}, bf16[8,256,384]{2,1,0:T(8,128)(2,1)}, bf16[40,384]{1,0:T(8,128)(2,1)}, b...) custom-call(s32[4]{0:T(128)} %pad_add_fusion.info, ...), custom_call_target="tpu_custom_call" | custom-call | flops 16307453952 | bytes 11010048 | tf_op jit(solution)/shard_map/pallas_call | solution.py:461
  71.7 3.0 %collective-permute-done.19 = bf16[40,384]{1,0:T(8,128)(2,1)S(1)} collective-permute-done((bf16[40,384]{1,0:T(8,128)(2,1)}, bf16[40,384]{1,0:T(8,128)(2,1)S(1)}, u32[]{:S(2)}, u32[]{:S(2)}) %collective-permute-start.19) | collective-permute-done | bytes 30752 | tf_op jit(solution)/shard_map/ppermute | solution.py:499
  75.5 1.6 %fusion.3 = (bf16[432,384]{1,0:T(8,128)(2,1)S(1)}, bf16[432,384]{1,0:T(8,128)(2,1)S(1)}, bf16[432,384]{1,0:T(8,128)(2,1)S(1)}, bf16[432,384]{1,0:T(8,128)(2,1)S(1)}) fusion(bf16[2,2,432,384]{3,2,1,0:T(8,128)(2,1)S(1)} %collective-permute-done.15, s32[]{:T(128)S(6)} %select_n.285, s32[]{:T(128)S(6)} %select_n.283, ...), kind=kLoop, calls=%fused_computation.18 | loop fusion | flops 2654208 | bytes 3981328 | tf_op jit(solution)/shard_map/convert_element_type | solution.py:617
  80.6 11.7 %shard_map.232 = (f32[8,256,384]{2,1,0:T(8,128)}, f32[384,1152]{1,0:T(8,128)}, f32[8,768]{1,0:T(8,128)}, f32[8,384]{1,0:T(8,128)}) custom-call(s32[4]{0:T(128)} %pad_add_fusion.info, bf16[8,256,384]{2,1,0:T(8,128)(2,1)} %tok.7, bf16[8,256,384]{2,1,0:T(8,128)(2,1)} %get-tuple-element.133.m1_i, bf16[8,256,1152]{2,1,0:T(8,128)(2,1)} %get-tuple-element.134.qkv_i, ...), custom_call_target="tpu_custom_call" | custom-call | flops 2818572288 | bytes 11796480 | tf_op jit(solution)/shard_map/pallas_call | solution.py:461
  92.4 1.8 %collective-permute-done.17 = bf16[432,384]{1,0:T(8,128)(2,1)S(1)} collective-permute-done((bf16[432,384]{1,0:T(8,128)(2,1)S(1)}, bf16[432,384]{1,0:T(8,128)(2,1)S(1)}, u32[]{:S(2)}, u32[]{:S(2)}) %collective-permute-start.17) | collective-permute-done | bytes 331808 | tf_op jit(solution)/shard_map/ppermute | solution.py:499
  94.5 1.6 %collective-permute-start.20 = (bf16[224,384]{1,0:T(8,128)(2,1)S(1)}, bf16[224,384]{1,0:T(8,128)(2,1)S(1)}, u32[]{:S(2)}, u32[]{:S(2)}) collective-permute-start(bf16[224,384]{1,0:T(8,128)(2,1)S(1)} %get-tuple-element.257), channel_id=1, source_target_pairs={{0,8},{1,9},{2,10},{3,11},{4,12},{5,13},{6,14},{7,15},{8,0},{9,1},... | collective-permute-start | bytes 516104 | tf_op jit(solution)/shard_map/ppermute | solution.py:499
  96.2 2.6 %collective-permute-start.21 = (bf16[224,384]{1,0:T(8,128)(2,1)S(1)}, bf16[224,384]{1,0:T(8,128)(2,1)S(1)}, u32[]{:S(2)}, u32[]{:S(2)}) collective-permute-start(bf16[224,384]{1,0:T(8,128)(2,1)S(1)} %get-tuple-element.258), channel_id=1, source_target_pairs={{0,16},{1,17},{2,18},{3,19},{4,20},{5,21},{6,22},{7,23},{8,24},{9,... | collective-permute-start | bytes 516104 | tf_op jit(solution)/shard_map/ppermute | solution.py:499
  99.0 12.2 %shard_map.233 = (f32[8,256,384]{2,1,0:T(8,128)}, bf16[32,384]{1,0:T(8,128)(2,1)}, bf16[2,2,48,1152]{3,2,1,0:T(8,128)(2,1)}, bf16[2,2,48,1152]{3,2,1,0:T(8,128)(2,1)}) custom-call(s32[4]{0:T(128)} %pad_add_fusion.info, bf16[8,256,384]{2,1,0:T(8,128)(2,1)} %tok.7, bf16[8,256,384]{2,1,0:T(8,128)(2,1)} %get-tuple-element.133.m1_i, ...), custom_call_target="tpu_custom_call", output_to_operand_aliasing={{0}: (9, {})} | custom-call | flops 2818572288 | bytes 11796480 | tf_op jit(solution)/shard_map/pallas_call | solution.py:461
  111.3 2.0 %collective-permute-start.25 = (bf16[32,384]{1,0:T(8,128)(2,1)}, bf16[32,384]{1,0:T(8,128)(2,1)S(1)}, u32[]{:S(2)}, u32[]{:S(2)}) collective-permute-start(bf16[32,384]{1,0:T(8,128)(2,1)} %get-tuple-element.163.refs_0_), channel_id=1, source_target_pairs={{0,16},{1,17},{2,18},{3,19},{4,20},{5,21},{6,22},{7,23},{8,24},{9,... | collective-permute-start | bytes 73736 | tf_op jit(solution)/shard_map/ppermute | solution.py:499
  113.2 1.8 %collective-permute-start.26 = (bf16[32,384]{1,0:T(8,128)(2,1)}, bf16[32,384]{1,0:T(8,128)(2,1)S(1)}, u32[]{:S(2)}, u32[]{:S(2)}) collective-permute-start(bf16[32,384]{1,0:T(8,128)(2,1)} %get-tuple-element.163.refs_0_), channel_id=1, source_target_pairs={{0,24},{1,25},{2,26},{3,27},{4,28},{5,29},{6,30},{7,31},{8,16},{9,... | collective-permute-start | bytes 73736 | tf_op jit(solution)/shard_map/ppermute | solution.py:499
  116.5 2.7 %collective-permute-done.26.refs_3_ = bf16[32,384]{1,0:T(8,128)(2,1)S(1)} collective-permute-done((bf16[32,384]{1,0:T(8,128)(2,1)}, bf16[32,384]{1,0:T(8,128)(2,1)S(1)}, u32[]{:S(2)}, u32[]{:S(2)}) %collective-permute-start.26) | collective-permute-done | bytes 24608 | tf_op jit(solution)/shard_map/ppermute | solution.py:499
  119.2 2.1 %collective-permute-done.24.refs_1_ = bf16[128,384]{1,0:T(8,128)(2,1)S(1)} collective-permute-done((bf16[128,384]{1,0:T(8,128)(2,1)S(1)}, bf16[128,384]{1,0:T(8,128)(2,1)S(1)}, u32[]{:S(2)}, u32[]{:S(2)}) %collective-permute-start.24) | collective-permute-done | bytes 98336 | tf_op jit(solution)/shard_map/ppermute | solution.py:499
  128.2 1.9 %collective-permute-done.31 = bf16[320,384]{1,0:T(8,128)(2,1)S(1)} collective-permute-done((bf16[320,384]{1,0:T(8,128)(2,1)S(1)}, bf16[320,384]{1,0:T(8,128)(2,1)S(1)}, u32[]{:S(2)}, u32[]{:S(2)}) %collective-permute-start.31) | collective-permute-done | bytes 245792 | tf_op jit(solution)/shard_map/ppermute | solution.py:499
  130.2 4.4 %collective-permute-done.30 = bf16[192,384]{1,0:T(8,128)(2,1)S(1)} collective-permute-done((bf16[192,384]{1,0:T(8,128)(2,1)S(1)}, bf16[192,384]{1,0:T(8,128)(2,1)S(1)}, u32[]{:S(2)}, u32[]{:S(2)}) %collective-permute-start.30) | collective-permute-done | bytes 147488 | tf_op jit(solution)/shard_map/ppermute | solution.py:499
  134.7 3.4 %collective-permute-done.29 = bf16[272,384]{1,0:T(8,128)(2,1)S(1)} collective-permute-done((bf16[272,384]{1,0:T(8,128)(2,1)S(1)}, bf16[272,384]{1,0:T(8,128)(2,1)S(1)}, u32[]{:S(2)}, u32[]{:S(2)}) %collective-permute-start.29) | collective-permute-done | bytes 208928 | tf_op jit(solution)/shard_map/ppermute | solution.py:499
  138.7 2.0 %collective-permute-start.36 = (bf16[144,384]{1,0:T(8,128)(2,1)S(1)}, bf16[144,384]{1,0:T(8,128)(2,1)S(1)}, u32[]{:S(2)}, u32[]{:S(2)}) collective-permute-start(bf16[144,384]{1,0:T(8,128)(2,1)S(1)} %add_convert_fusion.6), channel_id=1, source_target_pairs={{0,16},{1,17},{2,18},{3,19},{4,20},{5,21},{6,22},{7,23},{8,24},{9,... | collective-permute-start | bytes 331784 | tf_op jit(solution)/shard_map/ppermute | solution.py:499
  140.7 1.9 %collective-permute-start.37 = (bf16[144,384]{1,0:T(8,128)(2,1)S(1)}, bf16[144,384]{1,0:T(8,128)(2,1)S(1)}, u32[]{:S(2)}, u32[]{:S(2)}) collective-permute-start(bf16[144,384]{1,0:T(8,128)(2,1)S(1)} %add_convert_fusion.6), channel_id=1, source_target_pairs={{0,24},{1,25},{2,26},{3,27},{4,28},{5,29},{6,30},{7,31},{8,16},{9,... | collective-permute-start | bytes 331784 | tf_op jit(solution)/shard_map/ppermute | solution.py:499
  151.8 1.8 %collective-permute-done.32 = bf16[432,384]{1,0:T(8,128)(2,1)S(1)} collective-permute-done((bf16[432,384]{1,0:T(8,128)(2,1)S(1)}, bf16[432,384]{1,0:T(8,128)(2,1)S(1)}, u32[]{:S(2)}, u32[]{:S(2)}) %collective-permute-start.32) | collective-permute-done | bytes 331808 | tf_op jit(solution)/shard_map/ppermute | solution.py:499
  (188 shorter events, 42.2 us)
Async XLA Ops:
  7.0 10.2 %collective-permute-start.7 = (bf16[96,1152]{1,0:T(8,128)(2,1)}, bf16[96,1152]{1,0:T(8,128)(2,1)S(1)}, u32[]{:S(2)}, u32[]{:S(2)}) collective-permute-start(bf16[96,1152]{1,0:T(8,128)(2,1)} %refs_4_.1), channel_id=1, source_target_pairs={{0,2},{1,3},{2,0},{3,1},{4,6},{5,7},{6,4},{7,5},{8,10},{9,11},{10,... | collective-permute-start | bytes 663560 | tf_op jit(solution)/shard_map/ppermute | solution.py:499
  16.3 18.7 %collective-permute-start.9 = (bf16[864,384]{1,0:T(8,128)(2,1)}, bf16[864,384]{1,0:T(8,128)(2,1)S(1)}, u32[]{:S(2)}, u32[]{:S(2)}) collective-permute-start(bf16[864,384]{1,0:T(8,128)(2,1)} %shard_map.230.refs_4_), channel_id=1, source_target_pairs={{0,2},{1,3},{2,0},{3,1},{4,6},{5,7},{6,4},{7,5},{8,10},{9,11},{10,... | collective-permute-start | bytes 1990664 | tf_op jit(solution)/shard_map/ppermute | solution.py:499
  17.8 17.7 %collective-permute-start.13 = (bf16[864,384]{1,0:T(8,128)(2,1)}, bf16[864,384]{1,0:T(8,128)(2,1)S(1)}, u32[]{:S(2)}, u32[]{:S(2)}) collective-permute-start(bf16[864,384]{1,0:T(8,128)(2,1)} %shard_map.230.refs_4_), channel_id=1, source_target_pairs={{0,1},{1,0},{2,3},{3,2},{4,5},{5,4},{6,7},{7,6},{8,9},{9,8},{10,11... | collective-permute-start | bytes 1990664 | tf_op jit(solution)/shard_map/ppermute | solution.py:499
  17.9 16.6 %collective-permute-start.10 = (f32[8,1536]{1,0:T(8,128)}, f32[8,1536]{1,0:T(8,128)S(1)}, u32[]{:S(2)}, u32[]{:S(2)}) collective-permute-start(f32[8,1536]{1,0:T(8,128)} %get-tuple-element.120), channel_id=1, source_target_pairs={{0,1},{1,0},{2,3},{3,2},{4,5},{5,4},{6,7},{7,6},{8,9},{9,8},{10,11... | collective-permute-start | bytes 147464 | tf_op jit(solution)/shard_map/ppermute | solution.py:499
  18.7 16.3 %collective-permute-start.11 = (f32[8,1536]{1,0:T(8,128)}, f32[8,1536]{1,0:T(8,128)S(1)}, u32[]{:S(2)}, u32[]{:S(2)}) collective-permute-start(f32[8,1536]{1,0:T(8,128)} %get-tuple-element.121), channel_id=1, source_target_pairs={{0,2},{1,3},{2,0},{3,1},{4,6},{5,7},{6,4},{7,5},{8,10},{9,11},{10,... | collective-permute-start | bytes 147464 | tf_op jit(solution)/shard_map/ppermute | solution.py:499
  19.9 15.2 %collective-permute-start.12 = (f32[8,1536]{1,0:T(8,128)}, f32[8,1536]{1,0:T(8,128)S(1)}, u32[]{:S(2)}, u32[]{:S(2)}) collective-permute-start(f32[8,1536]{1,0:T(8,128)} %get-tuple-element.122), channel_id=1, source_target_pairs={{0,3},{1,2},{2,1},{3,0},{4,7},{5,6},{6,5},{7,4},{8,11},{9,10},{10,... | collective-permute-start | bytes 147464 | tf_op jit(solution)/shard_map/ppermute | solution.py:499
  77.1 15.3 %collective-permute-start.16 = (bf16[432,384]{1,0:T(8,128)(2,1)S(1)}, bf16[432,384]{1,0:T(8,128)(2,1)S(1)}, u32[]{:S(2)}, u32[]{:S(2)}) collective-permute-start(bf16[432,384]{1,0:T(8,128)(2,1)S(1)} %get-tuple-element.221), channel_id=1, source_target_pairs={{0,4},{1,5},{2,6},{3,7},{4,0},{5,1},{6,2},{7,3},{8,12},{9,13},{10,... | collective-permute-start | bytes 995336 | tf_op jit(solution)/shard_map/ppermute | solution.py:499
  78.6 15.6 %collective-permute-start.17 = (bf16[432,384]{1,0:T(8,128)(2,1)S(1)}, bf16[432,384]{1,0:T(8,128)(2,1)S(1)}, u32[]{:S(2)}, u32[]{:S(2)}) collective-permute-start(bf16[432,384]{1,0:T(8,128)(2,1)S(1)} %get-tuple-element.220), channel_id=1, source_target_pairs={{0,2},{1,3},{2,0},{3,1},{4,6},{5,7},{6,4},{7,5},{8,10},{9,11},{10,... | collective-permute-start | bytes 995336 | tf_op jit(solution)/shard_map/ppermute | solution.py:499
  79.7 14.5 %collective-permute-start.18 = (bf16[432,384]{1,0:T(8,128)(2,1)S(1)}, bf16[432,384]{1,0:T(8,128)(2,1)S(1)}, u32[]{:S(2)}, u32[]{:S(2)}) collective-permute-start(bf16[432,384]{1,0:T(8,128)(2,1)S(1)} %get-tuple-element.219), channel_id=1, source_target_pairs={{0,6},{1,7},{2,4},{3,5},{4,2},{5,3},{6,0},{7,1},{8,14},{9,15},{10,... | collective-permute-start | bytes 995336 | tf_op jit(solution)/shard_map/ppermute | solution.py:499
  94.5 16.7 %collective-permute-start.20 = (bf16[224,384]{1,0:T(8,128)(2,1)S(1)}, bf16[224,384]{1,0:T(8,128)(2,1)S(1)}, u32[]{:S(2)}, u32[]{:S(2)}) collective-permute-start(bf16[224,384]{1,0:T(8,128)(2,1)S(1)} %get-tuple-element.257), channel_id=1, source_target_pairs={{0,8},{1,9},{2,10},{3,11},{4,12},{5,13},{6,14},{7,15},{8,0},{9,1},... | collective-permute-start | bytes 516104 | tf_op jit(solution)/shard_map/ppermute | solution.py:499
  96.2 15.1 %collective-permute-start.21 = (bf16[224,384]{1,0:T(8,128)(2,1)S(1)}, bf16[224,384]{1,0:T(8,128)(2,1)S(1)}, u32[]{:S(2)}, u32[]{:S(2)}) collective-permute-start(bf16[224,384]{1,0:T(8,128)(2,1)S(1)} %get-tuple-element.258), channel_id=1, source_target_pairs={{0,16},{1,17},{2,18},{3,19},{4,20},{5,21},{6,22},{7,23},{8,24},{9,... | collective-permute-start | bytes 516104 | tf_op jit(solution)/shard_map/ppermute | solution.py:499
  98.8 12.5 %collective-permute-start.22 = (bf16[224,384]{1,0:T(8,128)(2,1)S(1)}, bf16[224,384]{1,0:T(8,128)(2,1)S(1)}, u32[]{:S(2)}, u32[]{:S(2)}) collective-permute-start(bf16[224,384]{1,0:T(8,128)(2,1)S(1)} %get-tuple-element.256), channel_id=1, source_target_pairs={{0,24},{1,25},{2,26},{3,27},{4,28},{5,29},{6,30},{7,31},{8,16},{9,... | collective-permute-start | bytes 516104 | tf_op jit(solution)/shard_map/ppermute | solution.py:499
  113.2 6.0 %collective-permute-start.26 = (bf16[32,384]{1,0:T(8,128)(2,1)}, bf16[32,384]{1,0:T(8,128)(2,1)S(1)}, u32[]{:S(2)}, u32[]{:S(2)}) collective-permute-start(bf16[32,384]{1,0:T(8,128)(2,1)} %get-tuple-element.163.refs_0_), channel_id=1, source_target_pairs={{0,24},{1,25},{2,26},{3,27},{4,28},{5,29},{6,30},{7,31},{8,16},{9,... | collective-permute-start | bytes 73736 | tf_op jit(solution)/shard_map/ppermute | solution.py:499
  115.0 6.3 %collective-permute-start.23 = (bf16[2,2,48,1152]{3,2,1,0:T(8,128)(2,1)}, bf16[2,2,48,1152]{3,2,1,0:T(8,128)(2,1)S(1)}, u32[]{:S(2)}, u32[]{:S(2)}) collective-permute-start(bf16[2,2,48,1152]{3,2,1,0:T(8,128)(2,1)} %get-tuple-element.156), channel_id=1, source_target_pairs={{0,1},{1,0},{2,3},{3,2},{4,5},{5,4},{6,7},{7,6},{8,9},{9,8},{10,11... | collective-permute-start | bytes 1327112 | tf_op jit(solution)/shard_map/ppermute | solution.py:499
  121.3 8.8 %collective-permute-start.31 = (bf16[320,384]{1,0:T(8,128)(2,1)S(1)}, bf16[320,384]{1,0:T(8,128)(2,1)S(1)}, u32[]{:S(2)}, u32[]{:S(2)}) collective-permute-start(bf16[320,384]{1,0:T(8,128)(2,1)S(1)} %pad_maximum_fusion.13), channel_id=1, source_target_pairs={{0,4},{1,5},{2,6},{3,7},{4,0},{5,1},{6,2},{7,3},{8,12},{9,13},{10,... | collective-permute-start | bytes 737288 | tf_op jit(solution)/shard_map/ppermute | solution.py:499
  123.0 11.7 %collective-permute-start.27 = (bf16[272,384]{1,0:T(8,128)(2,1)S(1)}, bf16[272,384]{1,0:T(8,128)(2,1)S(1)}, u32[]{:S(2)}, u32[]{:S(2)}) collective-permute-start(bf16[272,384]{1,0:T(8,128)(2,1)S(1)} %get-tuple-element.168), channel_id=1, source_target_pairs={{0,4},{1,5},{2,6},{3,7},{4,0},{5,1},{6,2},{7,3},{8,12},{9,13},{10,... | collective-permute-start | bytes 626696 | tf_op jit(solution)/shard_map/ppermute | solution.py:499
  124.1 10.6 %collective-permute-start.28 = (bf16[272,384]{1,0:T(8,128)(2,1)S(1)}, bf16[272,384]{1,0:T(8,128)(2,1)S(1)}, u32[]{:S(2)}, u32[]{:S(2)}) collective-permute-start(bf16[272,384]{1,0:T(8,128)(2,1)S(1)} %get-tuple-element.169), channel_id=1, source_target_pairs={{0,2},{1,3},{2,0},{3,1},{4,6},{5,7},{6,4},{7,5},{8,10},{9,11},{10,... | collective-permute-start | bytes 626696 | tf_op jit(solution)/shard_map/ppermute | solution.py:499
  125.0 13.1 %collective-permute-start.29 = (bf16[272,384]{1,0:T(8,128)(2,1)S(1)}, bf16[272,384]{1,0:T(8,128)(2,1)S(1)}, u32[]{:S(2)}, u32[]{:S(2)}) collective-permute-start(bf16[272,384]{1,0:T(8,128)(2,1)S(1)} %get-tuple-element.170), channel_id=1, source_target_pairs={{0,6},{1,7},{2,4},{3,5},{4,2},{5,3},{6,0},{7,1},{8,14},{9,15},{10,... | collective-permute-start | bytes 626696 | tf_op jit(solution)/shard_map/ppermute | solution.py:499
  126.6 8.1 %collective-permute-start.30 = (bf16[192,384]{1,0:T(8,128)(2,1)S(1)}, bf16[192,384]{1,0:T(8,128)(2,1)S(1)}, u32[]{:S(2)}, u32[]{:S(2)}) collective-permute-start(bf16[192,384]{1,0:T(8,128)(2,1)S(1)} %pad_maximum_fusion.14), channel_id=1, source_target_pairs={{0,16},{1,17},{2,18},{3,19},{4,20},{5,21},{6,22},{7,23},{8,24},{9,... | collective-permute-start | bytes 442376 | tf_op jit(solution)/shard_map/ppermute | solution.py:499
  138.2 15.4 %collective-permute-start.35 = (bf16[144,384]{1,0:T(8,128)(2,1)S(1)}, bf16[144,384]{1,0:T(8,128)(2,1)S(1)}, u32[]{:S(2)}, u32[]{:S(2)}) collective-permute-start(bf16[144,384]{1,0:T(8,128)(2,1)S(1)} %add_convert_fusion.6), channel_id=1, source_target_pairs={{0,8},{1,9},{2,10},{3,11},{4,12},{5,13},{6,14},{7,15},{8,0},{9,1},... | collective-permute-start | bytes 331784 | tf_op jit(solution)/shard_map/ppermute | solution.py:499
  138.7 14.9 %collective-permute-start.36 = (bf16[144,384]{1,0:T(8,128)(2,1)S(1)}, bf16[144,384]{1,0:T(8,128)(2,1)S(1)}, u32[]{:S(2)}, u32[]{:S(2)}) collective-permute-start(bf16[144,384]{1,0:T(8,128)(2,1)S(1)} %add_convert_fusion.6), channel_id=1, source_target_pairs={{0,16},{1,17},{2,18},{3,19},{4,20},{5,21},{6,22},{7,23},{8,24},{9,... | collective-permute-start | bytes 331784 | tf_op jit(solution)/shard_map/ppermute | solution.py:499
  140.7 12.9 %collective-permute-start.37 = (bf16[144,384]{1,0:T(8,128)(2,1)S(1)}, bf16[144,384]{1,0:T(8,128)(2,1)S(1)}, u32[]{:S(2)}, u32[]{:S(2)}) collective-permute-start(bf16[144,384]{1,0:T(8,128)(2,1)S(1)} %add_convert_fusion.6), channel_id=1, source_target_pairs={{0,24},{1,25},{2,26},{3,27},{4,28},{5,29},{6,30},{7,31},{8,16},{9,... | collective-permute-start | bytes 331784 | tf_op jit(solution)/shard_map/ppermute | solution.py:499
  143.3 10.3 %collective-permute-start.32 = (bf16[432,384]{1,0:T(8,128)(2,1)S(1)}, bf16[432,384]{1,0:T(8,128)(2,1)S(1)}, u32[]{:S(2)}, u32[]{:S(2)}) collective-permute-start(bf16[432,384]{1,0:T(8,128)(2,1)S(1)} %fusion.6), channel_id=1, source_target_pairs={{0,4},{1,5},{2,6},{3,7},{4,0},{5,1},{6,2},{7,3},{8,12},{9,13},{10,... | collective-permute-start | bytes 995336 | tf_op jit(solution)/shard_map/ppermute | solution.py:499
  147.4 6.2 %collective-permute-start.34 = (f32[16,96]{1,0:T(8,128)S(1)}, f32[16,96]{1,0:T(8,128)S(1)}, u32[]{:S(2)}, u32[]{:S(2)}) collective-permute-start(f32[16,96]{1,0:T(8,128)S(1)} %slice_select_fusion.1), channel_id=1, source_target_pairs={{0,2},{1,3},{2,0},{3,1},{4,6},{5,7},{6,4},{7,5},{8,10},{9,11},{10,... | collective-permute-start | bytes 18440 | tf_op jit(solution)/shard_map/ppermute | solution.py:499
  (37 other events, 152.5 us)

commit v6 on v5

--- a/solution.py
+++ b/solution.py
@@ -642,7 +642,7 @@
             [at(length, width)] + out_specs,
             scratch,
             (half_n // per3,),
-            60,
+            50,
             6 * tokens * width * width + 5 * tokens * length * width,
             15 * tokens * width,
             0,

time: 160 us -> 160 us (level)
  Pallas kernels: 77.7 us -> 75.9 us
    pallas_call x8, Pallas kernels: 77.7 us -> 75.9 us  [call(): pl.pallas_call(body, out_shape=outs, input_output_aliases=alias or {}, gr...]
  transfers between devices with their start and end apart: 40 -> 40, of which waited for: 15 -> 16; matrix products, arithmetic and copies ran while one was open for 6% -> 5% of each run, Pallas kernels for 29% -> 27%
where the time goes in v6:
time: 160 us; the launch traced here: 159 us
  Pallas kernels  75.9 us (47%)
  starting transfers between devices  38.4 us (24%)
  waiting for transfers between devices  30 us (19%)
  other arithmetic  8.26 us (5%)
  local copies, waits for them, and re-layouts  4.66 us (3%)
    pallas_call x8, Pallas kernels, call(): pl.pallas_call(body, out_shape=outs, input_output_aliases=alias or {}, gr...  75.9 us
    ppermute x40, starting transfers between devices, swap(): return lax.ppermute(v, ('rep', 'shard'), pairs)  38.4 us
    ppermute x40, waiting for transfers between devices, swap(): return lax.ppermute(v, ('rep', 'shard'), pairs)  30 us
  transfers between devices with their start and end apart: 40, of which 16 were waited for; matrix products, arithmetic and copies ran while one was open for 5% of the time, Pallas kernels for 27%

profile of v6, /device:TPU:0, one launch (start us, length us, event | category | flops | bytes accessed | tf_op | source)
XLA Modules:
  0.0 159.3 jit_solution(18027593593115567395)
XLA Ops:
  1.2 2.6 %collective-permute-start.1 = (bf16[8,384]{1,0:T(8,128)(2,1)}, bf16[8,384]{1,0:T(8,128)(2,1)S(1)}, u32[]{:S(2)}, u32[]{:S(2)}) collective-permute-start(bf16[8,384]{1,0:T(8,128)(2,1)} %cond.1), channel_id=1, source_target_pairs={{0,2},{1,3},{2,0},{3,1},{4,6},{5,7},{6,4},{7,5},{8,10},{9,11},{10,... | collective-permute-start | bytes 18440 | tf_op jit(solution)/shard_map/ppermute | solution.py:499
  3.8 1.7 %collective-permute-done.1.c2 = bf16[8,384]{1,0:T(8,128)(2,1)S(1)} collective-permute-done((bf16[8,384]{1,0:T(8,128)(2,1)}, bf16[8,384]{1,0:T(8,128)(2,1)S(1)}, u32[]{:S(2)}, u32[]{:S(2)}) %collective-permute-start.1) | collective-permute-done | bytes 6176 | tf_op jit(solution)/shard_map/ppermute | solution.py:499
  8.3 2.8 %shard_map.228 = (f32[8,1152]{1,0:T(8,128)}, f32[8,1152]{1,0:T(8,128)}, f32[8,1152]{1,0:T(8,128)}, f32[8,1152]{1,0:T(8,128)}, f32[8,1536]{1,0:T(8,128)}, /*index...) custom-call(s32[4]{0:T(128)} %pad_add_fusion.info, bf16[8,384]{1,0:T(8,128)(2,1)} %cond.1, ...), custom_call_target="tpu_custom_call" | custom-call | flops 16777216 | bytes 1048576 | tf_op jit(solution)/shard_map/pallas_call | solution.py:461
  13.0 2.7 %shard_map.230.refs_4_ = bf16[864,384]{1,0:T(8,128)(2,1)} custom-call(s32[4]{0:T(128)} %pad_add_fusion.info, bf16[96,384]{1,0:T(8,128)(2,1)} %w_o, bf16[96,1536]{1,0:T(8,128)(2,1)} %w_1, bf16[384,384]{1,0:T(8,128)(2,1)} %w_2), custom_call_target="tpu_custom_call" | custom-call | bytes 1048576 | tf_op jit(solution)/shard_map/pallas_call | solution.py:461
  20.5 13.9 %shard_map.229 = (bf16[8,256,384]{2,1,0:T(8,128)(2,1)}, bf16[8,256,1152]{2,1,0:T(8,128)(2,1)}, bf16[8,6,256,256]{3,2,1,0:T(8,128)(2,1)}, bf16[8,256,384]{2,1,0:T...) custom-call(s32[4]{0:T(128)} %pad_add_fusion.info, bf16[8,256,384]{2,1,0:T(8,128)(2,1)} %tok.7, ...), custom_call_target="tpu_custom_call" | custom-call | flops 4026531840 | bytes 15728640 | tf_op jit(solution)/shard_map/pallas_call | solution.py:461
  35.5 1.8 %collective-permute-done.14.refs_7_ = bf16[864,384]{1,0:T(8,128)(2,1)S(1)} collective-permute-done((bf16[864,384]{1,0:T(8,128)(2,1)S(1)}, bf16[864,384]{1,0:T(8,128)(2,1)S(1)}, u32[]{:S(2)}, u32[]{:S(2)}) %collective-permute-start.14) | collective-permute-done | bytes 663584 | tf_op jit(solution)/shard_map/ppermute | solution.py:499
  38.1 32.1 %shard_map.231 = (bf16[8,256,384]{2,1,0:T(8,128)(2,1)}, f32[8,256,384]{2,1,0:T(8,128)}, bf16[8,256,384]{2,1,0:T(8,128)(2,1)}, bf16[40,384]{1,0:T(8,128)(2,1)}, b...) custom-call(s32[4]{0:T(128)} %pad_add_fusion.info, ...), custom_call_target="tpu_custom_call" | custom-call | flops 16307453952 | bytes 11010048 | tf_op jit(solution)/shard_map/pallas_call | solution.py:461
  71.7 3.0 %collective-permute-done.19 = bf16[40,384]{1,0:T(8,128)(2,1)S(1)} collective-permute-done((bf16[40,384]{1,0:T(8,128)(2,1)}, bf16[40,384]{1,0:T(8,128)(2,1)S(1)}, u32[]{:S(2)}, u32[]{:S(2)}) %collective-permute-start.19) | collective-permute-done | bytes 30752 | tf_op jit(solution)/shard_map/ppermute | solution.py:499
  75.5 1.8 %fusion.3 = (bf16[432,384]{1,0:T(8,128)(2,1)S(1)}, bf16[432,384]{1,0:T(8,128)(2,1)S(1)}, bf16[432,384]{1,0:T(8,128)(2,1)S(1)}, bf16[432,384]{1,0:T(8,128)(2,1)S(1)}) fusion(bf16[2,2,432,384]{3,2,1,0:T(8,128)(2,1)S(1)} %collective-permute-done.15, s32[]{:T(128)S(6)} %select_n.285, s32[]{:T(128)S(6)} %select_n.283, ...), kind=kLoop, calls=%fused_computation.18 | loop fusion | flops 2654208 | bytes 3981328 | tf_op jit(solution)/shard_map/convert_element_type | solution.py:617
  77.3 1.6 collective-permute-start.16
  80.9 10.8 %shard_map.232 = (f32[8,256,384]{2,1,0:T(8,128)}, f32[384,1152]{1,0:T(8,128)}, f32[8,768]{1,0:T(8,128)S(1)}, f32[8,384]{1,0:T(8,128)S(1)}) custom-call(s32[4]{0:T(128)S(1)} %copy-done.4, bf16[8,256,384]{2,1,0:T(8,128)(2,1)S(1)} %copy-done, bf16[8,256,384]{2,1,0:T(8,128)(2,1)S(1)} %copy-done.1, bf16[8,256,1152]{2,1,0:T(8,128)(2,1)} %get-tuple-element.134.qkv_i, ...), custom_call_target="tpu_custom_call" | custom-call | flops 2818572288 | bytes 11796480 | tf_op jit(solution)/shard_map/pallas_call | solution.py:461
  91.8 2.7 %collective-permute-done.17 = bf16[432,384]{1,0:T(8,128)(2,1)S(1)} collective-permute-done((bf16[432,384]{1,0:T(8,128)(2,1)S(1)}, bf16[432,384]{1,0:T(8,128)(2,1)S(1)}, u32[]{:S(2)}, u32[]{:S(2)}) %collective-permute-start.17) | collective-permute-done | bytes 331808 | tf_op jit(solution)/shard_map/ppermute | solution.py:499
  94.8 1.6 %collective-permute-start.20 = (bf16[224,384]{1,0:T(8,128)(2,1)S(1)}, bf16[224,384]{1,0:T(8,128)(2,1)S(1)}, u32[]{:S(2)}, u32[]{:S(2)}) collective-permute-start(bf16[224,384]{1,0:T(8,128)(2,1)S(1)} %get-tuple-element.257), channel_id=1, source_target_pairs={{0,8},{1,9},{2,10},{3,11},{4,12},{5,13},{6,14},{7,15},{8,0},{9,1},... | collective-permute-start | bytes 516104 | tf_op jit(solution)/shard_map/ppermute | solution.py:499
  96.4 2.6 %collective-permute-start.21 = (bf16[224,384]{1,0:T(8,128)(2,1)S(1)}, bf16[224,384]{1,0:T(8,128)(2,1)S(1)}, u32[]{:S(2)}, u32[]{:S(2)}) collective-permute-start(bf16[224,384]{1,0:T(8,128)(2,1)S(1)} %get-tuple-element.258), channel_id=1, source_target_pairs={{0,16},{1,17},{2,18},{3,19},{4,20},{5,21},{6,22},{7,23},{8,24},{9,... | collective-permute-start | bytes 516104 | tf_op jit(solution)/shard_map/ppermute | solution.py:499
  99.2 11.3 %shard_map.233 = (f32[8,256,384]{2,1,0:T(8,128)}, bf16[32,384]{1,0:T(8,128)(2,1)S(1)}, bf16[2,2,48,1152]{3,2,1,0:T(8,128)(2,1)S(1)}, bf16[2,2,48,1152]{3,2,1,0:T(8,128)(2,1)S(1)}) custom-call(s32[4]{0:T(128)S(1)} %copy-done.4, bf16[8,256,384]{2,1,0:T(8,128)(2,1)S(1)} %copy-done, ...), custom_call_target="tpu_custom_call", output_to_operand_aliasing={{0}: (9, {})} | custom-call | flops 2818572288 | bytes 11796480 | tf_op jit(solution)/shard_map/pallas_call | solution.py:461
  110.5 2.9 %collective-permute-start.25 = (bf16[32,384]{1,0:T(8,128)(2,1)S(1)}, bf16[32,384]{1,0:T(8,128)(2,1)S(1)}, u32[]{:S(2)}, u32[]{:S(2)}) collective-permute-start(bf16[32,384]{1,0:T(8,128)(2,1)S(1)} %get-tuple-element.163.refs_0_), channel_id=1, source_target_pairs={{0,16},{1,17},{2,18},{3,19},{4,20},{5,21},{6,22},{7,23},{8,24},{9,... | collective-permute-start | bytes 73736 | tf_op jit(solution)/shard_map/ppermute | solution.py:499
  115.3 3.9 %collective-permute-done.26.refs_3_ = bf16[32,384]{1,0:T(8,128)(2,1)S(1)} collective-permute-done((bf16[32,384]{1,0:T(8,128)(2,1)S(1)}, bf16[32,384]{1,0:T(8,128)(2,1)S(1)}, u32[]{:S(2)}, u32[]{:S(2)}) %collective-permute-start.26) | collective-permute-done | bytes 24608 | tf_op jit(solution)/shard_map/ppermute | solution.py:499
  124.1 2.0 %collective-permute-start.29 = (bf16[272,384]{1,0:T(8,128)(2,1)S(1)}, bf16[272,384]{1,0:T(8,128)(2,1)S(1)}, u32[]{:S(2)}, u32[]{:S(2)}) collective-permute-start(bf16[272,384]{1,0:T(8,128)(2,1)S(1)} %get-tuple-element.170), channel_id=1, source_target_pairs={{0,6},{1,7},{2,4},{3,5},{4,2},{5,3},{6,0},{7,1},{8,14},{9,15},{10,... | collective-permute-start | bytes 626696 | tf_op jit(solution)/shard_map/ppermute | solution.py:499
  127.5 1.7 %collective-permute-done.31 = bf16[320,384]{1,0:T(8,128)(2,1)S(1)} collective-permute-done((bf16[320,384]{1,0:T(8,128)(2,1)S(1)}, bf16[320,384]{1,0:T(8,128)(2,1)S(1)}, u32[]{:S(2)}, u32[]{:S(2)}) %collective-permute-start.31) | collective-permute-done | bytes 245792 | tf_op jit(solution)/shard_map/ppermute | solution.py:499
  129.3 5.0 %collective-permute-done.30 = bf16[192,384]{1,0:T(8,128)(2,1)S(1)} collective-permute-done((bf16[192,384]{1,0:T(8,128)(2,1)S(1)}, bf16[192,384]{1,0:T(8,128)(2,1)S(1)}, u32[]{:S(2)}, u32[]{:S(2)}) %collective-permute-start.30) | collective-permute-done | bytes 147488 | tf_op jit(solution)/shard_map/ppermute | solution.py:499
  134.4 2.9 %collective-permute-done.29 = bf16[272,384]{1,0:T(8,128)(2,1)S(1)} collective-permute-done((bf16[272,384]{1,0:T(8,128)(2,1)S(1)}, bf16[272,384]{1,0:T(8,128)(2,1)S(1)}, u32[]{:S(2)}, u32[]{:S(2)}) %collective-permute-start.29) | collective-permute-done | bytes 208928 | tf_op jit(solution)/shard_map/ppermute | solution.py:499
  137.8 2.6 %collective-permute-start.36 = (bf16[144,384]{1,0:T(8,128)(2,1)S(1)}, bf16[144,384]{1,0:T(8,128)(2,1)S(1)}, u32[]{:S(2)}, u32[]{:S(2)}) collective-permute-start(bf16[144,384]{1,0:T(8,128)(2,1)S(1)} %add_convert_fusion.6), channel_id=1, source_target_pairs={{0,16},{1,17},{2,18},{3,19},{4,20},{5,21},{6,22},{7,23},{8,24},{9,... | collective-permute-start | bytes 331784 | tf_op jit(solution)/shard_map/ppermute | solution.py:499
  149.2 1.6 shard_map.235
  150.8 2.0 %collective-permute-done.32 = bf16[432,384]{1,0:T(8,128)(2,1)S(1)} collective-permute-done((bf16[432,384]{1,0:T(8,128)(2,1)S(1)}, bf16[432,384]{1,0:T(8,128)(2,1)S(1)}, u32[]{:S(2)}, u32[]{:S(2)}) %collective-permute-start.32) | collective-permute-done | bytes 331808 | tf_op jit(solution)/shard_map/ppermute | solution.py:499
  (194 shorter events, 40.3 us)
Async XLA Ops:
  7.0 10.2 %collective-permute-start.7 = (bf16[96,1152]{1,0:T(8,128)(2,1)}, bf16[96,1152]{1,0:T(8,128)(2,1)S(1)}, u32[]{:S(2)}, u32[]{:S(2)}) collective-permute-start(bf16[96,1152]{1,0:T(8,128)(2,1)} %refs_4_.1), channel_id=1, source_target_pairs={{0,2},{1,3},{2,0},{3,1},{4,6},{5,7},{6,4},{7,5},{8,10},{9,11},{10,... | collective-permute-start | bytes 663560 | tf_op jit(solution)/shard_map/ppermute | solution.py:499
  16.3 18.7 %collective-permute-start.9 = (bf16[864,384]{1,0:T(8,128)(2,1)}, bf16[864,384]{1,0:T(8,128)(2,1)S(1)}, u32[]{:S(2)}, u32[]{:S(2)}) collective-permute-start(bf16[864,384]{1,0:T(8,128)(2,1)} %shard_map.230.refs_4_), channel_id=1, source_target_pairs={{0,2},{1,3},{2,0},{3,1},{4,6},{5,7},{6,4},{7,5},{8,10},{9,11},{10,... | collective-permute-start | bytes 1990664 | tf_op jit(solution)/shard_map/ppermute | solution.py:499
  17.8 17.7 %collective-permute-start.13 = (bf16[864,384]{1,0:T(8,128)(2,1)}, bf16[864,384]{1,0:T(8,128)(2,1)S(1)}, u32[]{:S(2)}, u32[]{:S(2)}) collective-permute-start(bf16[864,384]{1,0:T(8,128)(2,1)} %shard_map.230.refs_4_), channel_id=1, source_target_pairs={{0,1},{1,0},{2,3},{3,2},{4,5},{5,4},{6,7},{7,6},{8,9},{9,8},{10,11... | collective-permute-start | bytes 1990664 | tf_op jit(solution)/shard_map/ppermute | solution.py:499
  17.9 16.6 %collective-permute-start.10 = (f32[8,1536]{1,0:T(8,128)}, f32[8,1536]{1,0:T(8,128)S(1)}, u32[]{:S(2)}, u32[]{:S(2)}) collective-permute-start(f32[8,1536]{1,0:T(8,128)} %get-tuple-element.120), channel_id=1, source_target_pairs={{0,1},{1,0},{2,3},{3,2},{4,5},{5,4},{6,7},{7,6},{8,9},{9,8},{10,11... | collective-permute-start | bytes 147464 | tf_op jit(solution)/shard_map/ppermute | solution.py:499
  18.7 16.3 %collective-permute-start.11 = (f32[8,1536]{1,0:T(8,128)}, f32[8,1536]{1,0:T(8,128)S(1)}, u32[]{:S(2)}, u32[]{:S(2)}) collective-permute-start(f32[8,1536]{1,0:T(8,128)} %get-tuple-element.121), channel_id=1, source_target_pairs={{0,2},{1,3},{2,0},{3,1},{4,6},{5,7},{6,4},{7,5},{8,10},{9,11},{10,... | collective-permute-start | bytes 147464 | tf_op jit(solution)/shard_map/ppermute | solution.py:499
  19.9 15.2 %collective-permute-start.12 = (f32[8,1536]{1,0:T(8,128)}, f32[8,1536]{1,0:T(8,128)S(1)}, u32[]{:S(2)}, u32[]{:S(2)}) collective-permute-start(f32[8,1536]{1,0:T(8,128)} %get-tuple-element.122), channel_id=1, source_target_pairs={{0,3},{1,2},{2,1},{3,0},{4,7},{5,6},{6,5},{7,4},{8,11},{9,10},{10,... | collective-permute-start | bytes 147464 | tf_op jit(solution)/shard_map/ppermute | solution.py:499
  77.3 14.5 %collective-permute-start.16 = (bf16[432,384]{1,0:T(8,128)(2,1)S(1)}, bf16[432,384]{1,0:T(8,128)(2,1)S(1)}, u32[]{:S(2)}, u32[]{:S(2)}) collective-permute-start(bf16[432,384]{1,0:T(8,128)(2,1)S(1)} %get-tuple-element.221), channel_id=1, source_target_pairs={{0,4},{1,5},{2,6},{3,7},{4,0},{5,1},{6,2},{7,3},{8,12},{9,13},{10,... | collective-permute-start | bytes 995336 | tf_op jit(solution)/shard_map/ppermute | solution.py:499
  78.9 15.6 %collective-permute-start.17 = (bf16[432,384]{1,0:T(8,128)(2,1)S(1)}, bf16[432,384]{1,0:T(8,128)(2,1)S(1)}, u32[]{:S(2)}, u32[]{:S(2)}) collective-permute-start(bf16[432,384]{1,0:T(8,128)(2,1)S(1)} %get-tuple-element.220), channel_id=1, source_target_pairs={{0,2},{1,3},{2,0},{3,1},{4,6},{5,7},{6,4},{7,5},{8,10},{9,11},{10,... | collective-permute-start | bytes 995336 | tf_op jit(solution)/shard_map/ppermute | solution.py:499
  80.0 14.5 %collective-permute-start.18 = (bf16[432,384]{1,0:T(8,128)(2,1)S(1)}, bf16[432,384]{1,0:T(8,128)(2,1)S(1)}, u32[]{:S(2)}, u32[]{:S(2)}) collective-permute-start(bf16[432,384]{1,0:T(8,128)(2,1)S(1)} %get-tuple-element.219), channel_id=1, source_target_pairs={{0,6},{1,7},{2,4},{3,5},{4,2},{5,3},{6,0},{7,1},{8,14},{9,15},{10,... | collective-permute-start | bytes 995336 | tf_op jit(solution)/shard_map/ppermute | solution.py:499
  94.8 15.7 %collective-permute-start.20 = (bf16[224,384]{1,0:T(8,128)(2,1)S(1)}, bf16[224,384]{1,0:T(8,128)(2,1)S(1)}, u32[]{:S(2)}, u32[]{:S(2)}) collective-permute-start(bf16[224,384]{1,0:T(8,128)(2,1)S(1)} %get-tuple-element.257), channel_id=1, source_target_pairs={{0,8},{1,9},{2,10},{3,11},{4,12},{5,13},{6,14},{7,15},{8,0},{9,1},... | collective-permute-start | bytes 516104 | tf_op jit(solution)/shard_map/ppermute | solution.py:499
  96.4 14.1 %collective-permute-start.21 = (bf16[224,384]{1,0:T(8,128)(2,1)S(1)}, bf16[224,384]{1,0:T(8,128)(2,1)S(1)}, u32[]{:S(2)}, u32[]{:S(2)}) collective-permute-start(bf16[224,384]{1,0:T(8,128)(2,1)S(1)} %get-tuple-element.258), channel_id=1, source_target_pairs={{0,16},{1,17},{2,18},{3,19},{4,20},{5,21},{6,22},{7,23},{8,24},{9,... | collective-permute-start | bytes 516104 | tf_op jit(solution)/shard_map/ppermute | solution.py:499
  99.0 11.5 %collective-permute-start.22 = (bf16[224,384]{1,0:T(8,128)(2,1)S(1)}, bf16[224,384]{1,0:T(8,128)(2,1)S(1)}, u32[]{:S(2)}, u32[]{:S(2)}) collective-permute-start(bf16[224,384]{1,0:T(8,128)(2,1)S(1)} %get-tuple-element.256), channel_id=1, source_target_pairs={{0,24},{1,25},{2,26},{3,27},{4,28},{5,29},{6,30},{7,31},{8,16},{9,... | collective-permute-start | bytes 516104 | tf_op jit(solution)/shard_map/ppermute | solution.py:499
  113.4 5.8 %collective-permute-start.26 = (bf16[32,384]{1,0:T(8,128)(2,1)S(1)}, bf16[32,384]{1,0:T(8,128)(2,1)S(1)}, u32[]{:S(2)}, u32[]{:S(2)}) collective-permute-start(bf16[32,384]{1,0:T(8,128)(2,1)S(1)} %get-tuple-element.163.refs_0_), channel_id=1, source_target_pairs={{0,24},{1,25},{2,26},{3,27},{4,28},{5,29},{6,30},{7,31},{8,16},{9,... | collective-permute-start | bytes 73736 | tf_op jit(solution)/shard_map/ppermute | solution.py:499
  114.7 5.6 %collective-permute-start.23 = (bf16[2,2,48,1152]{3,2,1,0:T(8,128)(2,1)S(1)}, bf16[2,2,48,1152]{3,2,1,0:T(8,128)(2,1)S(1)}, u32[]{:S(2)}, u32[]{:S(2)}) collective-permute-start(bf16[2,2,48,1152]{3,2,1,0:T(8,128)(2,1)S(1)} %get-tuple-element.156), channel_id=1, source_target_pairs={{0,1},{1,0},{2,3},{3,2},{4,5},{5,4},{6,7},{7,6},{8,9},{9,8},{10,11... | collective-permute-start | bytes 1327112 | tf_op jit(solution)/shard_map/ppermute | solution.py:499
  120.4 8.9 %collective-permute-start.31 = (bf16[320,384]{1,0:T(8,128)(2,1)S(1)}, bf16[320,384]{1,0:T(8,128)(2,1)S(1)}, u32[]{:S(2)}, u32[]{:S(2)}) collective-permute-start(bf16[320,384]{1,0:T(8,128)(2,1)S(1)} %pad_maximum_fusion.13), channel_id=1, source_target_pairs={{0,4},{1,5},{2,6},{3,7},{4,0},{5,1},{6,2},{7,3},{8,12},{9,13},{10,... | collective-permute-start | bytes 737288 | tf_op jit(solution)/shard_map/ppermute | solution.py:499
  122.5 11.9 %collective-permute-start.27 = (bf16[272,384]{1,0:T(8,128)(2,1)S(1)}, bf16[272,384]{1,0:T(8,128)(2,1)S(1)}, u32[]{:S(2)}, u32[]{:S(2)}) collective-permute-start(bf16[272,384]{1,0:T(8,128)(2,1)S(1)} %get-tuple-element.168), channel_id=1, source_target_pairs={{0,4},{1,5},{2,6},{3,7},{4,0},{5,1},{6,2},{7,3},{8,12},{9,13},{10,... | collective-permute-start | bytes 626696 | tf_op jit(solution)/shard_map/ppermute | solution.py:499
  123.1 11.2 %collective-permute-start.28 = (bf16[272,384]{1,0:T(8,128)(2,1)S(1)}, bf16[272,384]{1,0:T(8,128)(2,1)S(1)}, u32[]{:S(2)}, u32[]{:S(2)}) collective-permute-start(bf16[272,384]{1,0:T(8,128)(2,1)S(1)} %get-tuple-element.169), channel_id=1, source_target_pairs={{0,2},{1,3},{2,0},{3,1},{4,6},{5,7},{6,4},{7,5},{8,10},{9,11},{10,... | collective-permute-start | bytes 626696 | tf_op jit(solution)/shard_map/ppermute | solution.py:499
  124.1 13.2 %collective-permute-start.29 = (bf16[272,384]{1,0:T(8,128)(2,1)S(1)}, bf16[272,384]{1,0:T(8,128)(2,1)S(1)}, u32[]{:S(2)}, u32[]{:S(2)}) collective-permute-start(bf16[272,384]{1,0:T(8,128)(2,1)S(1)} %get-tuple-element.170), channel_id=1, source_target_pairs={{0,6},{1,7},{2,4},{3,5},{4,2},{5,3},{6,0},{7,1},{8,14},{9,15},{10,... | collective-permute-start | bytes 626696 | tf_op jit(solution)/shard_map/ppermute | solution.py:499
  126.1 8.3 %collective-permute-start.30 = (bf16[192,384]{1,0:T(8,128)(2,1)S(1)}, bf16[192,384]{1,0:T(8,128)(2,1)S(1)}, u32[]{:S(2)}, u32[]{:S(2)}) collective-permute-start(bf16[192,384]{1,0:T(8,128)(2,1)S(1)} %pad_maximum_fusion.14), channel_id=1, source_target_pairs={{0,16},{1,17},{2,18},{3,19},{4,20},{5,21},{6,22},{7,23},{8,24},{9,... | collective-permute-start | bytes 442376 | tf_op jit(solution)/shard_map/ppermute | solution.py:499
  137.3 15.4 %collective-permute-start.35 = (bf16[144,384]{1,0:T(8,128)(2,1)S(1)}, bf16[144,384]{1,0:T(8,128)(2,1)S(1)}, u32[]{:S(2)}, u32[]{:S(2)}) collective-permute-start(bf16[144,384]{1,0:T(8,128)(2,1)S(1)} %add_convert_fusion.6), channel_id=1, source_target_pairs={{0,8},{1,9},{2,10},{3,11},{4,12},{5,13},{6,14},{7,15},{8,0},{9,1},... | collective-permute-start | bytes 331784 | tf_op jit(solution)/shard_map/ppermute | solution.py:499
  137.8 15.0 %collective-permute-start.36 = (bf16[144,384]{1,0:T(8,128)(2,1)S(1)}, bf16[144,384]{1,0:T(8,128)(2,1)S(1)}, u32[]{:S(2)}, u32[]{:S(2)}) collective-permute-start(bf16[144,384]{1,0:T(8,128)(2,1)S(1)} %add_convert_fusion.6), channel_id=1, source_target_pairs={{0,16},{1,17},{2,18},{3,19},{4,20},{5,21},{6,22},{7,23},{8,24},{9,... | collective-permute-start | bytes 331784 | tf_op jit(solution)/shard_map/ppermute | solution.py:499
  140.4 12.4 %collective-permute-start.37 = (bf16[144,384]{1,0:T(8,128)(2,1)S(1)}, bf16[144,384]{1,0:T(8,128)(2,1)S(1)}, u32[]{:S(2)}, u32[]{:S(2)}) collective-permute-start(bf16[144,384]{1,0:T(8,128)(2,1)S(1)} %add_convert_fusion.6), channel_id=1, source_target_pairs={{0,24},{1,25},{2,26},{3,27},{4,28},{5,29},{6,30},{7,31},{8,16},{9,... | collective-permute-start | bytes 331784 | tf_op jit(solution)/shard_map/ppermute | solution.py:499
  142.5 10.3 %collective-permute-start.32 = (bf16[432,384]{1,0:T(8,128)(2,1)S(1)}, bf16[432,384]{1,0:T(8,128)(2,1)S(1)}, u32[]{:S(2)}, u32[]{:S(2)}) collective-permute-start(bf16[432,384]{1,0:T(8,128)(2,1)S(1)} %fusion.6), channel_id=1, source_target_pairs={{0,4},{1,5},{2,6},{3,7},{4,0},{5,1},{6,2},{7,3},{8,12},{9,13},{10,... | collective-permute-start | bytes 995336 | tf_op jit(solution)/shard_map/ppermute | solution.py:499
  146.6 6.2 %collective-permute-start.34 = (f32[16,96]{1,0:T(8,128)S(1)}, f32[16,96]{1,0:T(8,128)S(1)}, u32[]{:S(2)}, u32[]{:S(2)}) collective-permute-start(f32[16,96]{1,0:T(8,128)S(1)} %slice_select_fusion.1), channel_id=1, source_target_pairs={{0,2},{1,3},{2,0},{3,1},{4,6},{5,7},{6,4},{7,5},{8,10},{9,11},{10,... | collective-permute-start | bytes 18440 | tf_op jit(solution)/shard_map/ppermute | solution.py:499
  (40 other events, 150.8 us)

commit v7 on v6

--- a/solution.py
+++ b/solution.py
@@ -723,10 +723,8 @@
 
     n_l, n_e = late.shape[0], early.shape[0]
     got_a = swap(send_a, 1)
-    both = jnp.concatenate([late, piece_f], axis=0)
-    late_z = over_z(late, [both] + [late] * (n_z - 2))
-    got_a, *late_z, early_g = after([got_a] + late_z + [early_g])
-    first_f = late_z[1][n_l:]
+    late_z, first_f = over_z(late, [late] * (n_z - 1)), swap(piece_f, 0, 2)
+    got_a, *late_z, first_f, early_g = after([got_a] + late_z + [first_f, early_g])
 
     ins = (keep_a, got_a) + tuple(late_z)
     outs = [jax.ShapeDtypeStruct((3 * half + n_z * n_l, width), BF16)] * 4

time: 160 us -> 159 us (level)
    ppermute x40 -> x41, waiting for transfers between devices: 30 us -> 28.9 us  [swap(): return lax.ppermute(v, ('rep', 'shard'), pairs)]
    ppermute x40 -> x41, starting transfers between devices: 38.4 us -> 38.9 us  [swap(): return lax.ppermute(v, ('rep', 'shard'), pairs)]
  transfers between devices with their start and end apart: 40 -> 41, of which waited for: 16 -> 16; matrix products, arithmetic and copies ran while one was open for 5% -> 5% of each run, Pallas kernels for 27% -> 28%
where the time goes in v7:
time: 159 us
  Pallas kernels  75.8 us (48%)
  starting transfers between devices  38.9 us (24%)
  waiting for transfers between devices  28.9 us (18%)
  other arithmetic  8.26 us (5%)
  local copies, waits for them, and re-layouts  4.65 us (3%)
    pallas_call x8, Pallas kernels, call(): pl.pallas_call(body, out_shape=outs, input_output_aliases=alias or {}, gr...  75.8 us
    ppermute x41, starting transfers between devices, swap(): return lax.ppermute(v, ('rep', 'shard'), pairs)  38.9 us
    ppermute x41, waiting for transfers between devices, swap(): return lax.ppermute(v, ('rep', 'shard'), pairs)  28.9 us
  transfers between devices with their start and end apart: 41, of which 16 were waited for; matrix products, arithmetic and copies ran while one was open for 5% of the time, Pallas kernels for 28%

profile of v7, /device:TPU:0, one launch (start us, length us, event | category | flops | bytes accessed | tf_op | source)
XLA Modules:
  0.0 158.6 jit_solution(11985264389127407591)
XLA Ops:
  1.2 2.6 %collective-permute-start.1 = (bf16[8,384]{1,0:T(8,128)(2,1)}, bf16[8,384]{1,0:T(8,128)(2,1)S(1)}, u32[]{:S(2)}, u32[]{:S(2)}) collective-permute-start(bf16[8,384]{1,0:T(8,128)(2,1)} %cond.1), channel_id=1, source_target_pairs={{0,2},{1,3},{2,0},{3,1},{4,6},{5,7},{6,4},{7,5},{8,10},{9,11},{10,... | collective-permute-start | bytes 18440 | tf_op jit(solution)/shard_map/ppermute | solution.py:499
  3.8 1.7 %collective-permute-done.1.c2 = bf16[8,384]{1,0:T(8,128)(2,1)S(1)} collective-permute-done((bf16[8,384]{1,0:T(8,128)(2,1)}, bf16[8,384]{1,0:T(8,128)(2,1)S(1)}, u32[]{:S(2)}, u32[]{:S(2)}) %collective-permute-start.1) | collective-permute-done | bytes 6176 | tf_op jit(solution)/shard_map/ppermute | solution.py:499
  8.3 2.9 %shard_map.228 = (f32[8,1152]{1,0:T(8,128)}, f32[8,1152]{1,0:T(8,128)}, f32[8,1152]{1,0:T(8,128)}, f32[8,1152]{1,0:T(8,128)}, f32[8,1536]{1,0:T(8,128)}, /*index...) custom-call(s32[4]{0:T(128)} %pad_add_fusion.info, bf16[8,384]{1,0:T(8,128)(2,1)} %cond.1, ...), custom_call_target="tpu_custom_call" | custom-call | flops 16777216 | bytes 1048576 | tf_op jit(solution)/shard_map/pallas_call | solution.py:461
  13.0 2.7 %shard_map.230.refs_4_ = bf16[864,384]{1,0:T(8,128)(2,1)} custom-call(s32[4]{0:T(128)} %pad_add_fusion.info, bf16[96,384]{1,0:T(8,128)(2,1)} %w_o, bf16[96,1536]{1,0:T(8,128)(2,1)} %w_1, bf16[384,384]{1,0:T(8,128)(2,1)} %w_2), custom_call_target="tpu_custom_call" | custom-call | bytes 1048576 | tf_op jit(solution)/shard_map/pallas_call | solution.py:461
  20.5 13.9 %shard_map.229 = (bf16[8,256,384]{2,1,0:T(8,128)(2,1)}, bf16[8,256,1152]{2,1,0:T(8,128)(2,1)}, bf16[8,6,256,256]{3,2,1,0:T(8,128)(2,1)}, bf16[8,256,384]{2,1,0:T...) custom-call(s32[4]{0:T(128)} %pad_add_fusion.info, bf16[8,256,384]{2,1,0:T(8,128)(2,1)} %tok.7, ...), custom_call_target="tpu_custom_call" | custom-call | flops 4026531840 | bytes 15728640 | tf_op jit(solution)/shard_map/pallas_call | solution.py:461
  35.5 1.8 %collective-permute-done.14.refs_7_ = bf16[864,384]{1,0:T(8,128)(2,1)S(1)} collective-permute-done((bf16[864,384]{1,0:T(8,128)(2,1)S(1)}, bf16[864,384]{1,0:T(8,128)(2,1)S(1)}, u32[]{:S(2)}, u32[]{:S(2)}) %collective-permute-start.14) | collective-permute-done | bytes 663584 | tf_op jit(solution)/shard_map/ppermute | solution.py:499
  38.1 32.1 %shard_map.231 = (bf16[8,256,384]{2,1,0:T(8,128)(2,1)}, f32[8,256,384]{2,1,0:T(8,128)}, bf16[8,256,384]{2,1,0:T(8,128)(2,1)}, bf16[40,384]{1,0:T(8,128)(2,1)}, b...) custom-call(s32[4]{0:T(128)} %pad_add_fusion.info, ...), custom_call_target="tpu_custom_call" | custom-call | flops 16307453952 | bytes 11010048 | tf_op jit(solution)/shard_map/pallas_call | solution.py:461
  71.7 3.0 %collective-permute-done.19 = bf16[40,384]{1,0:T(8,128)(2,1)S(1)} collective-permute-done((bf16[40,384]{1,0:T(8,128)(2,1)}, bf16[40,384]{1,0:T(8,128)(2,1)S(1)}, u32[]{:S(2)}, u32[]{:S(2)}) %collective-permute-start.19) | collective-permute-done | bytes 30752 | tf_op jit(solution)/shard_map/ppermute | solution.py:499
  75.5 1.8 %fusion.3 = (bf16[432,384]{1,0:T(8,128)(2,1)S(1)}, bf16[432,384]{1,0:T(8,128)(2,1)S(1)}, bf16[432,384]{1,0:T(8,128)(2,1)S(1)}, bf16[432,384]{1,0:T(8,128)(2,1)S(1)}) fusion(bf16[2,2,432,384]{3,2,1,0:T(8,128)(2,1)S(1)} %collective-permute-done.15, s32[]{:T(128)S(6)} %select_n.285, s32[]{:T(128)S(6)} %select_n.283, ...), kind=kLoop, calls=%fused_computation.18 | loop fusion | flops 2654208 | bytes 3981328 | tf_op jit(solution)/shard_map/convert_element_type | solution.py:617
  77.3 1.6 collective-permute-start.16
  80.9 10.8 %shard_map.232 = (f32[8,256,384]{2,1,0:T(8,128)}, f32[384,1152]{1,0:T(8,128)}, f32[8,768]{1,0:T(8,128)S(1)}, f32[8,384]{1,0:T(8,128)S(1)}) custom-call(s32[4]{0:T(128)S(1)} %copy-done.4, bf16[8,256,384]{2,1,0:T(8,128)(2,1)S(1)} %copy-done, bf16[8,256,384]{2,1,0:T(8,128)(2,1)S(1)} %copy-done.1, bf16[8,256,1152]{2,1,0:T(8,128)(2,1)} %get-tuple-element.135.qkv_i, ...), custom_call_target="tpu_custom_call" | custom-call | flops 2818572288 | bytes 11796480 | tf_op jit(solution)/shard_map/pallas_call | solution.py:461
  91.8 2.7 %collective-permute-done.17 = bf16[432,384]{1,0:T(8,128)(2,1)S(1)} collective-permute-done((bf16[432,384]{1,0:T(8,128)(2,1)S(1)}, bf16[432,384]{1,0:T(8,128)(2,1)S(1)}, u32[]{:S(2)}, u32[]{:S(2)}) %collective-permute-start.17) | collective-permute-done | bytes 331808 | tf_op jit(solution)/shard_map/ppermute | solution.py:499
  94.8 1.7 %collective-permute-start.20 = (bf16[224,384]{1,0:T(8,128)(2,1)S(1)}, bf16[224,384]{1,0:T(8,128)(2,1)S(1)}, u32[]{:S(2)}, u32[]{:S(2)}) collective-permute-start(bf16[224,384]{1,0:T(8,128)(2,1)S(1)} %get-tuple-element.259), channel_id=1, source_target_pairs={{0,8},{1,9},{2,10},{3,11},{4,12},{5,13},{6,14},{7,15},{8,0},{9,1},... | collective-permute-start | bytes 516104 | tf_op jit(solution)/shard_map/ppermute | solution.py:499
  96.4 2.6 %collective-permute-start.21 = (bf16[224,384]{1,0:T(8,128)(2,1)S(1)}, bf16[224,384]{1,0:T(8,128)(2,1)S(1)}, u32[]{:S(2)}, u32[]{:S(2)}) collective-permute-start(bf16[224,384]{1,0:T(8,128)(2,1)S(1)} %get-tuple-element.260), channel_id=1, source_target_pairs={{0,16},{1,17},{2,18},{3,19},{4,20},{5,21},{6,22},{7,23},{8,24},{9,... | collective-permute-start | bytes 516104 | tf_op jit(solution)/shard_map/ppermute | solution.py:499
  99.2 11.3 %shard_map.233 = (f32[8,256,384]{2,1,0:T(8,128)}, bf16[32,384]{1,0:T(8,128)(2,1)S(1)}, bf16[2,2,48,1152]{3,2,1,0:T(8,128)(2,1)S(1)}, bf16[2,2,48,1152]{3,2,1,0:T(8,128)(2,1)S(1)}) custom-call(s32[4]{0:T(128)S(1)} %copy-done.4, bf16[8,256,384]{2,1,0:T(8,128)(2,1)S(1)} %copy-done, ...), custom_call_target="tpu_custom_call", output_to_operand_aliasing={{0}: (9, {})} | custom-call | flops 2818572288 | bytes 11796480 | tf_op jit(solution)/shard_map/pallas_call | solution.py:461
  110.5 1.9 %collective-permute-start.24 = (bf16[32,384]{1,0:T(8,128)(2,1)S(1)}, bf16[32,384]{1,0:T(8,128)(2,1)S(1)}, u32[]{:S(2)}, u32[]{:S(2)}) collective-permute-start(bf16[32,384]{1,0:T(8,128)(2,1)S(1)} %get-tuple-element.164.refs_0_), channel_id=1, source_target_pairs={{0,8},{1,9},{2,10},{3,11},{4,12},{5,13},{6,14},{7,15},{8,0},{9,1},... | collective-permute-start | bytes 73736 | tf_op jit(solution)/shard_map/ppermute | solution.py:499
  112.4 2.4 %collective-permute-start.25 = (bf16[32,384]{1,0:T(8,128)(2,1)S(1)}, bf16[32,384]{1,0:T(8,128)(2,1)S(1)}, u32[]{:S(2)}, u32[]{:S(2)}) collective-permute-start(bf16[32,384]{1,0:T(8,128)(2,1)S(1)} %get-tuple-element.164.refs_0_), channel_id=1, source_target_pairs={{0,16},{1,17},{2,18},{3,19},{4,20},{5,21},{6,22},{7,23},{8,24},{9,... | collective-permute-start | bytes 73736 | tf_op jit(solution)/shard_map/ppermute | solution.py:499
  117.2 3.4 %collective-permute-done.26.refs_3_ = bf16[32,384]{1,0:T(8,128)(2,1)S(1)} collective-permute-done((bf16[32,384]{1,0:T(8,128)(2,1)S(1)}, bf16[32,384]{1,0:T(8,128)(2,1)S(1)}, u32[]{:S(2)}, u32[]{:S(2)}) %collective-permute-start.26) | collective-permute-done | bytes 24608 | tf_op jit(solution)/shard_map/ppermute | solution.py:499
  125.6 2.0 %collective-permute-start.31 = (bf16[192,384]{1,0:T(8,128)(2,1)S(1)}, bf16[192,384]{1,0:T(8,128)(2,1)S(1)}, u32[]{:S(2)}, u32[]{:S(2)}) collective-permute-start(bf16[192,384]{1,0:T(8,128)(2,1)S(1)} %pad_maximum_fusion.14), channel_id=1, source_target_pairs={{0,16},{1,17},{2,18},{3,19},{4,20},{5,21},{6,22},{7,23},{8,24},{9,... | collective-permute-start | bytes 442376 | tf_op jit(solution)/shard_map/ppermute | solution.py:499
  127.6 1.9 %collective-permute-done.32 = bf16[320,384]{1,0:T(8,128)(2,1)S(1)} collective-permute-done((bf16[320,384]{1,0:T(8,128)(2,1)S(1)}, bf16[320,384]{1,0:T(8,128)(2,1)S(1)}, u32[]{:S(2)}, u32[]{:S(2)}) %collective-permute-start.32) | collective-permute-done | bytes 245792 | tf_op jit(solution)/shard_map/ppermute | solution.py:499
  129.7 4.2 %collective-permute-done.31 = bf16[192,384]{1,0:T(8,128)(2,1)S(1)} collective-permute-done((bf16[192,384]{1,0:T(8,128)(2,1)S(1)}, bf16[192,384]{1,0:T(8,128)(2,1)S(1)}, u32[]{:S(2)}, u32[]{:S(2)}) %collective-permute-start.31) | collective-permute-done | bytes 147488 | tf_op jit(solution)/shard_map/ppermute | solution.py:499
  134.0 2.8 %collective-permute-done.30 = bf16[272,384]{1,0:T(8,128)(2,1)S(1)} collective-permute-done((bf16[272,384]{1,0:T(8,128)(2,1)S(1)}, bf16[272,384]{1,0:T(8,128)(2,1)S(1)}, u32[]{:S(2)}, u32[]{:S(2)}) %collective-permute-start.30) | collective-permute-done | bytes 208928 | tf_op jit(solution)/shard_map/ppermute | solution.py:499
  137.7 3.4 %collective-permute-start.37 = (bf16[144,384]{1,0:T(8,128)(2,1)S(1)}, bf16[144,384]{1,0:T(8,128)(2,1)S(1)}, u32[]{:S(2)}, u32[]{:S(2)}) collective-permute-start(bf16[144,384]{1,0:T(8,128)(2,1)S(1)} %add_convert_fusion.6), channel_id=1, source_target_pairs={{0,16},{1,17},{2,18},{3,19},{4,20},{5,21},{6,22},{7,23},{8,24},{9,... | collective-permute-start | bytes 331784 | tf_op jit(solution)/shard_map/ppermute | solution.py:499
  150.2 2.1 %collective-permute-done.33 = bf16[432,384]{1,0:T(8,128)(2,1)S(1)} collective-permute-done((bf16[432,384]{1,0:T(8,128)(2,1)S(1)}, bf16[432,384]{1,0:T(8,128)(2,1)S(1)}, u32[]{:S(2)}, u32[]{:S(2)}) %collective-permute-start.33) | collective-permute-done | bytes 331808 | tf_op jit(solution)/shard_map/ppermute | solution.py:499
  (194 shorter events, 40.3 us)
Async XLA Ops:
  7.0 10.2 %collective-permute-start.7 = (bf16[96,1152]{1,0:T(8,128)(2,1)}, bf16[96,1152]{1,0:T(8,128)(2,1)S(1)}, u32[]{:S(2)}, u32[]{:S(2)}) collective-permute-start(bf16[96,1152]{1,0:T(8,128)(2,1)} %refs_4_.1), channel_id=1, source_target_pairs={{0,2},{1,3},{2,0},{3,1},{4,6},{5,7},{6,4},{7,5},{8,10},{9,11},{10,... | collective-permute-start | bytes 663560 | tf_op jit(solution)/shard_map/ppermute | solution.py:499
  16.3 18.7 %collective-permute-start.9 = (bf16[864,384]{1,0:T(8,128)(2,1)}, bf16[864,384]{1,0:T(8,128)(2,1)S(1)}, u32[]{:S(2)}, u32[]{:S(2)}) collective-permute-start(bf16[864,384]{1,0:T(8,128)(2,1)} %shard_map.230.refs_4_), channel_id=1, source_target_pairs={{0,2},{1,3},{2,0},{3,1},{4,6},{5,7},{6,4},{7,5},{8,10},{9,11},{10,... | collective-permute-start | bytes 1990664 | tf_op jit(solution)/shard_map/ppermute | solution.py:499
  17.8 17.7 %collective-permute-start.13 = (bf16[864,384]{1,0:T(8,128)(2,1)}, bf16[864,384]{1,0:T(8,128)(2,1)S(1)}, u32[]{:S(2)}, u32[]{:S(2)}) collective-permute-start(bf16[864,384]{1,0:T(8,128)(2,1)} %shard_map.230.refs_4_), channel_id=1, source_target_pairs={{0,1},{1,0},{2,3},{3,2},{4,5},{5,4},{6,7},{7,6},{8,9},{9,8},{10,11... | collective-permute-start | bytes 1990664 | tf_op jit(solution)/shard_map/ppermute | solution.py:499
  17.9 16.6 %collective-permute-start.10 = (f32[8,1536]{1,0:T(8,128)}, f32[8,1536]{1,0:T(8,128)S(1)}, u32[]{:S(2)}, u32[]{:S(2)}) collective-permute-start(f32[8,1536]{1,0:T(8,128)} %get-tuple-element.121), channel_id=1, source_target_pairs={{0,1},{1,0},{2,3},{3,2},{4,5},{5,4},{6,7},{7,6},{8,9},{9,8},{10,11... | collective-permute-start | bytes 147464 | tf_op jit(solution)/shard_map/ppermute | solution.py:499
  18.7 16.3 %collective-permute-start.11 = (f32[8,1536]{1,0:T(8,128)}, f32[8,1536]{1,0:T(8,128)S(1)}, u32[]{:S(2)}, u32[]{:S(2)}) collective-permute-start(f32[8,1536]{1,0:T(8,128)} %get-tuple-element.122), channel_id=1, source_target_pairs={{0,2},{1,3},{2,0},{3,1},{4,6},{5,7},{6,4},{7,5},{8,10},{9,11},{10,... | collective-permute-start | bytes 147464 | tf_op jit(solution)/shard_map/ppermute | solution.py:499
  19.9 15.2 %collective-permute-start.12 = (f32[8,1536]{1,0:T(8,128)}, f32[8,1536]{1,0:T(8,128)S(1)}, u32[]{:S(2)}, u32[]{:S(2)}) collective-permute-start(f32[8,1536]{1,0:T(8,128)} %get-tuple-element.123), channel_id=1, source_target_pairs={{0,3},{1,2},{2,1},{3,0},{4,7},{5,6},{6,5},{7,4},{8,11},{9,10},{10,... | collective-permute-start | bytes 147464 | tf_op jit(solution)/shard_map/ppermute | solution.py:499
  77.3 14.4 %collective-permute-start.16 = (bf16[432,384]{1,0:T(8,128)(2,1)S(1)}, bf16[432,384]{1,0:T(8,128)(2,1)S(1)}, u32[]{:S(2)}, u32[]{:S(2)}) collective-permute-start(bf16[432,384]{1,0:T(8,128)(2,1)S(1)} %get-tuple-element.223), channel_id=1, source_target_pairs={{0,4},{1,5},{2,6},{3,7},{4,0},{5,1},{6,2},{7,3},{8,12},{9,13},{10,... | collective-permute-start | bytes 995336 | tf_op jit(solution)/shard_map/ppermute | solution.py:499
  78.9 15.6 %collective-permute-start.17 = (bf16[432,384]{1,0:T(8,128)(2,1)S(1)}, bf16[432,384]{1,0:T(8,128)(2,1)S(1)}, u32[]{:S(2)}, u32[]{:S(2)}) collective-permute-start(bf16[432,384]{1,0:T(8,128)(2,1)S(1)} %get-tuple-element.222), channel_id=1, source_target_pairs={{0,2},{1,3},{2,0},{3,1},{4,6},{5,7},{6,4},{7,5},{8,10},{9,11},{10,... | collective-permute-start | bytes 995336 | tf_op jit(solution)/shard_map/ppermute | solution.py:499
  79.9 14.5 %collective-permute-start.18 = (bf16[432,384]{1,0:T(8,128)(2,1)S(1)}, bf16[432,384]{1,0:T(8,128)(2,1)S(1)}, u32[]{:S(2)}, u32[]{:S(2)}) collective-permute-start(bf16[432,384]{1,0:T(8,128)(2,1)S(1)} %get-tuple-element.221), channel_id=1, source_target_pairs={{0,6},{1,7},{2,4},{3,5},{4,2},{5,3},{6,0},{7,1},{8,14},{9,15},{10,... | collective-permute-start | bytes 995336 | tf_op jit(solution)/shard_map/ppermute | solution.py:499
  94.8 15.7 %collective-permute-start.20 = (bf16[224,384]{1,0:T(8,128)(2,1)S(1)}, bf16[224,384]{1,0:T(8,128)(2,1)S(1)}, u32[]{:S(2)}, u32[]{:S(2)}) collective-permute-start(bf16[224,384]{1,0:T(8,128)(2,1)S(1)} %get-tuple-element.259), channel_id=1, source_target_pairs={{0,8},{1,9},{2,10},{3,11},{4,12},{5,13},{6,14},{7,15},{8,0},{9,1},... | collective-permute-start | bytes 516104 | tf_op jit(solution)/shard_map/ppermute | solution.py:499
  96.4 14.1 %collective-permute-start.21 = (bf16[224,384]{1,0:T(8,128)(2,1)S(1)}, bf16[224,384]{1,0:T(8,128)(2,1)S(1)}, u32[]{:S(2)}, u32[]{:S(2)}) collective-permute-start(bf16[224,384]{1,0:T(8,128)(2,1)S(1)} %get-tuple-element.260), channel_id=1, source_target_pairs={{0,16},{1,17},{2,18},{3,19},{4,20},{5,21},{6,22},{7,23},{8,24},{9,... | collective-permute-start | bytes 516104 | tf_op jit(solution)/shard_map/ppermute | solution.py:499
  99.0 11.5 %collective-permute-start.22 = (bf16[224,384]{1,0:T(8,128)(2,1)S(1)}, bf16[224,384]{1,0:T(8,128)(2,1)S(1)}, u32[]{:S(2)}, u32[]{:S(2)}) collective-permute-start(bf16[224,384]{1,0:T(8,128)(2,1)S(1)} %get-tuple-element.258), channel_id=1, source_target_pairs={{0,24},{1,25},{2,26},{3,27},{4,28},{5,29},{6,30},{7,31},{8,16},{9,... | collective-permute-start | bytes 516104 | tf_op jit(solution)/shard_map/ppermute | solution.py:499
  114.7 5.9 %collective-permute-start.26 = (bf16[32,384]{1,0:T(8,128)(2,1)S(1)}, bf16[32,384]{1,0:T(8,128)(2,1)S(1)}, u32[]{:S(2)}, u32[]{:S(2)}) collective-permute-start(bf16[32,384]{1,0:T(8,128)(2,1)S(1)} %get-tuple-element.164.refs_0_), channel_id=1, source_target_pairs={{0,24},{1,25},{2,26},{3,27},{4,28},{5,29},{6,30},{7,31},{8,16},{9,... | collective-permute-start | bytes 73736 | tf_op jit(solution)/shard_map/ppermute | solution.py:499
  115.0 5.7 %collective-permute-start.23 = (bf16[2,2,48,1152]{3,2,1,0:T(8,128)(2,1)S(1)}, bf16[2,2,48,1152]{3,2,1,0:T(8,128)(2,1)S(1)}, u32[]{:S(2)}, u32[]{:S(2)}) collective-permute-start(bf16[2,2,48,1152]{3,2,1,0:T(8,128)(2,1)S(1)} %get-tuple-element.157), channel_id=1, source_target_pairs={{0,1},{1,0},{2,3},{3,2},{4,5},{5,4},{6,7},{7,6},{8,9},{9,8},{10,11... | collective-permute-start | bytes 1327112 | tf_op jit(solution)/shard_map/ppermute | solution.py:499
  120.6 8.9 %collective-permute-start.32 = (bf16[320,384]{1,0:T(8,128)(2,1)S(1)}, bf16[320,384]{1,0:T(8,128)(2,1)S(1)}, u32[]{:S(2)}, u32[]{:S(2)}) collective-permute-start(bf16[320,384]{1,0:T(8,128)(2,1)S(1)} %pad_maximum_fusion.13), channel_id=1, source_target_pairs={{0,4},{1,5},{2,6},{3,7},{4,0},{5,1},{6,2},{7,3},{8,12},{9,13},{10,... | collective-permute-start | bytes 737288 | tf_op jit(solution)/shard_map/ppermute | solution.py:499
  122.1 11.9 %collective-permute-start.28 = (bf16[272,384]{1,0:T(8,128)(2,1)S(1)}, bf16[272,384]{1,0:T(8,128)(2,1)S(1)}, u32[]{:S(2)}, u32[]{:S(2)}) collective-permute-start(bf16[272,384]{1,0:T(8,128)(2,1)S(1)} %get-tuple-element.169), channel_id=1, source_target_pairs={{0,4},{1,5},{2,6},{3,7},{4,0},{5,1},{6,2},{7,3},{8,12},{9,13},{10,... | collective-permute-start | bytes 626696 | tf_op jit(solution)/shard_map/ppermute | solution.py:499
  123.4 10.6 %collective-permute-start.29 = (bf16[272,384]{1,0:T(8,128)(2,1)S(1)}, bf16[272,384]{1,0:T(8,128)(2,1)S(1)}, u32[]{:S(2)}, u32[]{:S(2)}) collective-permute-start(bf16[272,384]{1,0:T(8,128)(2,1)S(1)} %get-tuple-element.170), channel_id=1, source_target_pairs={{0,2},{1,3},{2,0},{3,1},{4,6},{5,7},{6,4},{7,5},{8,10},{9,11},{10,... | collective-permute-start | bytes 626696 | tf_op jit(solution)/shard_map/ppermute | solution.py:499
  124.5 12.3 %collective-permute-start.30 = (bf16[272,384]{1,0:T(8,128)(2,1)S(1)}, bf16[272,384]{1,0:T(8,128)(2,1)S(1)}, u32[]{:S(2)}, u32[]{:S(2)}) collective-permute-start(bf16[272,384]{1,0:T(8,128)(2,1)S(1)} %get-tuple-element.171), channel_id=1, source_target_pairs={{0,6},{1,7},{2,4},{3,5},{4,2},{5,3},{6,0},{7,1},{8,14},{9,15},{10,... | collective-permute-start | bytes 626696 | tf_op jit(solution)/shard_map/ppermute | solution.py:499
  125.6 8.2 %collective-permute-start.31 = (bf16[192,384]{1,0:T(8,128)(2,1)S(1)}, bf16[192,384]{1,0:T(8,128)(2,1)S(1)}, u32[]{:S(2)}, u32[]{:S(2)}) collective-permute-start(bf16[192,384]{1,0:T(8,128)(2,1)S(1)} %pad_maximum_fusion.14), channel_id=1, source_target_pairs={{0,16},{1,17},{2,18},{3,19},{4,20},{5,21},{6,22},{7,23},{8,24},{9,... | collective-permute-start | bytes 442376 | tf_op jit(solution)/shard_map/ppermute | solution.py:499
  136.9 15.4 %collective-permute-start.36 = (bf16[144,384]{1,0:T(8,128)(2,1)S(1)}, bf16[144,384]{1,0:T(8,128)(2,1)S(1)}, u32[]{:S(2)}, u32[]{:S(2)}) collective-permute-start(bf16[144,384]{1,0:T(8,128)(2,1)S(1)} %add_convert_fusion.6), channel_id=1, source_target_pairs={{0,8},{1,9},{2,10},{3,11},{4,12},{5,13},{6,14},{7,15},{8,0},{9,1},... | collective-permute-start | bytes 331784 | tf_op jit(solution)/shard_map/ppermute | solution.py:499
  137.7 14.6 %collective-permute-start.37 = (bf16[144,384]{1,0:T(8,128)(2,1)S(1)}, bf16[144,384]{1,0:T(8,128)(2,1)S(1)}, u32[]{:S(2)}, u32[]{:S(2)}) collective-permute-start(bf16[144,384]{1,0:T(8,128)(2,1)S(1)} %add_convert_fusion.6), channel_id=1, source_target_pairs={{0,16},{1,17},{2,18},{3,19},{4,20},{5,21},{6,22},{7,23},{8,24},{9,... | collective-permute-start | bytes 331784 | tf_op jit(solution)/shard_map/ppermute | solution.py:499
  141.1 11.2 %collective-permute-start.38 = (bf16[144,384]{1,0:T(8,128)(2,1)S(1)}, bf16[144,384]{1,0:T(8,128)(2,1)S(1)}, u32[]{:S(2)}, u32[]{:S(2)}) collective-permute-start(bf16[144,384]{1,0:T(8,128)(2,1)S(1)} %add_convert_fusion.6), channel_id=1, source_target_pairs={{0,24},{1,25},{2,26},{3,27},{4,28},{5,29},{6,30},{7,31},{8,16},{9,... | collective-permute-start | bytes 331784 | tf_op jit(solution)/shard_map/ppermute | solution.py:499
  142.0 10.3 %collective-permute-start.33 = (bf16[432,384]{1,0:T(8,128)(2,1)S(1)}, bf16[432,384]{1,0:T(8,128)(2,1)S(1)}, u32[]{:S(2)}, u32[]{:S(2)}) collective-permute-start(bf16[432,384]{1,0:T(8,128)(2,1)S(1)} %fusion.6), channel_id=1, source_target_pairs={{0,4},{1,5},{2,6},{3,7},{4,0},{5,1},{6,2},{7,3},{8,12},{9,13},{10,... | collective-permute-start | bytes 995336 | tf_op jit(solution)/shard_map/ppermute | solution.py:499
  146.1 6.2 %collective-permute-start.35 = (f32[16,96]{1,0:T(8,128)S(1)}, f32[16,96]{1,0:T(8,128)S(1)}, u32[]{:S(2)}, u32[]{:S(2)}) collective-permute-start(f32[16,96]{1,0:T(8,128)S(1)} %slice_select_fusion.1), channel_id=1, source_target_pairs={{0,2},{1,3},{2,0},{3,1},{4,6},{5,7},{6,4},{7,5},{8,10},{9,11},{10,... | collective-permute-start | bytes 18440 | tf_op jit(solution)/shard_map/ppermute | solution.py:499
  (41 other events, 156.4 us)
